TPU v7x, 32 devices: a whole 2x2x4 slice. The times are simulated.
32 devices in a mesh: dp: 8 (over z, core), tensor: 4 (over y, x).
Axes of the slice: x: 2, y: 2, z: 4, core: 2. Of those that a mesh axis runs over, the one named last changes fastest.
Arguments:
- tokens: bfloat16 [16384, 1152], P(('dp', 'tensor')), may hold values from -6 to 6
- norm_gains: float32 [2, 1152], P(None, ('dp', 'tensor')), may hold values from 0.5 to 1.5
- row_biases: float32 [4, 1152], P(None, ('dp', 'tensor')), may hold values from -3 to 3
- w_qkv: bfloat16 [3, 1152, 1152], P(None, 'dp', 'tensor'), may hold values from -1 to 1
- head_bias: float32 [2, 1152], P(None, 'tensor'), may hold values from -3 to 3
- w_out: bfloat16 [1152, 1152], P('tensor', 'dp'), may hold values from -1.5 to 1.5
- w_fc1: bfloat16 [1152, 4304], P('dp', 'tensor'), may hold values from -0.1875 to 0.1875
- fc1_bias: float32 [4304], P('tensor'), may hold values from -3 to 3
- w_fc2: bfloat16 [4304, 1152], P('tensor', 'dp'), may hold values from -0.09375 to 0.09375
- cotangent: bfloat16 [16384, 1152], P(('dp', 'tensor')), may hold values from -6 to 6
Outputs:
- output: float32 [16384, 1152], P(('dp', 'tensor'))
- grad_tokens: float32 [16384, 1152], P(('dp', 'tensor'))
- grad_norm_gains: float32 [2, 1152], P(None, ('dp', 'tensor'))
- grad_row_biases: float32 [4, 1152], P(None, ('dp', 'tensor'))
- grad_w_qkv: float32 [3, 1152, 1152], P(None, 'dp', 'tensor')
- grad_head_bias: float32 [2, 1152], P(None, 'tensor')
- grad_w_out: float32 [1152, 1152], P('tensor', 'dp')
- grad_w_fc1: float32 [1152, 4304], P('dp', 'tensor')
- grad_fc1_bias: float32 [4304], P('tensor')
- grad_w_fc2: float32 [4304, 1152], P('tensor', 'dp')
All inputs are finite; a program needn't handle non-finite values.
Results may differ from a plain program's by a relative error of at most 0.04.
Values may be sent and summed in bfloat16 or wider, within the bound.
No kernel may reach another device: no remote copies, remote signals or barrier semaphores. Data moves between devices by JAX's collectives and lax.ppermute only.
A program may use at most 192 MiB of HBM per device.

v0:
```python
import functools

import jax
import jax.numpy as jnp
from jax import lax
from jax.experimental import pallas as pl
from jax.experimental.pallas import tpu as pltpu
from jax.sharding import PartitionSpec as P


HD = 72
SEQ = 256
EPS = 1e-06
F32 = jnp.float32
BF16 = jnp.bfloat16
AXES = ("dp", "tensor")


def norm_rows(values, gain_row, shifts):
    center = values - jnp.mean(values, axis=-1, keepdims=True)
    spread = lax.rsqrt(jnp.mean(center * center, axis=-1, keepdims=True) + EPS)
    normed = center * spread
    return (normed * gain_row + shifts, normed, spread)


def norm_back(grad_rows, normed, spread, gain_row):
    scaled = grad_rows * gain_row
    return spread * (
        scaled
        - jnp.mean(scaled, axis=-1, keepdims=True)
        - normed * jnp.mean(scaled * normed, axis=-1, keepdims=True)
    )


def tie(value, *others):
    return lax.optimization_barrier((value, *others))[0]


def dot_nn(a, b):
    return lax.dot_general(a, b, (((1,), (0,)), ((), ())), preferred_element_type=F32)


def dot_nt(a, b):
    return lax.dot_general(a, b, (((1,), (1,)), ((), ())), preferred_element_type=F32)


def dot_tn(a, b):
    return lax.dot_general(a, b, (((0,), (0,)), ((), ())), preferred_element_type=F32)


LANES = 128


def padded(size):
    return -(-size // LANES) * LANES


def segments(heads):
    return [
        (kind * heads * HD + h * HD, (kind * heads + h) * LANES)
        for kind in range(4)
        for h in range(heads)
    ]


def attend_kernel(heads, images, rows_ref, w_ref, bias_ref, qkv_ref, mixed_ref, lse_ref, wide_ref):
    hp = heads * LANES

    @pl.when(pl.program_id(0) == 0)
    def _():
        lane = lax.broadcasted_iota(jnp.int32, (1, LANES), 1)
        for src, dst in segments(heads):
            piece = w_ref[:, src : src + LANES]
            wide_ref[:, dst : dst + LANES] = jnp.where(lane < HD, piece, jnp.zeros_like(piece))

    proj = dot_nn(rows_ref[...], wide_ref[:, : 3 * hp])
    query = ((proj[:, :hp] + bias_ref[0:1, :]) * HD ** (-0.5)).astype(BF16)
    keys = proj[:, hp : 2 * hp].astype(BF16)
    vals = (proj[:, 2 * hp :] + bias_ref[1:2, :]).astype(BF16)
    qkv_ref[:, :hp] = query
    qkv_ref[:, hp : 2 * hp] = keys
    qkv_ref[:, 2 * hp :] = vals
    units = [(m, h) for m in range(images) for h in range(heads)]

    def cut(array, m, h):
        return array[m * SEQ : (m + 1) * SEQ, h * LANES : (h + 1) * LANES]

    scores = [dot_nt(cut(query, m, h), cut(keys, m, h)) for m, h in units]
    tops = [jnp.max(s, axis=-1, keepdims=True) for s in scores]
    exps = [jnp.exp(s - top) for s, top in zip(scores, tops)]
    sums = [jnp.sum(e, axis=-1, keepdims=True) for e in exps]
    probs = [(e * (1.0 / total)).astype(BF16) for e, total in zip(exps, sums)]
    for (m, h), p, top, total in zip(units, probs, tops, sums):
        rows = slice(m * SEQ, (m + 1) * SEQ)
        mixed_ref[rows, h * LANES : (h + 1) * LANES] = dot_nn(p, cut(vals, m, h)).astype(BF16)
        lse_ref[rows, h : h + 1] = top + jnp.log(total)


def attend(rows, weight, bias, images=2):
    total, width = rows.shape
    heads = bias.shape[1] // LANES
    hp = heads * LANES
    tile = images * SEQ
    return pl.pallas_call(
        functools.partial(attend_kernel, heads, images),
        grid=(total // tile,),
        in_specs=[
            pl.BlockSpec((tile, width), lambda i: (i, 0)),
            pl.BlockSpec(weight.shape, lambda i: (0, 0)),
            pl.BlockSpec(bias.shape, lambda i: (0, 0)),
        ],
        out_specs=[
            pl.BlockSpec((tile, 3 * hp), lambda i: (i, 0)),
            pl.BlockSpec((tile, hp), lambda i: (i, 0)),
            pl.BlockSpec((tile, heads), lambda i: (i, 0)),
            pl.BlockSpec((width, 4 * hp), lambda i: (0, 0)),
        ],
        out_shape=[
            jax.ShapeDtypeStruct((total, 3 * hp), BF16),
            jax.ShapeDtypeStruct((total, hp), BF16),
            jax.ShapeDtypeStruct((total, heads), F32),
            jax.ShapeDtypeStruct((width, 4 * hp), BF16),
        ],
        cost_estimate=pl.CostEstimate(
            flops=2 * total * width * 3 * hp + 4 * total * SEQ * hp,
            bytes_accessed=2 * (total * (width + 4 * hp) + 2 * weight.size),
            transcendentals=total * SEQ * heads,
        ),
        compiler_params=pltpu.CompilerParams(vmem_limit_bytes=24 << 20),
        name="attend",
    )(rows, weight, bias)


def attend_back_kernel(
    heads, images, grad_ref, rows_ref, wide_ref, qkv_ref, mixed_ref, lse_ref,
    proj_ref, gw_ref, sums_ref, acc,
):
    hp = heads * LANES
    step = pl.program_id(0)
    gh = grad_ref[...]
    gmix = dot_nn(gh, wide_ref[...]).astype(BF16)
    units = [(m, h) for m in range(images) for h in range(heads)]

    def cut(array, m, h, kind=0):
        lo = (kind * heads + h) * LANES
        return array[m * SEQ : (m + 1) * SEQ, lo : lo + LANES]

    query = [cut(qkv_ref, m, h, 0) for m, h in units]
    keys = [cut(qkv_ref, m, h, 1) for m, h in units]
    vals = [cut(qkv_ref, m, h, 2) for m, h in units]
    gm = [cut(gmix, m, h) for m, h in units]
    lse = [lse_ref[m * SEQ : (m + 1) * SEQ, h : h + 1] for m, h in units]
    probs = [jnp.exp(dot_nt(q, k) - top) for q, k, top in zip(query, keys, lse)]
    dprobs = [dot_nt(g, v) for g, v in zip(gm, vals)]
    dots = [jnp.sum(p * dp, axis=-1, keepdims=True) for p, dp in zip(probs, dprobs)]
    dscores = [(p * (dp - dt)).astype(BF16) for p, dp, dt in zip(probs, dprobs, dots)]
    sums = [[None] * heads for _ in range(2)]
    for n, (m, h) in enumerate(units):
        rows = slice(m * SEQ, (m + 1) * SEQ)
        grad_v = dot_tn(probs[n].astype(BF16), gm[n])
        grad_q = dot_nn(dscores[n], keys[n]) * HD ** (-0.5)
        grad_k = dot_tn(dscores[n], query[n])
        for kind, value in enumerate((grad_q, grad_k, grad_v)):
            lo = (kind * heads + h) * LANES
            proj_ref[rows, lo : lo + LANES] = value.astype(BF16)
        for kind, value in enumerate((grad_q, grad_v)):
            column = jnp.sum(value, axis=0, keepdims=True)
            sums[kind][h] = column if sums[kind][h] is None else sums[kind][h] + column
    sums = jnp.concatenate([jnp.concatenate(s, axis=1) for s in sums], axis=0)
    gw_qkv = dot_tn(rows_ref[...], proj_ref[...])
    gw_out = dot_tn(gh, mixed_ref[...])

    @pl.when(step == 0)
    def _():
        acc[:, : 3 * hp] = gw_qkv
        acc[:, 3 * hp :] = gw_out
        sums_ref[...] = sums

    @pl.when(step > 0)
    def _():
        acc[:, : 3 * hp] += gw_qkv
        acc[:, 3 * hp :] += gw_out
        sums_ref[...] += sums

    @pl.when(step == pl.num_programs(0) - 1)
    def _():
        gw_ref[...] = jnp.zeros_like(gw_ref)
        for dst, src in segments(heads):
            gw_ref[:, dst : dst + HD] = acc[:, src : src + HD].astype(BF16)


def attend_back(grad_rows, rows, wide, qkv, mixed, lse, packed, images=2):
    total, width = rows.shape
    heads = lse.shape[1]
    hp = heads * LANES
    tile = images * SEQ
    return pl.pallas_call(
        functools.partial(attend_back_kernel, heads, images),
        grid=(total // tile,),
        in_specs=[
            pl.BlockSpec((tile, width), lambda i: (i, 0)),
            pl.BlockSpec((tile, width), lambda i: (i, 0)),
            pl.BlockSpec((width, hp), lambda i: (0, 3)),
            pl.BlockSpec((tile, 3 * hp), lambda i: (i, 0)),
            pl.BlockSpec((tile, hp), lambda i: (i, 0)),
            pl.BlockSpec((tile, heads), lambda i: (i, 0)),
        ],
        out_specs=[
            pl.BlockSpec((tile, 3 * hp), lambda i: (i, 0)),
            pl.BlockSpec((width, packed), lambda i: (0, 0)),
            pl.BlockSpec((2, hp), lambda i: (0, 0)),
        ],
        out_shape=[
            jax.ShapeDtypeStruct((total, 3 * hp), BF16),
            jax.ShapeDtypeStruct((width, packed), BF16),
            jax.ShapeDtypeStruct((2, hp), F32),
        ],
        scratch_shapes=[pltpu.VMEM((width, 4 * hp), F32)],
        cost_estimate=pl.CostEstimate(
            flops=2 * total * width * 5 * hp + 10 * total * SEQ * hp,
            bytes_accessed=2 * (2 * total * width + 7 * total * hp + width * (hp + packed)),
            transcendentals=total * SEQ * heads,
        ),
        compiler_params=pltpu.CompilerParams(vmem_limit_bytes=30 << 20),
        name="attend_back",
    )(grad_rows, rows, wide, qkv, mixed, lse)


def sum_nt_kernel(count, half_steps, *refs):
    lefts, rights = refs[:count], refs[count : 2 * count]
    mine_ref, other_ref = refs[2 * count :]
    total = dot_nt(lefts[0][...], rights[0][...])
    for left, right in zip(lefts[1:], rights[1:]):
        total += dot_nt(left[...], right[...])
    value = total.astype(BF16)
    step = pl.program_id(0)

    @pl.when(step < half_steps)
    def _():
        other_ref[...] = value

    @pl.when(step >= half_steps)
    def _():
        mine_ref[...] = value


def sum_nt(lefts, rights, column, tile=SEQ):
    count = len(lefts)
    total, inner = lefts[0].shape
    width = rights[0].shape[0]
    half = total // 2 // tile
    return pl.pallas_call(
        functools.partial(sum_nt_kernel, count, half),
        grid=(2 * half,),
        in_specs=[pl.BlockSpec((tile, inner), lambda i: (lax.rem(i + half, 2 * half), 0))] * count
        + [
            pl.BlockSpec((width, inner), lambda i: (0, column), pipeline_mode=pl.Buffered(1))
        ]
        * count,
        out_specs=[
            pl.BlockSpec((tile, width), lambda i: (jnp.maximum(i - half, 0), 0)),
            pl.BlockSpec((tile, width), lambda i: (jnp.minimum(i, half - 1), 0)),
        ],
        out_shape=[jax.ShapeDtypeStruct((total // 2, width), BF16)] * 2,
        cost_estimate=pl.CostEstimate(
            flops=2 * total * inner * width * count,
            bytes_accessed=2 * (count * (total + width) * inner + total * width),
            transcendentals=0,
        ),
        compiler_params=pltpu.CompilerParams(vmem_limit_bytes=24 << 20),
        name="sum_nt",
    )(*lefts, *rights)


def fetch_weights(core_ref, own, got, kept, sems):
    def fetch(sources):
        copies = [
            pltpu.make_async_copy(source, target, sems.at[i])
            for i, (source, target) in enumerate(zip(sources, kept))
        ]
        for copy in copies:
            copy.start()
        for copy in copies:
            copy.wait()

    @pl.when(core_ref[0] == 0)
    def _():
        fetch(own)

    @pl.when(core_ref[0] != 0)
    def _():
        fetch(got)


def feed_in_kernel(
    half, core_ref, rows0, rows1, w1_own, w1_got, bias_ref, rows_ref, act_ref, slope_ref, w1, sems
):
    step = pl.program_id(0)

    @pl.when(step == 0)
    def _():
        fetch_weights(core_ref, [w1_own], [w1_got], [w1], sems)

    rows = jnp.where(step < half, rows0[...], rows1[...])
    rows_ref[...] = rows
    pre = dot_nn(rows, w1[...]) + bias_ref[...]
    root = (2.0 / jnp.pi) ** 0.5
    square = pre * pre
    tanh = jnp.tanh(root * (pre + 0.044715 * (pre * square)))
    gate = 0.5 * (1.0 + tanh)
    slope = gate + 0.5 * pre * (1.0 - tanh * tanh) * (root * (1.0 + 3 * 0.044715 * square))
    act_ref[...] = (pre * gate).astype(BF16)
    slope_ref[...] = slope.astype(BF16)


def feed_in(core, rows, weights, bias, tile=SEQ):
    count, width = rows[0].shape
    ff = weights[0].shape[1]
    half = count // tile
    step = lambda i: (i, 0)
    anywhere = pl.BlockSpec(memory_space=pl.ANY)
    return pl.pallas_call(
        functools.partial(feed_in_kernel, half),
        grid=(2 * half,),
        in_specs=[
            pl.BlockSpec(memory_space=pltpu.SMEM),
            pl.BlockSpec((tile, width), lambda i: (jnp.minimum(i, half - 1), 0)),
            pl.BlockSpec((tile, width), lambda i: (jnp.maximum(i - half, 0), 0)),
            anywhere,
            anywhere,
            pl.BlockSpec((1, ff), lambda i: (0, 0)),
        ],
        out_specs=[
            pl.BlockSpec((tile, width), step),
            pl.BlockSpec((tile, ff), step),
            pl.BlockSpec((tile, ff), step),
        ],
        out_shape=[
            jax.ShapeDtypeStruct((2 * count, width), BF16),
            jax.ShapeDtypeStruct((2 * count, ff), BF16),
            jax.ShapeDtypeStruct((2 * count, ff), BF16),
        ],
        scratch_shapes=[pltpu.VMEM((width, ff), BF16), pltpu.SemaphoreType.DMA((1,))],
        compiler_params=pltpu.CompilerParams(vmem_limit_bytes=24 << 20),
        cost_estimate=pl.CostEstimate(
            flops=4 * count * width * ff,
            bytes_accessed=2 * (width * ff + 4 * count * (width + ff)),
            transcendentals=2 * count * ff,
        ),
        name="feed_in",
    )(core, *rows, *weights, bias)


def feed_out_kernel(
    half, core_ref, cot0, cot1, act_ref, slope_ref, w1_own, w1_got, w2_own, w2_got,
    gpre_ref, out0, out1, grad0, grad1, sums_ref, w1, w2, sems,
):
    step = pl.program_id(0)

    @pl.when(step == 0)
    def _():
        fetch_weights(core_ref, [w1_own, w2_own], [w1_got, w2_got], [w1, w2], sems)

    first = step < half
    cot = jnp.where(first, cot0[...], cot1[...])
    grad_pre = dot_nn(cot, w2[...]) * slope_ref[...].astype(F32)
    sums = jnp.sum(grad_pre, axis=0, keepdims=True)
    grad_in = grad_pre.astype(BF16)
    gpre_ref[...] = grad_in
    grad = dot_nt(grad_in, w1[...]).astype(BF16)
    out = dot_nt(act_ref[...], w2[...]).astype(BF16)

    @pl.when(step == 0)
    def _():
        sums_ref[...] = sums

    @pl.when(step > 0)
    def _():
        sums_ref[...] += sums

    @pl.when(first)
    def _():
        out0[...] = out
        grad0[...] = grad

    @pl.when(jnp.logical_not(first))
    def _():
        out1[...] = out
        grad1[...] = grad


def feed_out(core, cots, act, slope, weights, tile=SEQ):
    count, width = cots[0].shape
    ff = act.shape[1]
    half = count // tile
    low = lambda i: (jnp.minimum(i, half - 1), 0)
    high = lambda i: (jnp.maximum(i - half, 0), 0)
    step = lambda i: (i, 0)
    anywhere = pl.BlockSpec(memory_space=pl.ANY)
    return pl.pallas_call(
        functools.partial(feed_out_kernel, half),
        grid=(2 * half,),
        in_specs=[
            pl.BlockSpec(memory_space=pltpu.SMEM),
            pl.BlockSpec((tile, width), low),
            pl.BlockSpec((tile, width), high),
            pl.BlockSpec((tile, ff), step),
            pl.BlockSpec((tile, ff), step),
        ]
        + [anywhere] * 4,
        out_specs=[
            pl.BlockSpec((tile, ff), step),
            pl.BlockSpec((tile, width), low),
            pl.BlockSpec((tile, width), high),
            pl.BlockSpec((tile, width), low),
            pl.BlockSpec((tile, width), high),
            pl.BlockSpec((1, ff), lambda i: (0, 0)),
        ],
        out_shape=[jax.ShapeDtypeStruct((2 * count, ff), BF16)]
        + [jax.ShapeDtypeStruct((count, width), BF16)] * 4
        + [jax.ShapeDtypeStruct((1, ff), F32)],
        scratch_shapes=[
            pltpu.VMEM((width, ff), BF16),
            pltpu.VMEM((width, ff), BF16),
            pltpu.SemaphoreType.DMA((2,)),
        ],
        compiler_params=pltpu.CompilerParams(vmem_limit_bytes=30 << 20),
        cost_estimate=pl.CostEstimate(
            flops=12 * count * width * ff,
            bytes_accessed=2 * (2 * width * ff + 2 * count * (3 * width + 3 * ff)),
            transcendentals=0,
        ),
        name="feed_out",
    )(core, *cots, act, slope, *weights)


def pack_kernel(count, where_ref, *refs):
    out_ref = refs[-1]
    vectors, units, bias_ref = refs[:count], refs[count:-2], refs[-2]
    out_ref[...] = jnp.zeros_like(out_ref)
    for i, vector in enumerate(vectors):
        out_ref[0, i : i + 1, : vector.shape[1]] = vector[...]
    core = where_ref[0]
    for n, unit in enumerate(units):
        hp = unit.shape[1]
        spot = 1 + where_ref[2 + n]

        @pl.when(core == 0)
        def _():
            out_ref[spot, 1:3, :hp] = unit[...]

        @pl.when(core != 0)
        def _():
            out_ref[spot, 3:5, :hp] = unit[...]

    out_ref[1 + where_ref[1], 0:1, : bias_ref.shape[1]] = bias_ref[...]


def pack_small(where, vectors, units, bias, spots):
    lanes = max(x.shape[1] for x in [*vectors, *units, bias])
    return pl.pallas_call(
        functools.partial(pack_kernel, len(vectors)),
        in_specs=[pl.BlockSpec(memory_space=pltpu.SMEM)]
        + [pl.BlockSpec(memory_space=pltpu.VMEM)] * (len(vectors) + len(units) + 1),
        out_specs=pl.BlockSpec(memory_space=pltpu.VMEM),
        out_shape=jax.ShapeDtypeStruct((1 + spots, 8, lanes), F32),
        name="pack_small",
    )(where, *vectors, *units, bias)


def make_body(ndp, nt):
    nz = ndp // 2
    bits = nt.bit_length() - 1
    top = nt // 2
    low = nt // 2

    def perm(move):
        pairs = []
        for d in range(ndp):
            for t in range(nt):
                d2, t2 = move(d, t)
                pairs.append((d * nt + t, d2 * nt + t2))
        return pairs

    def send(value, move):
        return lax.ppermute(value, AXES, perm(move))

    def swap_core(value):
        return send(value, lambda d, t: (d ^ 1, t))

    def swap_tensor(value, i):
        return send(value, lambda d, t: (d, t ^ i))

    def shift_z(value, k):
        return send(value, lambda d, t: ((d + 2 * k) % ndp, t))

    def stage(value, i):
        return send(
            value, lambda d, t: (d, t ^ ((1 << i) if d % 2 == 0 else (1 << (bits - 1 - i))))
        )

    def reverse_bits(p):
        return sum(((p >> i) & 1) << (bits - 1 - i) for i in range(bits))

    def swap_top(value):
        pairs = [(d * nt + t, d * nt + (t ^ top)) for d in range(1, ndp, 2) for t in range(nt)]
        return lax.ppermute(value, AXES, pairs)

    def gather_z(value, z):
        out = jnp.zeros((nz,) + value.shape, value.dtype)
        out = lax.dynamic_update_slice_in_dim(out, value[None], z, 0)
        for k in range(1, nz):
            got = shift_z(value, k)
            out = lax.dynamic_update_slice_in_dim(out, got[None], lax.rem(z - k + nz, nz), 0)
        return out

    def pick(selector, items):
        total = jnp.where(selector == 0, items[0], 0)
        for i in range(1, len(items)):
            total = total + jnp.where(selector == i, items[i], 0)
        return total

    def body(
        tokens, norm_gains, row_biases, w_qkv, head_bias, w_out, w_fc1, fc1_bias, w_fc2, cotangent
    ):
        d = lax.axis_index("dp")
        t = lax.axis_index("tensor")
        z, c = d // 2, d % 2
        core0 = c == 0
        _, width = tokens.shape
        block = w_qkv.shape[2]
        hh = block // 2
        part = w_qkv.shape[1]
        ff = w_fc1.shape[1]

        def by_core(zero, one):
            return jnp.where(core0, zero, one)

        w_out_t = w_out.T

        packed = padded(4 * hh)
        heads = hh // HD
        wide = padded(ff)

        def half(h):
            sl = slice(h * hh, (h + 1) * hh)
            cols = [w_qkv[0][:, sl], w_qkv[1][:, sl], w_qkv[2][:, sl], w_out_t[:, sl]]
            return jnp.pad(jnp.concatenate(cols, axis=1), ((0, 0), (0, packed - 4 * hh)))

        gathered = lax.all_gather(jnp.stack([half(0), half(1)]), "dp", axis=1, tiled=True)
        far = range(1, low)
        cot_far = [swap_tensor(cotangent, i) for i in far]
        own_half = lax.dynamic_index_in_dim(gathered, c, 0, keepdims=False)
        attn_w = [tie(own_half, *cot_far)]
        for i in range(bits):
            attn_w = attn_w + [stage(b, i) for b in attn_w]

        def gather_ff(own):
            return lax.all_gather(
                jnp.pad(own, ((0, 0), (0, wide - ff))), "dp", axis=0, tiled=True
            )

        fc1_own, fc2_own = gather_ff(w_fc1), gather_ff(w_fc2.T)

        gain_count, shift_count = norm_gains.shape[0], row_biases.shape[0]
        vec_count = gain_count + shift_count
        piece = norm_gains.shape[1]
        small = jnp.concatenate(
            [norm_gains.reshape(-1), row_biases.reshape(-1), head_bias.reshape(-1), fc1_bias]
        )
        smalls = [small] + [swap_tensor(small, i) for i in range(1, nt)]
        vec_size = vec_count * piece
        vecs = jnp.stack([pick(t ^ i, [s[:vec_size] for s in smalls]) for i in range(nt)])
        vecs = gather_z(vecs, z)
        vecs_other = swap_core(vecs)
        vecs = jnp.stack([by_core(vecs, vecs_other), by_core(vecs_other, vecs)], axis=1)
        vecs = vecs.reshape(nz * 2 * nt, vec_count, piece).transpose(1, 0, 2)
        vecs = vecs.reshape(vec_count, width)
        gain_rows, shifts = vecs[:gain_count], vecs[gain_count:]
        head_biases = jnp.stack([s[vec_size : vec_size + 2 * block] for s in smalls])
        turned = jnp.stack(
            [smalls[reverse_bits(p)][vec_size : vec_size + 2 * block] for p in range(nt)]
        )
        unit_bias = by_core(head_biases, turned).reshape(nt, 2, 2, heads, HD)
        unit_bias = by_core(unit_bias[:, :, 0], unit_bias[:, :, 1])
        unit_bias = jnp.pad(unit_bias, ((0, 0),) * 3 + ((0, LANES - HD),))
        unit_bias = unit_bias.reshape(nt, 2, heads * LANES)
        ff_bias = by_core(smalls[0][vec_size + 2 * block :], smalls[top][vec_size + 2 * block :])
        ff_bias = jnp.pad(ff_bias, (0, wide - ff)).reshape(1, wide)

        inputs_f = tokens.astype(F32)
        first_f, normed_one, spread_one = norm_rows(inputs_f, gain_rows[0], shifts[0])
        first = first_f.astype(BF16)
        first_chip = jnp.concatenate([first, swap_core(first)], axis=0)

        cots = [(g, swap_core(g)) for g in [cotangent, *cot_far]]
        cot_rows = [jnp.concatenate(pair, axis=0) for pair in cots]

        saved = []
        for p in range(nt):
            bias = unit_bias[p]
            if p == nt - 2:
                bias = tie(bias, *cot_rows)
            saved.append(attend(first_chip, attn_w[p], bias))
        mixed = [s[1] for s in saved]
        wides = [s[3] for s in saved]
        fc1_got = swap_top(tie(fc1_own, attn_w[nt - 1]))
        fc2_got = swap_top(fc2_own)
        attn_mine, attn_other = sum_nt(mixed, wides, 3)
        attention = attn_mine.astype(F32) + swap_core(attn_other).astype(F32)
        hidden_one = inputs_f + attention + shifts[1]
        second_f, normed_two, spread_two = norm_rows(hidden_one, gain_rows[1], shifts[2])

        core = c.astype(jnp.int32).reshape(1)
        second = second_f.astype(BF16)
        second_far = [swap_tensor(second, i) for i in far]
        fc1_pair, fc2_pair = (fc1_own, fc1_got), (fc2_own, fc2_got)
        ins = [None] * low
        ins[0] = feed_in(core, (second, swap_core(second)), fc1_pair, ff_bias)
        grad_fc2_t = dot_tn(cot_rows[0], ins[0][1])
        for i, rows_far in zip(far, second_far):
            rows_far = tie(rows_far, grad_fc2_t)
            ins[i] = feed_in(core, (rows_far, swap_core(rows_far)), fc1_pair, ff_bias)
            grad_fc2_t = grad_fc2_t + dot_tn(cot_rows[i], ins[i][1])
        grad_fc2_t = grad_fc2_t.astype(BF16)

        outs, grad_sums, pres, grad_fc1_bias = [None] * low, [None] * low, [None] * low, 0
        after = grad_fc2_t
        for i in reversed(range(low)):
            act, slope = ins[i][1:]
            if i == 0 or i == low - 1:
                slope = tie(slope, after)
            pres[i], out0, out1, grad0, grad1, sums = feed_out(
                core, cots[i], act, slope, fc1_pair + fc2_pair
            )
            outs[i] = (out0, out1)
            grad_fc1_bias = grad_fc1_bias + sums
            value = grad0.astype(F32) + swap_core(grad1).astype(F32)
            grad_sums[i] = value.astype(BF16) if i else value
            after = grad_sums[i]
        grad_fc1 = dot_tn(ins[0][0], pres[0])
        for i in far:
            grad_fc1 = grad_fc1 + dot_tn(ins[i][0], pres[i])
        grad_fc1 = grad_fc1.astype(BF16)

        def scatter_ff(partial):
            own = lax.psum_scatter(partial, "dp", scatter_dimension=0, tiled=True)
            return lax.optimization_barrier(own)[:, :ff].astype(F32)

        grad_fc2_t = by_core(grad_fc2_t, swap_top(grad_fc2_t))
        grad_fc2_own = scatter_ff(grad_fc2_t).T

        grad_second = grad_sums[0]
        for i in far:
            got = tie(swap_tensor(grad_sums[i], i), grad_fc1, grad_fc2_t)
            grad_second = grad_second + got.astype(F32)
        grad_fc1 = by_core(grad_fc1, swap_top(grad_fc1))
        grad_fc1_own = scatter_ff(grad_fc1)

        mlp_out = outs[0][0].astype(F32) + swap_core(outs[0][1]).astype(F32)
        for i in far:
            mine, other = outs[i]
            sent = (mine.astype(F32) + swap_core(other).astype(F32)).astype(BF16)
            mlp_out = mlp_out + swap_tensor(tie(sent, grad_second), i).astype(F32)

        cot_f = cotangent.astype(F32)
        gain_two = jnp.sum(grad_second * normed_two, axis=0)
        shift_two = jnp.sum(grad_second, axis=0)
        grad_hidden = cot_f + norm_back(grad_second, normed_two, spread_two, gain_rows[1])
        shift_out = jnp.sum(grad_hidden, axis=0)
        shift_fc2 = jnp.sum(cot_f, axis=0)
        hidden_in = grad_hidden.astype(BF16)
        hidden_chip = jnp.concatenate([hidden_in, swap_core(hidden_in)], axis=0)
        back, after = {}, None
        grad_w = [None] * nt
        got_w = {}
        for p in reversed(range(nt)):
            qkv, mix, lse = saved[p][:3]
            if after is not None:
                lse = tie(lse, *after)
            back[p] = attend_back(hidden_chip, first_chip, wides[p], qkv, mix, lse, packed)
            value = back[p][1]
            for q in sorted((q for q in got_w if got_w[q][0] == p), reverse=True):
                if p:
                    value = (value.astype(F32) + got_w[q][1].astype(F32)).astype(BF16)
            grad_w[p] = value
            after = [value]
            if p == 0:
                break
            i = p.bit_length() - 1
            got_w[p] = (p - (1 << i), stage(value, i))
            if p == 1:
                after = [value, grad_fc1]
        first_mine, first_other = sum_nt([back[p][0] for p in range(nt)], wides, 0)
        total = grad_w[0].astype(F32)
        for q in sorted((q for q in got_w if got_w[q][0] == 0), reverse=True):
            got = got_w[q][1]
            total = total + (tie(got, first_mine) if q == 1 else got).astype(F32)
        grad_w = [total.astype(BF16)]
        own_half = lax.psum_scatter(
            grad_w[0],
            "dp",
            scatter_dimension=0,
            axis_index_groups=[list(range(0, ndp, 2)), list(range(1, ndp, 2))],
            tiled=True,
        )
        own_half = own_half.reshape(2, part, packed)
        kept = by_core(own_half[0], own_half[1]).astype(F32)
        got = swap_core(by_core(own_half[1], own_half[0])).astype(F32)
        halves = [by_core(kept, got), by_core(got, kept)]
        grad_qkv_own = jnp.stack(
            [
                jnp.concatenate([g[:, k * hh : (k + 1) * hh] for g in halves], axis=1)
                for k in range(3)
            ]
        )
        grad_out_own = jnp.concatenate([g[:, 3 * hh : 4 * hh] for g in halves], axis=1).T

        first_mine = tie(first_mine, grad_w[0])
        grad_first = first_mine.astype(F32) + swap_core(first_other).astype(F32)
        gain_one = jnp.sum(grad_first * normed_one, axis=0)
        shift_one = jnp.sum(grad_first, axis=0)
        grad_tokens = grad_hidden + norm_back(grad_first, normed_one, spread_one, gain_rows[0])

        output = hidden_one + tie(mlp_out, grad_w[0]) + shifts[3]

        spots = [by_core(t ^ p, t ^ reverse_bits(p)) for p in range(nt)]
        where = jnp.stack([c, by_core(t, t ^ top)] + spots).astype(jnp.int32)
        vectors = [gain_one, gain_two, shift_one, shift_out, shift_two, shift_fc2]
        total = pack_small(
            where,
            [v.reshape(1, width) for v in vectors],
            [back[p][2] for p in range(nt)],
            grad_fc1_bias,
            nt,
        )
        total = functools.reduce(jnp.add, [swap_tensor(total, i) for i in range(1, nt)], total)
        total = functools.reduce(jnp.add, [shift_z(total, k) for k in range(1, nz)], total)
        total = total + swap_core(total)
        own = lax.dynamic_slice_in_dim(
            total[0, :vec_count, :width], (d * nt + t) * piece, piece, axis=1
        )
        mine = lax.dynamic_index_in_dim(total, 1 + t, 0, keepdims=False)
        units = mine[1:5, : heads * LANES].reshape(2, 2, heads, LANES)[:, :, :, :HD]
        head_total = units.transpose(1, 0, 2, 3).reshape(2, block)
        bias_total = mine[0, :ff]
        return (
            output,
            grad_tokens,
            own[:gain_count],
            own[gain_count:],
            grad_qkv_own,
            head_total,
            grad_out_own,
            grad_fc1_own,
            bias_total,
            grad_fc2_own,
        )

    return body


def solution(mesh):
    in_specs = (
        P(("dp", "tensor"), None),
        P(None, ("dp", "tensor")),
        P(None, ("dp", "tensor")),
        P(None, "dp", "tensor"),
        P(None, "tensor"),
        P("tensor", "dp"),
        P("dp", "tensor"),
        P("tensor"),
        P("tensor", "dp"),
        P(("dp", "tensor"), None),
    )
    out_specs = (
        P(("dp", "tensor"), None),
        P(("dp", "tensor"), None),
        P(None, ("dp", "tensor")),
        P(None, ("dp", "tensor")),
        P(None, "dp", "tensor"),
        P(None, "tensor"),
        P("tensor", "dp"),
        P("dp", "tensor"),
        P("tensor"),
        P("tensor", "dp"),
    )
    body = make_body(mesh.shape["dp"], mesh.shape["tensor"])

    return jax.shard_map(body, mesh=mesh, in_specs=in_specs, out_specs=out_specs, check_vma=False)
```

profile of v0, /device:TPU:0, one launch (start us, length us, event | category | flops | bytes accessed | tf_op | source)
XLA Modules:
  0.0 440.1 jit_solution(13405107919071477726)
XLA Ops:
  12.7 3.0 collective-permute-start.1
  26.0 2.6 collective-permute-start.4
  36.5 14.2 %all-gather.4.cloned.1.call-done = bf16[2,1152,640]{2,1,0:T(8,128)(2,1)} async-done(((bf16[2,144,640]{2,1,0:T(8,128)(2,1)}), bf16[2,1152,640]{2,1,0:T(8,128)(2,1)}) %all-gather.4.cloned.1.call-update) | async-done | bytes 2949136 | tf_op jit(solution)/shard_map/all_gather | solution.py:550
  50.7 2.6 dynamic-slice_bitcast_fusion.w_ref
  57.0 2.3 slice_reduce_fusion
  60.9 2.3 fusion.9
  68.3 8.1 %collective-permute-done.9.w_ref = bf16[1152,640]{1,0:T(8,128)(2,1)} collective-permute-done((bf16[1152,640]{1,0:T(8,128)(2,1)}, bf16[1152,640]{1,0:T(8,128)(2,1)}, u32[]{:S(2)}, u32[]{:S(2)}) %collective-permute-start.9) | collective-permute-done | bytes 1474592 | tf_op jit(solution)/shard_map/ppermute | solution.py:486
  80.2 2.7 pad_maximum_fusion.rows_ref
  84.7 6.6 %attend.4 = (bf16[1024,768]{1,0:T(8,128)(2,1)S(1)}, bf16[1024,256]{1,0:T(8,128)(2,1)S(1)}, f32[1024,2]{1,0:T(8,128)S(1)}, bf16[1152,1024]{1,0:T(8,128)(2,1)S(1)}) custom-call(bf16[1024,1152]{1,0:T(8,128)(2,1)S(1)} %pad_maximum_fusion.rows_ref, bf16[1152,640]{1,0:T(8,128)(2,1)} %dynamic-slice_bitcast_fusion.w_ref, f32[2,256]{1,0:T(2,128)S(1)} %bitcast.94), custom_call_target="tpu_custom_call" | custom-call | flops 2080374784 | bytes 7405568 | tf_op jit(solution)/shard_map/attend/pallas_call | solution.py:104
  93.3 7.2 %attend.5 = (bf16[1024,768]{1,0:T(8,128)(2,1)S(1)}, bf16[1024,256]{1,0:T(8,128)(2,1)S(1)}, f32[1024,2]{1,0:T(8,128)S(1)}, bf16[1152,1024]{1,0:T(8,128)(2,1)S(1)}) custom-call(bf16[1024,1152]{1,0:T(8,128)(2,1)S(1)} %pad_maximum_fusion.rows_ref, bf16[1152,640]{1,0:T(8,128)(2,1)} %collective-permute-done.9.w_ref, f32[2,256]{1,0:T(2,128)S(1)} %bitcast.93), custom_call_target="tpu_custom_call" | custom-call | flops 2080374784 | bytes 7405568 | tf_op jit(solution)/shard_map/attend/pallas_call | solution.py:104
  102.6 4.8 %attend.6 = (bf16[1024,768]{1,0:T(8,128)(2,1)S(1)}, bf16[1024,256]{1,0:T(8,128)(2,1)S(1)}, f32[1024,2]{1,0:T(8,128)S(1)}, bf16[1152,1024]{1,0:T(8,128)(2,1)S(1)}) custom-call(bf16[1024,1152]{1,0:T(8,128)(2,1)S(1)} %pad_maximum_fusion.rows_ref, bf16[1152,640]{1,0:T(8,128)(2,1)S(1)} %collective-permute-done.10.w_ref, f32[2,256]{1,0:T(2,128)S(1)} %bitcast.92), custom_call_target="tpu_custom_call" | custom-call | flops 2080374784 | bytes 7405568 | tf_op jit(solution)/shard_map/attend/pallas_call | solution.py:104
  109.3 4.8 %attend.7 = (bf16[1024,768]{1,0:T(8,128)(2,1)S(1)}, bf16[1024,256]{1,0:T(8,128)(2,1)S(1)}, f32[1024,2]{1,0:T(8,128)S(1)}, bf16[1152,1024]{1,0:T(8,128)(2,1)S(1)}) custom-call(bf16[1024,1152]{1,0:T(8,128)(2,1)S(1)} %pad_maximum_fusion.rows_ref, bf16[1152,640]{1,0:T(8,128)(2,1)S(1)} %collective-permute-done.13.w_ref, f32[2,256]{1,0:T(2,128)S(1)} %bitcast.91), custom_call_target="tpu_custom_call" | custom-call | flops 2080374784 | bytes 7405568 | tf_op jit(solution)/shard_map/attend/pallas_call | solution.py:104
  114.2 5.0 %sum_nt.2 = (bf16[512,1152]{1,0:T(8,128)(2,1)S(1)}, bf16[512,1152]{1,0:T(8,128)(2,1)}) custom-call(bf16[1024,256]{1,0:T(8,128)(2,1)S(1)} %get-tuple-element.75.refs_0_.mixed_ref, bf16[1024,256]{1,0:T(8,128)(2,1)S(1)} %get-tuple-element.76.refs_1_.mixed_ref, bf16[1024,256]{1,0:T(8,128)(2,1)S(1)} %get-tuple-element.78.refs_2_.mixed_ref, ...), custom_call_target="tpu_custom_call" | custom-call | flops 2415919104 | bytes 6815744 | tf_op jit(solution)/shard_map/sum_nt/pallas_call | solution.py:252
  123.2 2.3 collective-permute-start.16
  125.6 2.6 fusion.45
  135.9 7.4 %feed_in.2 = (bf16[1024,1152]{1,0:T(8,128)(2,1)S(1)}, bf16[1024,1152]{1,0:T(8,128)(2,1)S(1)}, bf16[1024,1152]{1,0:T(8,128)(2,1)S(1)}) custom-call(s32[1]{0:T(128)} %bitcast.20.core_ref, bf16[512,1152]{1,0:T(8,128)(2,1)} %add_convert_fusion.4.rows0, bf16[512,1152]{1,0:T(8,128)(2,1)} %collective-permute-done.15.rows1, bf16[1152,1152]{1,0:T(8,128)(2,1)S(1)} %copy-done.36, ...), custom_call_target="tpu_custom_call" | custom-call | flops 2717908992 | bytes 12091392 | tf_op jit(solution)/shard_map/feed_in/pallas_call | solution.py:322
  143.4 3.3 fusion.53
  146.7 13.1 %collective-permute-done.17.rows0 = bf16[512,1152]{1,0:T(8,128)(2,1)} collective-permute-done((bf16[512,1152]{1,0:T(8,128)(2,1)}, bf16[512,1152]{1,0:T(8,128)(2,1)}, u32[]{:S(2)}, u32[]{:S(2)}) %collective-permute-start.17) | collective-permute-done | bytes 1179680 | tf_op jit(solution)/shard_map/ppermute | solution.py:486
  159.8 11.5 %collective-permute-start.18 = (bf16[512,1152]{1,0:T(8,128)(2,1)}, bf16[512,1152]{1,0:T(8,128)(2,1)S(1)}, u32[]{:S(2)}, u32[]{:S(2)}) collective-permute-start(bf16[512,1152]{1,0:T(8,128)(2,1)} %collective-permute-done.17.rows0), channel_id=1, source_target_pairs={{0,4},{1,5},{2,6},{3,7},{4,0},{5,1},{6,2},{7,3},{8,12},{9,13},{10,... | collective-permute-start | bytes 3538952 | tf_op jit(solution)/shard_map/ppermute | solution.py:486
  171.3 2.7 collective-permute-done.18.rows1
  174.0 7.1 %feed_in.3 = (bf16[1024,1152]{1,0:T(8,128)(2,1)S(1)}, bf16[1024,1152]{1,0:T(8,128)(2,1)S(1)}, bf16[1024,1152]{1,0:T(8,128)(2,1)S(1)}) custom-call(s32[1]{0:T(128)} %bitcast.20.core_ref, bf16[512,1152]{1,0:T(8,128)(2,1)} %collective-permute-done.17.rows0, bf16[512,1152]{1,0:T(8,128)(2,1)S(1)} %collective-permute-done.18.rows1, ...), custom_call_target="tpu_custom_call" | custom-call | flops 2717908992 | bytes 12091392 | tf_op jit(solution)/shard_map/feed_in/pallas_call | solution.py:322
  182.5 4.8 %fusion = bf16[1152,1152]{1,0:T(8,128)(2,1)} fusion(f32[1152,1152]{1,0:T(8,128)S(1)} %fusion.53, bf16[1024,1152]{1,0:T(8,128)(2,1)S(1)} %copy-done.78, bf16[1024,1152]{1,0:T(8,128)(2,1)S(1)} %get-tuple-element.90.act_ref), kind=kOutput, calls=%fused_computation.2 | convolution fusion | flops 2720563200 | bytes 12681216 | tf_op jit(solution)/shard_map/dot_general | solution.py:48
  187.3 2.5 collective-permute-start.25
  189.9 13.9 %feed_out.2 = (bf16[1024,1152]{1,0:T(8,128)(2,1)S(1)}, bf16[512,1152]{1,0:T(8,128)(2,1)S(1)}, bf16[512,1152]{1,0:T(8,128)(2,1)}, bf16[512,1152]{1,0:T(8,128)(2,1...) custom-call(s32[1]{0:T(128)} %bitcast.20.core_ref, bf16[512,1152]{1,0:T(8,128)(2,1)} %collective-permute-done.8.cot0, ...), custom_call_target="tpu_custom_call" | custom-call | flops 8153726976 | bytes 19464192 | tf_op jit(solution)/shard_map/feed_out/pallas_call | solution.py:400
  204.9 3.3 collective-permute-start.20
  208.2 2.5 collective-permute-done.20
  212.0 12.0 %feed_out.3 = (bf16[1024,1152]{1,0:T(8,128)(2,1)S(1)}, bf16[512,1152]{1,0:T(8,128)(2,1)S(1)}, bf16[512,1152]{1,0:T(8,128)(2,1)S(1)}, bf16[512,1152]{1,0:T(8,128)...) custom-call(s32[1]{0:T(128)} %bitcast.20.core_ref, bf16[512,1152]{1,0:T(8,128)(2,1)S(1)} %copy-done, ...), custom_call_target="tpu_custom_call" | custom-call | flops 8153726976 | bytes 19464192 | tf_op jit(solution)/shard_map/feed_out/pallas_call | solution.py:400
  229.6 3.5 broadcast_select_fusion.1
  233.3 5.8 %fusion.54 = f32[1152,1152]{1,0:T(8,128)S(1)} fusion(bf16[1024,1152]{1,0:T(8,128)(2,1)} %copy-done.42, bf16[1024,1152]{1,0:T(8,128)(2,1)} %copy-done.65), kind=kOutput, calls=%fused_computation.148 | convolution fusion | flops 2717908992 | bytes 10027008 | tf_op jit(solution)/shard_map/dot_general | solution.py:48
  239.2 3.4 fusion.1
  243.5 2.1 collective-permute-start.24
  245.6 3.9 collective-permute-start.23
  249.6 19.4 %collective-permute-done.24 = bf16[512,1152]{1,0:T(8,128)(2,1)S(1)} collective-permute-done((bf16[512,1152]{1,0:T(8,128)(2,1)S(1)}, bf16[512,1152]{1,0:T(8,128)(2,1)S(1)}, u32[]{:S(2)}, u32[]{:S(2)}) %collective-permute-start.24) | collective-permute-done | bytes 1179680 | tf_op jit(solution)/shard_map/ppermute | solution.py:486
  274.3 3.4 collective-permute-start.27
  283.8 9.1 %attend_back.4 = (bf16[1024,768]{1,0:T(8,128)(2,1)S(1)}, bf16[1152,640]{1,0:T(8,128)(2,1)}, f32[2,256]{1,0:T(2,128)S(1)}) custom-call(bf16[1024,1152]{1,0:T(8,128)(2,1)S(1)} %pad_maximum_fusion.1.grad_ref, bf16[1024,1152]{1,0:T(8,128)(2,1)S(1)} %pad_maximum_fusion.rows_ref, bf16[1152,1024]{1,0:T(8,128)(2,1)S(1)} %copy-done.11, ...), custom_call_target="tpu_custom_call" | custom-call | flops 3690987520 | bytes 10452992 | tf_op jit(solution)/shard_map/attend_back/pallas_call | solution.py:197
  308.8 8.0 %attend_back.5 = (bf16[1024,768]{1,0:T(8,128)(2,1)S(1)}, bf16[1152,640]{1,0:T(8,128)(2,1)S(1)}, f32[2,256]{1,0:T(2,128)S(1)}) custom-call(bf16[1024,1152]{1,0:T(8,128)(2,1)S(1)} %copy-done.2, bf16[1024,1152]{1,0:T(8,128)(2,1)S(1)} %pad_maximum_fusion.rows_ref, bf16[1152,1024]{1,0:T(8,128)(2,1)S(1)} %copy-done.8, bf16[1024,768]{1,0:T(8,128)(2,1)S(1)} %copy-done.50, ...), custom_call_target="tpu_custom_call" | custom-call | flops 3690987520 | bytes 10452992 | tf_op jit(solution)/shard_map/attend_back/pallas_call | solution.py:197
  317.2 8.3 %attend_back.6 = (bf16[1024,768]{1,0:T(8,128)(2,1)S(1)}, bf16[1152,640]{1,0:T(8,128)(2,1)S(1)}, f32[2,256]{1,0:T(2,128)S(1)}) custom-call(bf16[1024,1152]{1,0:T(8,128)(2,1)S(1)} %copy-done.2, bf16[1024,1152]{1,0:T(8,128)(2,1)S(1)} %pad_maximum_fusion.rows_ref, bf16[1152,1024]{1,0:T(8,128)(2,1)S(1)} %copy-done.6, bf16[1024,768]{1,0:T(8,128)(2,1)S(1)} %copy-done.48, ...), custom_call_target="tpu_custom_call" | custom-call | flops 3690987520 | bytes 10452992 | tf_op jit(solution)/shard_map/attend_back/pallas_call | solution.py:197
  328.8 8.0 %attend_back.7 = (bf16[1024,768]{1,0:T(8,128)(2,1)S(1)}, bf16[1152,640]{1,0:T(8,128)(2,1)S(1)}, f32[2,256]{1,0:T(2,128)S(1)}) custom-call(bf16[1024,1152]{1,0:T(8,128)(2,1)S(1)} %copy-done.2, bf16[1024,1152]{1,0:T(8,128)(2,1)S(1)} %pad_maximum_fusion.rows_ref, bf16[1152,1024]{1,0:T(8,128)(2,1)S(1)} %copy-done.4, bf16[1024,768]{1,0:T(8,128)(2,1)S(1)} %copy-done.46, ...), custom_call_target="tpu_custom_call" | custom-call | flops 3690987520 | bytes 10452992 | tf_op jit(solution)/shard_map/attend_back/pallas_call | solution.py:197
  336.9 9.9 %sum_nt.3 = (bf16[512,1152]{1,0:T(8,128)(2,1)S(1)}, bf16[512,1152]{1,0:T(8,128)(2,1)S(1)}) custom-call(bf16[1024,768]{1,0:T(8,128)(2,1)S(1)} %get-tuple-element.123.refs_0_, bf16[1024,768]{1,0:T(8,128)(2,1)S(1)} %get-tuple-element.124.refs_1_, bf16[1024,768]{1,0:T(8,128)(2,1)S(1)} %get-tuple-element.125.refs_2_, bf16[1024,768]{1,0:T(8,128)(2,1)S(1)} %copy-done.54, ...), custom_call_target="tpu_custom_call" | custom-call | flops 7247757312 | bytes 15728640 | tf_op jit(solution)/shard_map/sum_nt/pallas_call | solution.py:252
  348.9 15.2 %collective-permute-done.31 = bf16[1152,640]{1,0:T(8,128)(2,1)S(1)} collective-permute-done((bf16[1152,640]{1,0:T(8,128)(2,1)S(1)}, bf16[1152,640]{1,0:T(8,128)(2,1)S(1)}, u32[]{:S(2)}, u32[]{:S(2)}) %collective-permute-start.31) | collective-permute-done | bytes 1474592 | tf_op jit(solution)/shard_map/ppermute | solution.py:486
  365.9 2.5 fusion.14
  374.7 2.2 collective-permute-done.33
  376.9 4.0 collective-permute-done.34
  383.8 2.3 collective-permute-start.38
  386.1 4.5 %fusion.13 = f32[512,1152]{1,0:T(8,128)} fusion(f32[512,1152]{1,0:T(8,128)} %copy-done.71, bf16[512,1152]{1,0:T(8,128)(2,1)S(1)} %copy-done.70, bf16[512,1152]{1,0:T(8,128)(2,1)} %collective-permute-done.32, bf16[512,1152]{1,0:T(8,128)(2,1)S(1)} %get-tuple-element.130, f32[512]{0:T(512)S(1)} %broadcast_multiply_fusion, f32[512]{0:T(512)S(1)} %broadcast_multiply_fusion.1, ...), kind=kLoop, calls=%fused_computation.24 | loop fusion | flops 7077888 | bytes 8270336 | tf_op jit(solution)/shard_map/add | solution.py:723
  390.6 16.3 %collective-permute-done.37 = f32[5,8,1152]{2,1,0:T(8,128)S(1)} collective-permute-done((f32[5,8,1152]{2,1,0:T(8,128)S(1)}, f32[5,8,1152]{2,1,0:T(8,128)S(1)}, u32[]{:S(2)}, u32[]{:S(2)}) %collective-permute-start.37) | collective-permute-done | bytes 184352 | tf_op jit(solution)/shard_map/ppermute | solution.py:486
  407.3 2.6 collective-permute-start.39
  416.0 10.5 %reduce-scatter.4.cloned.1.call-done = bf16[288,640]{1,0:T(8,128)(2,1)} async-done(((bf16[1152,640]{1,0:T(8,128)(2,1)}), bf16[288,640]{1,0:T(8,128)(2,1)}) %reduce-scatter.4.cloned.1.call-update) | async-done | bytes 368656 | tf_op jit(solution)/shard_map/reduce_scatter | solution.py:700
  (404 shorter events, 123.9 us)
Async XLA Ops:
  7.2 43.5 %all-gather.4.cloned.1.call-start = ((), (), s32[]{:S(2)}) async-start(), calls=%async_computation.3 | async-start | bytes 3317760 | tf_op jit(solution)/shard_map/all_gather | solution.py:550
  10.9 112.3 %all-gather.6.cloned.1.call-start = ((), (), s32[]{:S(2)}) async-start(), calls=%async_computation.4 | async-start | bytes 2985984 | tf_op jit(solution)/shard_map/all_gather | solution.py:559
  11.7 121.5 %all-gather.8.cloned.1.call-start = ((), (), s32[]{:S(2)}) async-start(), calls=%async_computation.5 | async-start | bytes 2985984 | tf_op jit(solution)/shard_map/all_gather | solution.py:559
  12.7 10.1 %collective-permute-start.1 = (f32[1868]{0:T(1024)}, f32[1868]{0:T(1024)S(1)}, u32[]{:S(2)}, u32[]{:S(2)}) collective-permute-start(f32[1868]{0:T(1024)} %concatenate.39), channel_id=1, source_target_pairs={{0,2},{1,3},{2,0},{3,1},{4,6},{5,7},{6,4},{7,5},{8,10},{9,11},{10,... | collective-permute-start | bytes 22424 | tf_op jit(solution)/shard_map/ppermute | solution.py:486
  15.7 7.1 %collective-permute-start = (f32[1868]{0:T(1024)}, f32[1868]{0:T(1024)}, u32[]{:S(2)}, u32[]{:S(2)}) collective-permute-start(f32[1868]{0:T(1024)} %concatenate.39), channel_id=1, source_target_pairs={{0,1},{1,0},{2,3},{3,2},{4,5},{5,4},{6,7},{7,6},{8,9},{9,8},{10,11... | collective-permute-start | bytes 22424 | tf_op jit(solution)/shard_map/ppermute | solution.py:486
  17.2 5.6 %collective-permute-start.2 = (f32[1868]{0:T(1024)}, f32[1868]{0:T(1024)}, u32[]{:S(2)}, u32[]{:S(2)}) collective-permute-start(f32[1868]{0:T(1024)} %concatenate.39), channel_id=1, source_target_pairs={{0,3},{1,2},{2,1},{3,0},{4,7},{5,6},{6,5},{7,4},{8,11},{9,10},{10,... | collective-permute-start | bytes 22424 | tf_op jit(solution)/shard_map/ppermute | solution.py:486
  17.2 36.1 %collective-permute-start.8 = (bf16[512,1152]{1,0:T(8,128)(2,1)S(1)}, bf16[512,1152]{1,0:T(8,128)(2,1)}, u32[]{:S(2)}, u32[]{:S(2)}) collective-permute-start(bf16[512,1152]{1,0:T(8,128)(2,1)S(1)} %copy-done), channel_id=1, source_target_pairs={{0,1},{1,0},{2,3},{3,2},{4,5},{5,4},{6,7},{7,6},{8,9},{9,8},{10,11... | collective-permute-start | bytes 3538952 | tf_op jit(solution)/shard_map/ppermute | solution.py:486
  19.2 60.0 %collective-permute-start.11 = (bf16[512,1152]{1,0:T(8,128)(2,1)S(1)}, bf16[512,1152]{1,0:T(8,128)(2,1)S(1)}, u32[]{:S(2)}, u32[]{:S(2)}) collective-permute-start(bf16[512,1152]{1,0:T(8,128)(2,1)S(1)} %copy-done), channel_id=1, source_target_pairs={{0,4},{1,5},{2,6},{3,7},{4,0},{5,1},{6,2},{7,3},{8,12},{9,13},{10,... | collective-permute-start | bytes 3538952 | tf_op jit(solution)/shard_map/ppermute | solution.py:486
  21.0 393.2 %reduce-scatter.8.cloned.1.call-start = ((), (), s32[]{:S(2)}) async-start(), calls=%async_computation.8 | async-start | bytes 2985984 | tf_op jit(solution)/shard_map/reduce_scatter | solution.py:647
  24.4 5.7 %collective-permute-start.3 = (f32[4,216]{1,0:T(4,128)S(1)}, f32[4,216]{1,0:T(4,128)S(1)}, u32[]{:S(2)}, u32[]{:S(2)}) collective-permute-start(f32[4,216]{1,0:T(4,128)S(1)} %pad_maximum_fusion.9), channel_id=1, source_target_pairs={{0,8},{1,9},{2,10},{3,11},{4,12},{5,13},{6,14},{7,15},{8,16},{9,17... | collective-permute-start | bytes 10376 | tf_op jit(solution)/shard_map/ppermute | solution.py:486
  26.0 4.8 %collective-permute-start.4 = (f32[4,216]{1,0:T(4,128)S(1)}, f32[4,216]{1,0:T(4,128)S(1)}, u32[]{:S(2)}, u32[]{:S(2)}) collective-permute-start(f32[4,216]{1,0:T(4,128)S(1)} %pad_maximum_fusion.9), channel_id=1, source_target_pairs={{0,16},{1,17},{2,18},{3,19},{4,20},{5,21},{6,22},{7,23},{8,24},{9,... | collective-permute-start | bytes 10376 | tf_op jit(solution)/shard_map/ppermute | solution.py:486
  28.6 3.9 collective-permute-start.5
  32.6 2.6 collective-permute-start.6
  53.4 23.0 %collective-permute-start.9 = (bf16[1152,640]{1,0:T(8,128)(2,1)}, bf16[1152,640]{1,0:T(8,128)(2,1)}, u32[]{:S(2)}, u32[]{:S(2)}) collective-permute-start(bf16[1152,640]{1,0:T(8,128)(2,1)} %dynamic-slice_bitcast_fusion.w_ref), channel_id=1, source_target_pairs={{0,1},{1,0},{2,3},{3,2},{4,6},{5,7},{6,4},{7,5},{8,9},{9,8},{10,11... | collective-permute-start | bytes 4423688 | tf_op jit(solution)/shard_map/ppermute | solution.py:486
  63.1 17.1 %collective-permute-start.7 = (bf16[512,1152]{1,0:T(8,128)(2,1)}, bf16[512,1152]{1,0:T(8,128)(2,1)}, u32[]{:S(2)}, u32[]{:S(2)}) collective-permute-start(bf16[512,1152]{1,0:T(8,128)(2,1)} %fusion.9), channel_id=1, source_target_pairs={{0,4},{1,5},{2,6},{3,7},{4,0},{5,1},{6,2},{7,3},{8,12},{9,13},{10,... | collective-permute-start | bytes 3538952 | tf_op jit(solution)/shard_map/ppermute | solution.py:486
  66.1 16.8 %collective-permute-start.12 = (bf16[512,1152]{1,0:T(8,128)(2,1)}, bf16[512,1152]{1,0:T(8,128)(2,1)S(1)}, u32[]{:S(2)}, u32[]{:S(2)}) collective-permute-start(bf16[512,1152]{1,0:T(8,128)(2,1)} %collective-permute-done.8.cot0), channel_id=1, source_target_pairs={{0,4},{1,5},{2,6},{3,7},{4,0},{5,1},{6,2},{7,3},{8,12},{9,13},{10,... | collective-permute-start | bytes 3538952 | tf_op jit(solution)/shard_map/ppermute | solution.py:486
  66.7 35.8 %collective-permute-start.10 = (bf16[1152,640]{1,0:T(8,128)(2,1)}, bf16[1152,640]{1,0:T(8,128)(2,1)S(1)}, u32[]{:S(2)}, u32[]{:S(2)}) collective-permute-start(bf16[1152,640]{1,0:T(8,128)(2,1)} %dynamic-slice_bitcast_fusion.w_ref), channel_id=1, source_target_pairs={{0,2},{1,3},{2,0},{3,1},{4,5},{5,4},{6,7},{7,6},{8,10},{9,11},{10,... | collective-permute-start | bytes 4423688 | tf_op jit(solution)/shard_map/ppermute | solution.py:486
  76.4 33.0 %collective-permute-start.13 = (bf16[1152,640]{1,0:T(8,128)(2,1)}, bf16[1152,640]{1,0:T(8,128)(2,1)S(1)}, u32[]{:S(2)}, u32[]{:S(2)}) collective-permute-start(bf16[1152,640]{1,0:T(8,128)(2,1)} %collective-permute-done.9.w_ref), channel_id=1, source_target_pairs={{0,2},{1,3},{2,0},{3,1},{4,5},{5,4},{6,7},{7,6},{8,10},{9,11},{10,... | collective-permute-start | bytes 4423688 | tf_op jit(solution)/shard_map/ppermute | solution.py:486
  120.3 5.3 %collective-permute-start.14 = (bf16[512,1152]{1,0:T(8,128)(2,1)}, bf16[512,1152]{1,0:T(8,128)(2,1)}, u32[]{:S(2)}, u32[]{:S(2)}) collective-permute-start(bf16[512,1152]{1,0:T(8,128)(2,1)} %get-tuple-element.85), channel_id=1, source_target_pairs={{0,4},{1,5},{2,6},{3,7},{4,0},{5,1},{6,2},{7,3},{8,12},{9,13},{10,... | collective-permute-start | bytes 3538952 | tf_op jit(solution)/shard_map/ppermute | solution.py:486
  123.2 10.9 %collective-permute-start.16 = (bf16[1152,1152]{1,0:T(8,128)(2,1)}, bf16[1152,1152]{1,0:T(8,128)(2,1)}, u32[]{:S(2)}, u32[]{:S(2)}) collective-permute-start(bf16[1152,1152]{1,0:T(8,128)(2,1)} %all-gather.6.cloned.1.call-done.w1_own), channel_id=1, source_target_pairs={{4,6},{5,7},{6,4},{7,5},{12,14},{13,15},{14,12},{15,13},{20,22},{2... | collective-permute-start | bytes 7962632 | tf_op jit(solution)/shard_map/ppermute | solution.py:507
  130.5 3.6 collective-permute-start.15
  131.1 28.7 %collective-permute-start.17 = (bf16[512,1152]{1,0:T(8,128)(2,1)}, bf16[512,1152]{1,0:T(8,128)(2,1)}, u32[]{:S(2)}, u32[]{:S(2)}) collective-permute-start(bf16[512,1152]{1,0:T(8,128)(2,1)} %add_convert_fusion.4.rows0), channel_id=1, source_target_pairs={{0,1},{1,0},{2,3},{3,2},{4,5},{5,4},{6,7},{7,6},{8,9},{9,8},{10,11... | collective-permute-start | bytes 3538952 | tf_op jit(solution)/shard_map/ppermute | solution.py:486
  133.3 56.6 %collective-permute-start.19 = (bf16[1152,1152]{1,0:T(8,128)(2,1)}, bf16[1152,1152]{1,0:T(8,128)(2,1)S(1)}, u32[]{:S(2)}, u32[]{:S(2)}) collective-permute-start(bf16[1152,1152]{1,0:T(8,128)(2,1)} %all-gather.8.cloned.1.call-done.w2_own), channel_id=1, source_target_pairs={{4,6},{5,7},{6,4},{7,5},{12,14},{13,15},{14,12},{15,13},{20,22},{2... | collective-permute-start | bytes 7962632 | tf_op jit(solution)/shard_map/ppermute | solution.py:507
  146.7 35.8 %copy-start.78 = (bf16[1024,1152]{1,0:T(8,128)(2,1)S(1)}, bf16[1024,1152]{1,0:T(8,128)(2,1)}, u32[]{:S(2)}) copy-start(bf16[1024,1152]{1,0:T(8,128)(2,1)} %copy-done.77) | copy-start | bytes 7077892
  159.8 14.2 %collective-permute-start.18 = (bf16[512,1152]{1,0:T(8,128)(2,1)}, bf16[512,1152]{1,0:T(8,128)(2,1)S(1)}, u32[]{:S(2)}, u32[]{:S(2)}) collective-permute-start(bf16[512,1152]{1,0:T(8,128)(2,1)} %collective-permute-done.17.rows0), channel_id=1, source_target_pairs={{0,4},{1,5},{2,6},{3,7},{4,0},{5,1},{6,2},{7,3},{8,12},{9,13},{10,... | collective-permute-start | bytes 3538952 | tf_op jit(solution)/shard_map/ppermute | solution.py:486
  187.3 42.3 %collective-permute-start.25 = (bf16[1152,1152]{1,0:T(8,128)(2,1)}, bf16[1152,1152]{1,0:T(8,128)(2,1)}, u32[]{:S(2)}, u32[]{:S(2)}) collective-permute-start(bf16[1152,1152]{1,0:T(8,128)(2,1)} %fusion), channel_id=1, source_target_pairs={{4,6},{5,7},{6,4},{7,5},{12,14},{13,15},{14,12},{15,13},{20,22},{2... | collective-permute-start | bytes 7962632 | tf_op jit(solution)/shard_map/ppermute | solution.py:507
  204.9 5.8 %collective-permute-start.20 = (bf16[512,1152]{1,0:T(8,128)(2,1)S(1)}, bf16[512,1152]{1,0:T(8,128)(2,1)S(1)}, u32[]{:S(2)}, u32[]{:S(2)}) collective-permute-start(bf16[512,1152]{1,0:T(8,128)(2,1)S(1)} %get-tuple-element.94), channel_id=1, source_target_pairs={{0,4},{1,5},{2,6},{3,7},{4,0},{5,1},{6,2},{7,3},{8,12},{9,13},{10,... | collective-permute-start | bytes 3538952 | tf_op jit(solution)/shard_map/ppermute | solution.py:486
  233.2 182.8 %reduce-scatter.6.cloned.1.call-start = ((), (), s32[]{:S(2)}) async-start(), calls=%async_computation.7 | async-start | bytes 2985984 | tf_op jit(solution)/shard_map/reduce_scatter | solution.py:647
  242.6 35.1 %collective-permute-start.29 = (bf16[1152,1152]{1,0:T(8,128)(2,1)S(1)}, bf16[1152,1152]{1,0:T(8,128)(2,1)S(1)}, u32[]{:S(2)}, u32[]{:S(2)}) collective-permute-start(bf16[1152,1152]{1,0:T(8,128)(2,1)S(1)} %fusion.1), channel_id=1, source_target_pairs={{4,6},{5,7},{6,4},{7,5},{12,14},{13,15},{14,12},{15,13},{20,22},{2... | collective-permute-start | bytes 7962632 | tf_op jit(solution)/shard_map/ppermute | solution.py:507
  243.5 25.4 %collective-permute-start.24 = (bf16[512,1152]{1,0:T(8,128)(2,1)S(1)}, bf16[512,1152]{1,0:T(8,128)(2,1)S(1)}, u32[]{:S(2)}, u32[]{:S(2)}) collective-permute-start(bf16[512,1152]{1,0:T(8,128)(2,1)S(1)} %copy-done.73), channel_id=1, source_target_pairs={{0,1},{1,0},{2,3},{3,2},{4,5},{5,4},{6,7},{7,6},{8,9},{9,8},{10,11... | collective-permute-start | bytes 3538952 | tf_op jit(solution)/shard_map/ppermute | solution.py:486
  245.6 23.3 %collective-permute-start.23 = (bf16[512,1152]{1,0:T(8,128)(2,1)S(1)}, bf16[512,1152]{1,0:T(8,128)(2,1)S(1)}, u32[]{:S(2)}, u32[]{:S(2)}) collective-permute-start(bf16[512,1152]{1,0:T(8,128)(2,1)S(1)} %copy-done.41), channel_id=1, source_target_pairs={{0,4},{1,5},{2,6},{3,7},{4,0},{5,1},{6,2},{7,3},{8,12},{9,13},{10,... | collective-permute-start | bytes 3538952 | tf_op jit(solution)/shard_map/ppermute | solution.py:486
  249.5 49.9 %collective-permute-start.22 = (bf16[512,1152]{1,0:T(8,128)(2,1)}, bf16[512,1152]{1,0:T(8,128)(2,1)}, u32[]{:S(2)}, u32[]{:S(2)}) collective-permute-start(bf16[512,1152]{1,0:T(8,128)(2,1)} %get-tuple-element.99), channel_id=1, source_target_pairs={{0,4},{1,5},{2,6},{3,7},{4,0},{5,1},{6,2},{7,3},{8,12},{9,13},{10,... | collective-permute-start | bytes 3538952 | tf_op jit(solution)/shard_map/ppermute | solution.py:486
  274.3 6.0 %collective-permute-start.27 = (bf16[512,1152]{1,0:T(8,128)(2,1)S(1)}, bf16[512,1152]{1,0:T(8,128)(2,1)}, u32[]{:S(2)}, u32[]{:S(2)}) collective-permute-start(bf16[512,1152]{1,0:T(8,128)(2,1)S(1)} %convert_element_type.147), channel_id=1, source_target_pairs={{0,4},{1,5},{2,6},{3,7},{4,0},{5,1},{6,2},{7,3},{8,12},{9,13},{10,... | collective-permute-start | bytes 3538952 | tf_op jit(solution)/shard_map/ppermute | solution.py:486
  279.5 147.0 %reduce-scatter.4.cloned.1.call-start = ((), (), s32[]{:S(2)}) async-start(), calls=%async_computation.6 | async-start | bytes 1843200 | tf_op jit(solution)/shard_map/reduce_scatter | solution.py:700
  294.8 30.8 %collective-permute-start.28 = (bf16[1152,640]{1,0:T(8,128)(2,1)}, bf16[1152,640]{1,0:T(8,128)(2,1)}, u32[]{:S(2)}, u32[]{:S(2)}) collective-permute-start(bf16[1152,640]{1,0:T(8,128)(2,1)} %get-tuple-element.116), channel_id=1, source_target_pairs={{0,2},{1,3},{2,0},{3,1},{4,5},{5,4},{6,7},{7,6},{8,10},{9,11},{10,... | collective-permute-start | bytes 4423688 | tf_op jit(solution)/shard_map/ppermute | solution.py:486
  298.6 48.3 %collective-permute-start.21 = (bf16[512,1152]{1,0:T(8,128)(2,1)}, bf16[512,1152]{1,0:T(8,128)(2,1)S(1)}, u32[]{:S(2)}, u32[]{:S(2)}) collective-permute-start(bf16[512,1152]{1,0:T(8,128)(2,1)} %copy-done.39), channel_id=1, source_target_pairs={{0,4},{1,5},{2,6},{3,7},{4,0},{5,1},{6,2},{7,3},{8,12},{9,13},{10,... | collective-permute-start | bytes 3538952 | tf_op jit(solution)/shard_map/ppermute | solution.py:486
  303.6 43.3 %collective-permute-start.26 = (bf16[512,1152]{1,0:T(8,128)(2,1)S(1)}, bf16[512,1152]{1,0:T(8,128)(2,1)S(1)}, u32[]{:S(2)}, u32[]{:S(2)}) collective-permute-start(bf16[512,1152]{1,0:T(8,128)(2,1)S(1)} %add_convert_fusion.2), channel_id=1, source_target_pairs={{0,1},{1,0},{2,3},{3,2},{4,5},{5,4},{6,7},{7,6},{8,9},{9,8},{10,11... | collective-permute-start | bytes 3538952 | tf_op jit(solution)/shard_map/ppermute | solution.py:486
  316.8 47.2 %collective-permute-start.30 = (bf16[1152,640]{1,0:T(8,128)(2,1)S(1)}, bf16[1152,640]{1,0:T(8,128)(2,1)S(1)}, u32[]{:S(2)}, u32[]{:S(2)}) collective-permute-start(bf16[1152,640]{1,0:T(8,128)(2,1)S(1)} %get-tuple-element.118), channel_id=1, source_target_pairs={{0,2},{1,3},{2,0},{3,1},{4,5},{5,4},{6,7},{7,6},{8,10},{9,11},{10,... | collective-permute-start | bytes 4423688 | tf_op jit(solution)/shard_map/ppermute | solution.py:486
  327.4 36.6 %collective-permute-start.31 = (bf16[1152,640]{1,0:T(8,128)(2,1)S(1)}, bf16[1152,640]{1,0:T(8,128)(2,1)S(1)}, u32[]{:S(2)}, u32[]{:S(2)}) collective-permute-start(bf16[1152,640]{1,0:T(8,128)(2,1)S(1)} %add_convert_fusion.1), channel_id=1, source_target_pairs={{0,1},{1,0},{2,3},{3,2},{4,6},{5,7},{6,4},{7,5},{8,9},{9,8},{10,11... | collective-permute-start | bytes 4423688 | tf_op jit(solution)/shard_map/ppermute | solution.py:486
  346.8 19.0 %collective-permute-start.32 = (bf16[512,1152]{1,0:T(8,128)(2,1)S(1)}, bf16[512,1152]{1,0:T(8,128)(2,1)}, u32[]{:S(2)}, u32[]{:S(2)}) collective-permute-start(bf16[512,1152]{1,0:T(8,128)(2,1)S(1)} %get-tuple-element.131), channel_id=1, source_target_pairs={{0,4},{1,5},{2,6},{3,7},{4,0},{5,1},{6,2},{7,3},{8,12},{9,13},{10,... | collective-permute-start | bytes 3538952 | tf_op jit(solution)/shard_map/ppermute | solution.py:486
  371.1 5.7 %collective-permute-start.33 = (f32[5,8,1152]{2,1,0:T(8,128)}, f32[5,8,1152]{2,1,0:T(8,128)S(1)}, u32[]{:S(2)}, u32[]{:S(2)}) collective-permute-start(f32[5,8,1152]{2,1,0:T(8,128)} %pack_small.1), channel_id=1, source_target_pairs={{0,1},{1,0},{2,3},{3,2},{4,5},{5,4},{6,7},{7,6},{8,9},{9,8},{10,11... | collective-permute-start | bytes 552968 | tf_op jit(solution)/shard_map/ppermute | solution.py:486
  373.2 7.7 %collective-permute-start.34 = (f32[5,8,1152]{2,1,0:T(8,128)}, f32[5,8,1152]{2,1,0:T(8,128)S(1)}, u32[]{:S(2)}, u32[]{:S(2)}) collective-permute-start(f32[5,8,1152]{2,1,0:T(8,128)} %pack_small.1), channel_id=1, source_target_pairs={{0,2},{1,3},{2,0},{3,1},{4,6},{5,7},{6,4},{7,5},{8,10},{9,11},{10,... | collective-permute-start | bytes 552968 | tf_op jit(solution)/shard_map/ppermute | solution.py:486
  373.4 7.4 %collective-permute-start.35 = (f32[5,8,1152]{2,1,0:T(8,128)}, f32[5,8,1152]{2,1,0:T(8,128)S(1)}, u32[]{:S(2)}, u32[]{:S(2)}) collective-permute-start(f32[5,8,1152]{2,1,0:T(8,128)} %pack_small.1), channel_id=1, source_target_pairs={{0,3},{1,2},{2,1},{3,0},{4,7},{5,6},{6,5},{7,4},{8,11},{9,10},{10,... | collective-permute-start | bytes 552968 | tf_op jit(solution)/shard_map/ppermute | solution.py:486
  381.9 8.7 %collective-permute-start.36 = (f32[5,8,1152]{2,1,0:T(8,128)S(1)}, f32[5,8,1152]{2,1,0:T(8,128)S(1)}, u32[]{:S(2)}, u32[]{:S(2)}) collective-permute-start(f32[5,8,1152]{2,1,0:T(8,128)S(1)} %add_add_fusion.2), channel_id=1, source_target_pairs={{0,8},{1,9},{2,10},{3,11},{4,12},{5,13},{6,14},{7,15},{8,16},{9,17... | collective-permute-start | bytes 552968 | tf_op jit(solution)/shard_map/ppermute | solution.py:486
  382.6 24.3 %collective-permute-start.37 = (f32[5,8,1152]{2,1,0:T(8,128)S(1)}, f32[5,8,1152]{2,1,0:T(8,128)S(1)}, u32[]{:S(2)}, u32[]{:S(2)}) collective-permute-start(f32[5,8,1152]{2,1,0:T(8,128)S(1)} %add_add_fusion.2), channel_id=1, source_target_pairs={{0,16},{1,17},{2,18},{3,19},{4,20},{5,21},{6,22},{7,23},{8,24},{9,... | collective-permute-start | bytes 552968 | tf_op jit(solution)/shard_map/ppermute | solution.py:486
  383.8 23.5 %collective-permute-start.38 = (f32[5,8,1152]{2,1,0:T(8,128)S(1)}, f32[5,8,1152]{2,1,0:T(8,128)S(1)}, u32[]{:S(2)}, u32[]{:S(2)}) collective-permute-start(f32[5,8,1152]{2,1,0:T(8,128)S(1)} %add_add_fusion.2), channel_id=1, source_target_pairs={{0,24},{1,25},{2,26},{3,27},{4,28},{5,29},{6,30},{7,31},{8,0},{9,1... | collective-permute-start | bytes 552968 | tf_op jit(solution)/shard_map/ppermute | solution.py:486
  407.3 4.2 collective-permute-start.39
  427.6 1.9 collective-permute-start.40
  (108 other events, 739.0 us)
Sparse Core Ops, SparseCore 0:
  11.0 39.6 all-gather.3
  52.4 32.7 all-gather.5
  86.8 33.0 all-gather.7
  233.3 39.0 reduce-scatter.7
  279.6 37.7 reduce-scatter.5
  374.8 51.7 reduce-scatter.3
where the time goes:
time: 447 us; the launch traced here: 440 us
  Pallas kernels  114 us (26%)
  waiting for transfers between devices  112 us (25%)
  starting transfers between devices  67.1 us (15%)
  local copies, waits for them, and re-layouts  59.9 us (13%)
  other arithmetic  54.5 us (12%)
  matrix products  17.4 us (4%)
  between operations  15.8 us (4%)
    ppermute x37, waiting for transfers between devices, send(): return lax.ppermute(value, AXES, perm(move))  86.8 us
    ppermute x37, starting transfers between devices, send(): return lax.ppermute(value, AXES, perm(move))  60.1 us
    pallas_call x4, Pallas kernels, attend_back(): pl.pallas_call(functools.partial(attend_back_kernel, heads, images), grid...  33.4 us
    unnamed x225, local copies, waits for them, and re-layouts  31 us
    pallas_call x2, Pallas kernels, feed_out(): pl.pallas_call(functools.partial(feed_out_kernel, half), grid=(2 * half,)...  25.9 us
    pallas_call x4, Pallas kernels, attend(): pl.pallas_call(functools.partial(attend_kernel, heads, images), grid=(tot...  23.4 us
    dot_general x4, matrix products, dot_tn(): lax.dot_general(a, b, (((0,), (0,)), ((), ())), preferred_element_type=F32)  17.4 us
    pallas_call x2, Pallas kernels, sum_nt(): pl.pallas_call(functools.partial(sum_nt_kernel, count, half), grid=(2 * h...  14.9 us
  transfers between devices with their start and end apart: 47, of which 16 were waited for; matrix products, arithmetic and copies ran while one was open for 21% of the time, Pallas kernels for 26%

commit v1 on v0

v1 whole, which is shorter than its diff:
```python
import functools

import jax
import jax.numpy as jnp
from jax import lax
from jax.experimental import pallas as pl
from jax.experimental.pallas import tpu as pltpu
from jax.sharding import PartitionSpec as P


HD = 72
SEQ = 256
EPS = 1e-06
F32 = jnp.float32
BF16 = jnp.bfloat16
AXES = ("dp", "tensor")


def norm_rows(values, gain_row, shifts):
    center = values - jnp.mean(values, axis=-1, keepdims=True)
    spread = lax.rsqrt(jnp.mean(center * center, axis=-1, keepdims=True) + EPS)
    normed = center * spread
    return (normed * gain_row + shifts, normed, spread)


def norm_back(grad_rows, normed, spread, gain_row):
    scaled = grad_rows * gain_row
    return spread * (
        scaled
        - jnp.mean(scaled, axis=-1, keepdims=True)
        - normed * jnp.mean(scaled * normed, axis=-1, keepdims=True)
    )


def tie(value, *others):
    return lax.optimization_barrier((value, *others))[0]


def dot_nn(a, b):
    return lax.dot_general(a, b, (((1,), (0,)), ((), ())), preferred_element_type=F32)


def dot_nt(a, b):
    return lax.dot_general(a, b, (((1,), (1,)), ((), ())), preferred_element_type=F32)


def dot_tn(a, b):
    return lax.dot_general(a, b, (((0,), (0,)), ((), ())), preferred_element_type=F32)


LANES = 128
ATTEND_VMEM = 22 << 20
BACK_VMEM = 30 << 20
FEED_VMEM = 18 << 20
FEED_OUT_VMEM = 24 << 20
SUM_VMEM = 20 << 20


def far(x):
    return pltpu.with_memory_space_constraint(x, pltpu.HBM)


def padded(size):
    return -(-size // LANES) * LANES


class Columns:
    def __init__(self, hh):
        self.hh = hh
        self.heads = hh // HD
        self.packed = padded(4 * hh)
        self.three = padded(3 * hh + LANES - HD)
        self.low = 3 * hh // LANES * LANES
        self.window = self.packed - self.low
        self.shift = 3 * hh - self.low


def cut(array, start):
    lane = lax.broadcasted_iota(jnp.int32, (1, LANES), 1)
    piece = array[:, start : start + LANES]
    return jnp.where(lane < HD, piece, jnp.zeros_like(piece))


def place(pieces, before, width):
    rows = pieces[0].shape[0]
    parts = [piece[:, :HD] for piece in pieces]
    if before:
        parts.insert(0, jnp.zeros((rows, before), pieces[0].dtype))
    after = width - before - HD * len(pieces)
    if after:
        parts.append(jnp.zeros((rows, after), pieces[0].dtype))
    return jnp.concatenate(parts, axis=1)


def attend_kernel(cols, images, before, rows_ref, w_ref, scale_ref, bias_ref, *refs):
    lefts, rights, outs = refs[:before], refs[before : 3 * before], refs[3 * before :]
    qkv_ref, mixed_ref, lse_ref = outs[:3]
    heads, hh = cols.heads, cols.hh
    proj = dot_nn(rows_ref[...], w_ref[...])[:, : cols.three]
    qkv = ((proj + bias_ref[...]) * scale_ref[...]).astype(BF16)
    qkv_ref[...] = qkv
    units = [(m, h) for m in range(images) for h in range(heads)]

    def unit(kind, m, h):
        return cut(qkv[m * SEQ : (m + 1) * SEQ], kind * hh + h * HD)

    scores = [dot_nt(unit(0, m, h), unit(1, m, h)) for m, h in units]
    tops = [jnp.max(s, axis=-1, keepdims=True) for s in scores]
    exps = [jnp.exp(s - top) for s, top in zip(scores, tops)]
    sums = [jnp.sum(e, axis=-1, keepdims=True) for e in exps]
    probs = [(e * (1.0 / total)).astype(BF16) for e, total in zip(exps, sums)]
    mixed = [dot_nn(p, unit(2, m, h)).astype(BF16) for (m, h), p in zip(units, probs)]
    for m in range(images):
        rows = slice(m * SEQ, (m + 1) * SEQ)
        group = slice(m * heads, (m + 1) * heads)
        mixed_ref[rows, :] = place(mixed[group], cols.shift, cols.window)
        for h, (top, total) in enumerate(zip(tops[group], sums[group])):
            lse_ref[rows, h : h + 1] = top + jnp.log(total)
    if len(outs) == 3:
        return
    mine_ref, other_ref = outs[3:]
    total = dot_nt(mixed_ref[...], w_ref[:, cols.low :])
    for n, left in enumerate(lefts):
        right = jnp.concatenate([rights[2 * n][...], rights[2 * n + 1][...]], axis=1)
        total += dot_nt(left[...], right)
    value = total.astype(BF16)

    @pl.when(pl.program_id(0) == 0)
    def _():
        other_ref[...] = value

    @pl.when(pl.program_id(0) != 0)
    def _():
        mine_ref[...] = value


def attend(cols, rows, weight, scale, bias, before=None):
    total, width = rows.shape
    last = before is not None
    mixeds, weights = before if last else ((), ())
    tile = total // 2
    images = tile // SEQ
    turn = (lambda i: (lax.rem(i + 1, 2), 0)) if last else (lambda i: (i, 0))
    whole = lambda i: (0, 0)
    block = cols.low // LANES
    assert not last or cols.window == 2 * LANES
    rights = [w for weight in weights for w in (weight, weight)]
    out_specs = [
        pl.BlockSpec((tile, cols.three), turn),
        pl.BlockSpec((tile, cols.window), turn),
        pl.BlockSpec((tile, cols.heads), turn),
    ]
    out_shape = [
        pltpu.HBM((total, cols.three), BF16),
        pltpu.HBM((total, cols.window), BF16),
        pltpu.HBM((total, cols.heads), F32),
    ]
    if last:
        out_specs += [pl.BlockSpec((tile, width), whole)] * 2
        out_shape += [jax.ShapeDtypeStruct((tile, width), BF16), pltpu.HBM((tile, width), BF16)]
    return pl.pallas_call(
        functools.partial(attend_kernel, cols, images, len(mixeds)),
        grid=(2,),
        in_specs=[
            pl.BlockSpec((tile, width), turn),
            pl.BlockSpec(weight.shape, whole),
            pl.BlockSpec(scale.shape, whole),
            pl.BlockSpec(bias.shape, whole),
        ]
        + [pl.BlockSpec((tile, cols.window), turn)] * len(mixeds)
        + [
            pl.BlockSpec((width, LANES), lambda i, j=j: (0, block + j))
            for _ in weights
            for j in range(2)
        ],
        out_specs=out_specs,
        out_shape=out_shape,
        compiler_params=pltpu.CompilerParams(vmem_limit_bytes=ATTEND_VMEM),
        cost_estimate=pl.CostEstimate(
            flops=2 * total * width * cols.packed + 4 * total * SEQ * LANES * cols.heads,
            bytes_accessed=2 * (total * (width + 4 * cols.hh) + weight.size),
            transcendentals=total * SEQ * cols.heads,
        ),
        name="attend",
    )(far(rows), weight, scale, bias, *[far(m) for m in mixeds], *rights)


def attend_back_kernel(
    cols, images, extras, own_ref, other_hbm, rows_ref, w_ref, qkv_ref, mixed_ref, lse_ref, *refs
):
    extra_hbm = refs[:extras]
    proj_ref, gw_ref, sums_ref, acc, grad, other, sems = refs[extras : extras + 7]
    extra = refs[extras + 7 :]
    heads, hh = cols.heads, cols.hh
    step = pl.program_id(0)
    copies = [pltpu.make_async_copy(other_hbm, other, sems.at[0])] + [
        pltpu.make_async_copy(source, target, sems.at[1 + i])
        for i, (source, target) in enumerate(zip(extra_hbm, extra))
    ]

    @pl.when(step == 0)
    def _():
        for copy in copies:
            copy.start()
        grad[...] = own_ref[...]

    @pl.when(step != 0)
    def _():
        copies[0].wait()
        grad[...] = other[...]

    gh = grad[...]
    gmix = dot_nn(gh, w_ref[:, cols.low :]).astype(BF16)
    units = [(m, h) for m in range(images) for h in range(heads)]

    def unit(kind, m, h):
        return cut(qkv_ref[m * SEQ : (m + 1) * SEQ, :], kind * hh + h * HD)

    query = [unit(0, m, h) for m, h in units]
    keys = [unit(1, m, h) for m, h in units]
    vals = [unit(2, m, h) for m, h in units]
    gm = [cut(gmix[m * SEQ : (m + 1) * SEQ], cols.shift + h * HD) for m, h in units]
    lse = [lse_ref[m * SEQ : (m + 1) * SEQ, h : h + 1] for m, h in units]
    probs = [jnp.exp(dot_nt(q, k) - top) for q, k, top in zip(query, keys, lse)]
    dprobs = [dot_nt(g, v) for g, v in zip(gm, vals)]
    dots = [jnp.sum(p * dp, axis=-1, keepdims=True) for p, dp in zip(probs, dprobs)]
    dscores = [(p * (dp - dt)).astype(BF16) for p, dp, dt in zip(probs, dprobs, dots)]
    grads = [
        (
            dot_nn(dscores[n], keys[n]) * HD ** (-0.5),
            dot_tn(dscores[n], query[n]),
            dot_tn(probs[n].astype(BF16), gm[n]),
        )
        for n in range(len(units))
    ]
    sums = [[0.0] * heads for _ in range(2)]
    for n, (m, h) in enumerate(units):
        for row, kind in enumerate((0, 2)):
            sums[row][h] = sums[row][h] + jnp.sum(grads[n][kind], axis=0, keepdims=True)
    sums = jnp.concatenate([jnp.concatenate(s, axis=1) for s in sums], axis=0)
    for m in range(images):
        pieces = [
            grads[m * heads + h][kind].astype(BF16) for kind in range(3) for h in range(heads)
        ]
        proj_ref[m * SEQ : (m + 1) * SEQ, :] = place(pieces, 0, cols.three)
    gw_qkv = dot_tn(rows_ref[...], proj_ref[...])
    gw_out = dot_tn(gh, mixed_ref[...])

    @pl.when(step == 0)
    def _():
        acc[...] = jnp.zeros_like(acc)
        sums_ref[...] = sums

    @pl.when(step > 0)
    def _():
        sums_ref[...] += sums

    acc[:, : cols.three] += gw_qkv
    acc[:, cols.low :] += gw_out

    @pl.when(step != 0)
    def _():
        total = acc[...]
        for i in range(extras):
            copies[1 + i].wait()
            total += extra[i][...].astype(F32)
        gw_ref[...] = total.astype(BF16)


def attend_back(cols, grad_rows, rows, weight, qkv, mixed, lse, extra):
    total, width = rows.shape
    tile = total // 2
    images = tile // SEQ
    step = lambda i: (i, 0)
    whole = lambda i: (0, 0)
    lanes = cols.heads * LANES
    anywhere = pl.BlockSpec(memory_space=pl.ANY)
    own, other = grad_rows
    return pl.pallas_call(
        functools.partial(attend_back_kernel, cols, images, len(extra)),
        grid=(2,),
        in_specs=[
            pl.BlockSpec((tile, width), whole),
            anywhere,
            pl.BlockSpec((tile, width), step),
            pl.BlockSpec(weight.shape, whole),
            pl.BlockSpec((tile, cols.three), step),
            pl.BlockSpec((tile, cols.window), step),
            pl.BlockSpec((tile, cols.heads), step),
        ]
        + [anywhere] * len(extra),
        out_specs=[
            pl.BlockSpec((tile, cols.three), step),
            pl.BlockSpec(weight.shape, whole),
            pl.BlockSpec((2, lanes), whole),
        ],
        out_shape=[
            pltpu.HBM((total, cols.three), BF16),
            jax.ShapeDtypeStruct(weight.shape, BF16),
            jax.ShapeDtypeStruct((2, lanes), F32),
        ],
        scratch_shapes=[
            pltpu.VMEM(weight.shape, F32),
            pltpu.VMEM((tile, width), BF16),
            pltpu.VMEM((tile, width), BF16),
            pltpu.SemaphoreType.DMA((1 + len(extra),)),
        ]
        + [pltpu.VMEM(weight.shape, BF16)] * len(extra),
        compiler_params=pltpu.CompilerParams(vmem_limit_bytes=BACK_VMEM),
        cost_estimate=pl.CostEstimate(
            flops=2 * total * width * (cols.packed + cols.window) + 10 * total * SEQ * lanes,
            bytes_accessed=2 * (2 * total * width + 7 * total * cols.hh + 2 * weight.size),
            transcendentals=total * SEQ * cols.heads,
        ),
        name="attend_back",
    )(own, far(other), far(rows), weight, far(qkv), far(mixed), far(lse), *map(far, extra))


def sum_nt_kernel(count, inner, *refs):
    lefts, rights = refs[:count], refs[count : 2 * count]
    mine_ref, other_ref = refs[2 * count :]
    total = dot_nt(lefts[0][...], rights[0][:, :inner])
    for left, right in zip(lefts[1:], rights[1:]):
        total += dot_nt(left[...], right[:, :inner])
    value = total.astype(BF16)
    half = pl.num_programs(0) // 2

    @pl.when(pl.program_id(0) < half)
    def _():
        other_ref[...] = value

    @pl.when(pl.program_id(0) >= half)
    def _():
        mine_ref[...] = value


def sum_nt(lefts, rights, tile=SEQ):
    count = len(lefts)
    total, inner = lefts[0].shape
    width = rights[0].shape[0]
    half = total // 2 // tile
    return pl.pallas_call(
        functools.partial(sum_nt_kernel, count, inner),
        grid=(2 * half,),
        in_specs=[pl.BlockSpec((tile, inner), lambda i: (lax.rem(i + half, 2 * half), 0))] * count
        + [pl.BlockSpec(right.shape, lambda i: (0, 0), pipeline_mode=pl.Buffered(1)) for right in rights],
        out_specs=[
            pl.BlockSpec((tile, width), lambda i: (jnp.maximum(i - half, 0), 0)),
            pl.BlockSpec((tile, width), lambda i: (jnp.minimum(i, half - 1), 0)),
        ],
        out_shape=[
            jax.ShapeDtypeStruct((total // 2, width), BF16),
            pltpu.HBM((total // 2, width), BF16),
        ],
        compiler_params=pltpu.CompilerParams(vmem_limit_bytes=SUM_VMEM),
        cost_estimate=pl.CostEstimate(
            flops=2 * total * inner * width * count,
            bytes_accessed=2 * (count * (total + width) * inner + total * width),
            transcendentals=0,
        ),
        name="sum_nt",
    )(*map(far, lefts), *rights)


def spread_kernel(count, in_ref, *out_refs):
    blocks = in_ref.shape[0]
    piece = out_refs[0].shape[1] // blocks
    for v in range(count):
        for i in range(blocks):
            out_refs[v][:, i * piece : (i + 1) * piece] = in_ref[
                i : i + 1, v * piece : (v + 1) * piece
            ]


def spread(vecs, count, width):
    return pl.pallas_call(
        functools.partial(spread_kernel, count),
        in_specs=[pl.BlockSpec(memory_space=pltpu.VMEM)],
        out_specs=[pl.BlockSpec(memory_space=pltpu.VMEM)] * count,
        out_shape=[jax.ShapeDtypeStruct((1, width), F32)] * count,
        name="spread",
    )(vecs)


def fetch_weights(core_ref, own, got, kept, sems):
    def fetch(sources):
        copies = [
            pltpu.make_async_copy(source, target, sems.at[i])
            for i, (source, target) in enumerate(zip(sources, kept))
        ]
        for copy in copies:
            copy.start()
        for copy in copies:
            copy.wait()

    @pl.when(core_ref[0] == 0)
    def _():
        fetch(own)

    @pl.when(core_ref[0] != 0)
    def _():
        fetch(got)


def feed_in_kernel(
    half, core_ref, rows0, rows1, w1_own, w1_got, bias_ref, rows_ref, act_ref, slope_ref, w1, sems
):
    step = pl.program_id(0)

    @pl.when(step == 0)
    def _():
        fetch_weights(core_ref, [w1_own], [w1_got], [w1], sems)

    rows = jnp.where(step < half, rows0[...], rows1[...])
    rows_ref[...] = rows
    pre = dot_nn(rows, w1[...]) + bias_ref[...]
    root = (2.0 / jnp.pi) ** 0.5
    square = pre * pre
    tanh = jnp.tanh(root * (pre + 0.044715 * (pre * square)))
    gate = 0.5 * (1.0 + tanh)
    slope = gate + 0.5 * pre * (1.0 - tanh * tanh) * (root * (1.0 + 3 * 0.044715 * square))
    act_ref[...] = (pre * gate).astype(BF16)
    slope_ref[...] = slope.astype(BF16)


def feed_in(core, rows, weights, bias, tile=SEQ):
    count, width = rows[0].shape
    ff = weights[0].shape[1]
    half = count // tile
    step = lambda i: (i, 0)
    anywhere = pl.BlockSpec(memory_space=pl.ANY)
    return pl.pallas_call(
        functools.partial(feed_in_kernel, half),
        grid=(2 * half,),
        in_specs=[
            pl.BlockSpec(memory_space=pltpu.SMEM),
            pl.BlockSpec((tile, width), lambda i: (jnp.minimum(i, half - 1), 0)),
            pl.BlockSpec((tile, width), lambda i: (jnp.maximum(i - half, 0), 0)),
            anywhere,
            anywhere,
            pl.BlockSpec((1, ff), lambda i: (0, 0)),
        ],
        out_specs=[
            pl.BlockSpec((tile, width), step),
            pl.BlockSpec((tile, ff), step),
            pl.BlockSpec((tile, ff), step),
        ],
        out_shape=[
            jax.ShapeDtypeStruct((2 * count, width), BF16),
            jax.ShapeDtypeStruct((2 * count, ff), BF16),
            jax.ShapeDtypeStruct((2 * count, ff), BF16),
        ],
        scratch_shapes=[pltpu.VMEM((width, ff), BF16), pltpu.SemaphoreType.DMA((1,))],
        compiler_params=pltpu.CompilerParams(vmem_limit_bytes=FEED_VMEM),
        cost_estimate=pl.CostEstimate(
            flops=4 * count * width * ff,
            bytes_accessed=2 * (width * ff + 4 * count * (width + ff)),
            transcendentals=2 * count * ff,
        ),
        name="feed_in",
    )(core, *rows, *[far(w) for w in weights], bias)


def feed_out_kernel(
    half, core_ref, cot0, cot1, act_ref, slope_ref, w1_own, w1_got, w2_own, w2_got,
    gpre_ref, out0, out1, grad0, grad1, sums_ref, w1, w2, sems,
):
    step = pl.program_id(0)

    @pl.when(step == 0)
    def _():
        fetch_weights(core_ref, [w1_own, w2_own], [w1_got, w2_got], [w1, w2], sems)

    first = step < half
    cot = jnp.where(first, cot0[...], cot1[...])
    grad_pre = dot_nn(cot, w2[...]) * slope_ref[...].astype(F32)
    sums = jnp.sum(grad_pre, axis=0, keepdims=True)
    grad_in = grad_pre.astype(BF16)
    gpre_ref[...] = grad_in
    grad = dot_nt(grad_in, w1[...]).astype(BF16)
    out = dot_nt(act_ref[...], w2[...]).astype(BF16)

    @pl.when(step == 0)
    def _():
        sums_ref[...] = sums

    @pl.when(step > 0)
    def _():
        sums_ref[...] += sums

    @pl.when(first)
    def _():
        out0[...] = out
        grad0[...] = grad

    @pl.when(jnp.logical_not(first))
    def _():
        out1[...] = out
        grad1[...] = grad


def feed_out(core, cots, act, slope, weights, tile=SEQ):
    count, width = cots[0].shape
    ff = act.shape[1]
    half = count // tile
    low = lambda i: (jnp.minimum(i, half - 1), 0)
    high = lambda i: (jnp.maximum(i - half, 0), 0)
    step = lambda i: (i, 0)
    anywhere = pl.BlockSpec(memory_space=pl.ANY)
    return pl.pallas_call(
        functools.partial(feed_out_kernel, half),
        grid=(2 * half,),
        in_specs=[
            pl.BlockSpec(memory_space=pltpu.SMEM),
            pl.BlockSpec((tile, width), low),
            pl.BlockSpec((tile, width), high),
            pl.BlockSpec((tile, ff), step),
            pl.BlockSpec((tile, ff), step),
        ]
        + [anywhere] * 4,
        out_specs=[
            pl.BlockSpec((tile, ff), step),
            pl.BlockSpec((tile, width), low),
            pl.BlockSpec((tile, width), high),
            pl.BlockSpec((tile, width), low),
            pl.BlockSpec((tile, width), high),
            pl.BlockSpec((1, ff), lambda i: (0, 0)),
        ],
        out_shape=[jax.ShapeDtypeStruct((2 * count, ff), BF16)]
        + [jax.ShapeDtypeStruct((count, width), BF16)] * 4
        + [jax.ShapeDtypeStruct((1, ff), F32)],
        scratch_shapes=[
            pltpu.VMEM((width, ff), BF16),
            pltpu.VMEM((width, ff), BF16),
            pltpu.SemaphoreType.DMA((2,)),
        ],
        compiler_params=pltpu.CompilerParams(vmem_limit_bytes=FEED_OUT_VMEM),
        cost_estimate=pl.CostEstimate(
            flops=12 * count * width * ff,
            bytes_accessed=2 * (2 * width * ff + 2 * count * (3 * width + 3 * ff)),
            transcendentals=0,
        ),
        name="feed_out",
    )(core, *cots, act, slope, *[far(w) for w in weights])


def norm_back_kernel(count, *refs):
    grads, (rows_ref, cot_ref, gain_ref) = refs[:count], refs[count : count + 3]
    out_ref, rounded_ref, sums_ref = refs[count + 3 :]
    grad = grads[0][...].astype(F32)
    for other in grads[1:]:
        grad += other[...].astype(F32)
    rows = rows_ref[...]
    center = rows - jnp.mean(rows, axis=-1, keepdims=True)
    spread = lax.rsqrt(jnp.mean(center * center, axis=-1, keepdims=True) + EPS)
    normed = center * spread
    cot = cot_ref[...].astype(F32)
    out = cot + norm_back(grad, normed, spread, gain_ref[...])
    out_ref[...] = out
    rounded_ref[...] = out.astype(BF16)

    @pl.when(pl.program_id(0) == 0)
    def _():
        sums_ref[...] = jnp.zeros_like(sums_ref)

    for i, value in enumerate((grad * normed, grad, out, cot)):
        sums_ref[i : i + 1, :] += jnp.sum(value, axis=0, keepdims=True)


def norm_back_rows(grads, rows, cot, gain, tile=128):
    count, width = rows.shape
    step = pl.BlockSpec((tile, width), lambda i: (i, 0))
    return pl.pallas_call(
        functools.partial(norm_back_kernel, len(grads)),
        grid=(count // tile,),
        in_specs=[step] * (len(grads) + 2) + [pl.BlockSpec((1, width), lambda i: (0, 0))],
        out_specs=[step, step, pl.BlockSpec((8, width), lambda i: (0, 0))],
        out_shape=[
            jax.ShapeDtypeStruct((count, width), F32),
            jax.ShapeDtypeStruct((count, width), BF16),
            jax.ShapeDtypeStruct((8, width), F32),
        ],
        compiler_params=pltpu.CompilerParams(vmem_limit_bytes=16 << 20),
        cost_estimate=pl.CostEstimate(
            flops=30 * count * width,
            bytes_accessed=count * width * (2 * len(grads) + 12),
            transcendentals=count,
        ),
        name="norm_back",
    )(*grads, rows, cot, gain)


def pack_kernel(where_ref, gain_ref, shift_ref, second_ref, *refs):
    units, bias_ref, out_ref = refs[:-2], refs[-2], refs[-1]
    out_ref[...] = jnp.zeros_like(out_ref)
    width = gain_ref.shape[1]
    out_ref[0, 0:1, :width] = gain_ref[...]
    out_ref[0, 2:3, :width] = shift_ref[...]
    for spot, row in ((1, 0), (3, 2), (4, 1), (5, 3)):
        out_ref[0, spot : spot + 1, :width] = second_ref[row : row + 1, :]
    core = where_ref[0]
    for n, unit in enumerate(units):
        hp = unit.shape[1]
        spot = 1 + where_ref[2 + n]

        @pl.when(core == 0)
        def _():
            out_ref[spot, 1:3, :hp] = unit[...]

        @pl.when(core != 0)
        def _():
            out_ref[spot, 3:5, :hp] = unit[...]

    out_ref[1 + where_ref[1], 0:1, : bias_ref.shape[1]] = bias_ref[...]


def pack_small(where, vectors, units, bias, spots):
    lanes = max(x.shape[1] for x in [*vectors, *units, bias])
    return pl.pallas_call(
        pack_kernel,
        in_specs=[pl.BlockSpec(memory_space=pltpu.SMEM)]
        + [pl.BlockSpec(memory_space=pltpu.VMEM)] * (len(vectors) + len(units) + 1),
        out_specs=pl.BlockSpec(memory_space=pltpu.VMEM),
        out_shape=jax.ShapeDtypeStruct((1 + spots, 8, lanes), F32),
        name="pack_small",
    )(where, *vectors, *units, bias)


def make_body(ndp, nt):
    nz = ndp // 2
    bits = nt.bit_length() - 1
    top = nt // 2
    low = nt // 2

    def perm(move):
        pairs = []
        for d in range(ndp):
            for t in range(nt):
                d2, t2 = move(d, t)
                pairs.append((d * nt + t, d2 * nt + t2))
        return pairs

    def send(value, move):
        return lax.ppermute(value, AXES, perm(move))

    def swap_core(value):
        return send(value, lambda d, t: (d ^ 1, t))

    def swap_tensor(value, i):
        return send(value, lambda d, t: (d, t ^ i))

    def shift_z(value, k):
        return send(value, lambda d, t: ((d + 2 * k) % ndp, t))

    def stage(value, i):
        return send(
            value, lambda d, t: (d, t ^ ((1 << i) if d % 2 == 0 else (1 << (bits - 1 - i))))
        )

    def reverse_bits(p):
        return sum(((p >> i) & 1) << (bits - 1 - i) for i in range(bits))

    def swap_top(value):
        pairs = [(d * nt + t, d * nt + (t ^ top)) for d in range(1, ndp, 2) for t in range(nt)]
        return lax.ppermute(value, AXES, pairs)

    def gather_z(value, z):
        out = jnp.zeros((nz,) + value.shape, value.dtype)
        out = lax.dynamic_update_slice_in_dim(out, value[None], z, 0)
        for k in range(1, nz):
            got = shift_z(value, k)
            out = lax.dynamic_update_slice_in_dim(out, got[None], lax.rem(z - k + nz, nz), 0)
        return out

    def pick(selector, items):
        total = jnp.where(selector == 0, items[0], 0)
        for i in range(1, len(items)):
            total = total + jnp.where(selector == i, items[i], 0)
        return total

    def body(
        tokens, norm_gains, row_biases, w_qkv, head_bias, w_out, w_fc1, fc1_bias, w_fc2, cotangent
    ):
        d = lax.axis_index("dp")
        t = lax.axis_index("tensor")
        z, c = d // 2, d % 2
        core0 = c == 0
        _, width = tokens.shape
        block = w_qkv.shape[2]
        hh = block // 2
        part = w_qkv.shape[1]
        ff = w_fc1.shape[1]

        def by_core(zero, one):
            return jnp.where(core0, zero, one)

        w_out_t = w_out.T

        cols = Columns(hh)
        packed, heads = cols.packed, cols.heads
        wide = padded(ff)

        def half(h):
            sl = slice(h * hh, (h + 1) * hh)
            cols = [w_qkv[0][:, sl], w_qkv[1][:, sl], w_qkv[2][:, sl], w_out_t[:, sl]]
            return jnp.pad(jnp.concatenate(cols, axis=1), ((0, 0), (0, packed - 4 * hh)))

        gathered = lax.all_gather(jnp.stack([half(0), half(1)]), "dp", axis=1, tiled=True)
        others = range(1, low)
        cot_far = [swap_tensor(cotangent, i) for i in others]

        gain_count, shift_count = norm_gains.shape[0], row_biases.shape[0]
        vec_count = gain_count + shift_count
        piece = norm_gains.shape[1]
        small = jnp.concatenate(
            [norm_gains.reshape(-1), row_biases.reshape(-1), head_bias.reshape(-1), fc1_bias]
        )
        smalls = [small] + [swap_tensor(small, i) for i in range(1, nt)]
        vec_size = vec_count * piece
        vecs = jnp.stack([pick(t ^ i, [s[:vec_size] for s in smalls]) for i in range(nt)])
        vecs = gather_z(vecs, z)
        vecs_other = swap_core(vecs)
        vecs = jnp.stack([by_core(vecs, vecs_other), by_core(vecs_other, vecs)], axis=1)
        vecs = spread(vecs.reshape(nz * 2 * nt, vec_size), vec_count, width)
        gain_rows, shifts = vecs[:gain_count], vecs[gain_count:]
        head_biases = jnp.stack([s[vec_size : vec_size + 2 * block] for s in smalls])
        turned = jnp.stack(
            [smalls[reverse_bits(p)][vec_size : vec_size + 2 * block] for p in range(nt)]
        )
        unit_bias = by_core(head_biases, turned).reshape(nt, 2, 2, hh)
        unit_bias = by_core(unit_bias[:, :, 0], unit_bias[:, :, 1])
        unit_bias = jnp.concatenate(
            [
                unit_bias[:, 0],
                jnp.zeros((nt, hh), F32),
                unit_bias[:, 1],
                jnp.zeros((nt, cols.three - 3 * hh), F32),
            ],
            axis=1,
        ).reshape(nt, 1, cols.three)
        scale = jnp.where(jnp.arange(cols.three) < hh, HD ** (-0.5), 1.0).astype(F32)
        scale = scale.reshape(1, cols.three)
        ff_bias = by_core(smalls[0][vec_size + 2 * block :], smalls[top][vec_size + 2 * block :])
        ff_bias = jnp.pad(ff_bias, (0, wide - ff)).reshape(1, wide)

        inputs_f = tokens.astype(F32)
        first_f, normed_one, spread_one = norm_rows(inputs_f, gain_rows[0], shifts[0])
        first = first_f.astype(BF16)
        first_chip = jnp.concatenate([first, swap_core(first)], axis=0)

        cots = [(g, swap_core(g)) for g in [cotangent, *cot_far]]
        cot_rows = [jnp.concatenate(pair, axis=0) for pair in cots]
        early = (first_chip, unit_bias, ff_bias)
        attn_w = [lax.dynamic_index_in_dim(tie(gathered, *early), c, 0, keepdims=False)]
        for i in range(bits):
            sent = list(attn_w)
            if i:
                sent[-1] = tie(sent[-1], *cot_rows)
            attn_w = attn_w + [stage(b, i) for b in sent]

        def gather_ff(own):
            return lax.all_gather(
                jnp.pad(own, ((0, 0), (0, wide - ff))), "dp", axis=0, tiled=True
            )

        fc1_own, fc2_own = gather_ff(w_fc1), gather_ff(tie(w_fc2.T, *vecs))

        saved = []
        for p in range(nt):
            before = None
            if p == nt - 1:
                before = ([s[1] for s in saved], attn_w[:p])
            saved.append(attend(cols, first_chip, attn_w[p], scale, unit_bias[p], before))
        attn_mine, attn_other = saved[-1][3:]
        fc1_got = swap_top(tie(fc1_own, attn_w[nt - 1], attn_w[nt - 2]))
        fc2_got = swap_top(fc2_own)
        attention = attn_mine.astype(F32) + swap_core(attn_other).astype(F32)
        hidden_one = inputs_f + attention + shifts[1]
        second_f = norm_rows(hidden_one, gain_rows[1], shifts[2])[0]

        core = c.astype(jnp.int32).reshape(1)
        second = second_f.astype(BF16)
        second_far = [swap_tensor(second, i) for i in others]
        fc1_pair, fc2_pair = (fc1_own, fc1_got), (fc2_own, fc2_got)
        ins = [None] * low
        ins[0] = feed_in(core, (second, swap_core(second)), fc1_pair, ff_bias)
        grad_fc2_t = dot_tn(cot_rows[0], ins[0][1])
        for i, rows_far in zip(others, second_far):
            rows_far = tie(rows_far, grad_fc2_t)
            ins[i] = feed_in(core, (rows_far, swap_core(rows_far)), fc1_pair, ff_bias)

        outs, grad_sums, pres, grad_fc1_bias = [None] * low, [None] * low, [None] * low, 0
        after = []
        for i in reversed(range(low)):
            act, slope = ins[i][1:]
            if i == 0 or i == low - 1:
                slope = tie(slope, *after)
            pres[i], out0, out1, grad0, grad1, sums = feed_out(
                core, cots[i], act, slope, fc1_pair + fc2_pair
            )
            grad_fc1_bias = grad_fc1_bias + sums
            got = swap_core(grad1)
            got_out = swap_core(out1).astype(F32)
            if i:
                grad_fc2_t = grad_fc2_t + dot_tn(cot_rows[i], tie(ins[i][1], pres[i]))
                got = tie(got, grad_fc2_t)
            if i:
                got = (grad0.astype(F32) + got.astype(F32)).astype(BF16)
            grad_sums[i] = got
            grad_near = grad0
            if i == 1:
                grad_fc2_t = tie(grad_fc2_t, grad_sums[i]).astype(BF16)
            outs[i] = out0.astype(F32) + got_out
            if i:
                outs[i] = tie(outs[i].astype(BF16), grad_sums[i])
            after = [grad_sums[i], grad_fc2_t, outs[i]]
        got_fc2 = swap_top(grad_fc2_t)
        grad_fc1 = 0
        for i in reversed(range(low)):
            grad_fc1 = grad_fc1 + dot_tn(ins[i][0], tie(pres[i], grad_sums[0]))
        grad_fc1 = grad_fc1.astype(BF16)
        got_fc1 = swap_top(grad_fc1)

        def scatter_ff(partial):
            own = lax.psum_scatter(partial, "dp", scatter_dimension=0, tiled=True)
            return lax.optimization_barrier(own)[:, :ff].astype(F32)

        grad_fc2_t = by_core(grad_fc2_t, tie(got_fc2, grad_fc1))
        grad_fc2_own = scatter_ff(grad_fc2_t).T

        grad_second = [grad_near, grad_sums[0]]
        for i in others:
            got = swap_tensor(grad_sums[i], i)
            grad_second.append(tie(got, grad_fc1, grad_fc2_t))
        mlp_out = outs[0]
        for i in others:
            mlp_out = mlp_out + swap_tensor(outs[i], i).astype(F32)

        grad_hidden, hidden_in, second_sums = norm_back_rows(
            grad_second, hidden_one, cotangent, gain_rows[1]
        )
        hidden_pair = (hidden_in, swap_core(hidden_in))
        back, after = {}, None
        grad_w = [None] * nt
        got_w = {}
        for p in reversed(range(nt)):
            qkv, mix, lse = saved[p][:3]
            if after is not None:
                lse = tie(lse, *after)
            come = sorted((q for q in got_w if got_w[q][0] == p and (p or q > 1)), reverse=True)
            extra = [got_w[q][1] for q in come]
            back[p] = attend_back(cols, hidden_pair, first_chip, attn_w[p], qkv, mix, lse, extra)
            value = back[p][1]
            grad_w[p] = value
            after = [value]
            if p == nt - 2:
                grad_fc1 = by_core(grad_fc1, tie(got_fc1, value))
                grad_fc1_own = scatter_ff(grad_fc1)
                after = [value, grad_fc1]
            if p == 0:
                break
            i = p.bit_length() - 1
            got_w[p] = (p - (1 << i), stage(value, i))
        grad_w = [(grad_w[0].astype(F32) + got_w[1][1].astype(F32)).astype(BF16)]
        own_half = lax.psum_scatter(
            grad_w[0],
            "dp",
            scatter_dimension=0,
            axis_index_groups=[list(range(0, ndp, 2)), list(range(1, ndp, 2))],
            tiled=True,
        )
        own_half = own_half.reshape(2, part, packed)
        kept = by_core(own_half[0], own_half[1]).astype(F32)
        got = swap_core(by_core(own_half[1], own_half[0])).astype(F32)
        halves = [by_core(kept, got), by_core(got, kept)]
        grad_qkv_own = jnp.stack(
            [
                jnp.concatenate([g[:, k * hh : (k + 1) * hh] for g in halves], axis=1)
                for k in range(3)
            ]
        )
        grad_out_own = jnp.concatenate([g[:, 3 * hh : 4 * hh] for g in halves], axis=1).T

        projs = [back[p][0] for p in range(nt)]
        projs[0] = tie(projs[0], grad_w[0])
        first_mine, first_other = sum_nt(projs, attn_w)
        grad_first = first_mine.astype(F32) + swap_core(first_other).astype(F32)
        gain_one = jnp.sum(grad_first * normed_one, axis=0, keepdims=True)
        shift_one = jnp.sum(grad_first, axis=0, keepdims=True)
        grad_tokens = grad_hidden + norm_back(grad_first, normed_one, spread_one, gain_rows[0])

        output = hidden_one + tie(mlp_out, grad_w[0]) + shifts[3]

        spots = [by_core(t ^ p, t ^ reverse_bits(p)) for p in range(nt)]
        where = jnp.stack([c, by_core(t, t ^ top)] + spots).astype(jnp.int32)
        total = pack_small(
            where,
            [gain_one, shift_one, second_sums],
            [back[p][2] for p in range(nt)],
            grad_fc1_bias,
            nt,
        )
        total = functools.reduce(jnp.add, [swap_tensor(total, i) for i in range(1, nt)], total)
        total = tie(total, grad_tokens)
        total = functools.reduce(jnp.add, [shift_z(total, k) for k in range(1, nz)], total)
        total = tie(total, output, grad_fc1_own, grad_fc2_own)
        total = total + swap_core(total)
        own = lax.dynamic_slice_in_dim(
            total[0, :vec_count, :width], (d * nt + t) * piece, piece, axis=1
        )
        mine = lax.dynamic_index_in_dim(total, 1 + t, 0, keepdims=False)
        units = mine[1:5, : heads * LANES].reshape(2, 2, heads, LANES)[:, :, :, :HD]
        head_total = units.transpose(1, 0, 2, 3).reshape(2, block)
        bias_total = mine[0, :ff]
        return (
            output,
            grad_tokens,
            own[:gain_count],
            own[gain_count:],
            grad_qkv_own,
            head_total,
            grad_out_own,
            grad_fc1_own,
            bias_total,
            grad_fc2_own,
        )

    return body


def solution(mesh):
    in_specs = (
        P(("dp", "tensor"), None),
        P(None, ("dp", "tensor")),
        P(None, ("dp", "tensor")),
        P(None, "dp", "tensor"),
        P(None, "tensor"),
        P("tensor", "dp"),
        P("dp", "tensor"),
        P("tensor"),
        P("tensor", "dp"),
        P(("dp", "tensor"), None),
    )
    out_specs = (
        P(("dp", "tensor"), None),
        P(("dp", "tensor"), None),
        P(None, ("dp", "tensor")),
        P(None, ("dp", "tensor")),
        P(None, "dp", "tensor"),
        P(None, "tensor"),
        P("tensor", "dp"),
        P("dp", "tensor"),
        P("tensor"),
        P("tensor", "dp"),
    )
    body = make_body(mesh.shape["dp"], mesh.shape["tensor"])

    return jax.shard_map(body, mesh=mesh, in_specs=in_specs, out_specs=out_specs, check_vma=False)
```

time: 447 us -> 473 us (1.058)
  Pallas kernels: 114 us -> 135 us
  waiting for transfers between devices: 112 us -> 132 us
  local copies, waits for them, and re-layouts: 59.9 us -> 40.6 us
  starting transfers between devices: 67.1 us -> 77.6 us
  other arithmetic: 54.5 us -> 45 us
    ppermute x37, waiting for transfers between devices: 86.8 us -> 120 us  [send(): return lax.ppermute(value, AXES, perm(move))]
    pallas_call x11 -> x12, Pallas kernels: 73.3 us -> 87.1 us  [the longest x4 41 us: attend_back(): pl.pallas_call(functools.partial(attend_back_kernel, cols, images, len(ex...]
    ppermute x37, starting transfers between devices: 60.1 us -> 71.6 us  [send(): return lax.ppermute(value, AXES, perm(move))]
    reduce_scatter x1, waiting for transfers between devices: 10.5 us -> 0.01 us  [body(): lax.psum_scatter(grad_w[0], 'dp', scatter_dimension=0, axis_index_groups=...]
    pallas_call x2, Pallas kernels: 25.9 us -> 31.5 us  [feed_out(): pl.pallas_call(functools.partial(feed_out_kernel, half), grid=(2 * half,)...]
    unnamed x225 -> x110, local copies, waits for them, and re-layouts: 31 us -> 25.7 us
    pallas_call x0 -> x6, other arithmetic: none -> 5.26 us  [spread(): pl.pallas_call(functools.partial(spread_kernel, count), in_specs=[pl.Bloc...]
  transfers between devices with their start and end apart: 47 -> 47, of which waited for: 16 -> 23; matrix products, arithmetic and copies ran while one was open for 21% -> 16% of each run, Pallas kernels for 26% -> 22%
where the time goes in v1:
time: 473 us; the launch traced here: 465 us
  Pallas kernels  135 us (29%)
  waiting for transfers between devices  132 us (28%)
  starting transfers between devices  77.6 us (16%)
  other arithmetic  45 us (10%)
  local copies, waits for them, and re-layouts  40.6 us (9%)
  matrix products  19.7 us (4%)
  between operations  15.5 us (3%)
    ppermute x37, waiting for transfers between devices, send(): return lax.ppermute(value, AXES, perm(move))  120 us
    ppermute x37, starting transfers between devices, send(): return lax.ppermute(value, AXES, perm(move))  71.6 us
    pallas_call x4, Pallas kernels, attend_back(): pl.pallas_call(functools.partial(attend_back_kernel, cols, images, len(ex...  41 us
    pallas_call x2, Pallas kernels, feed_out(): pl.pallas_call(functools.partial(feed_out_kernel, half), grid=(2 * half,)...  31.5 us
    pallas_call x4, Pallas kernels, attend(): pl.pallas_call(functools.partial(attend_kernel, cols, images, len(mixeds)...  28.7 us
    unnamed x110, local copies, waits for them, and re-layouts  25.7 us
    dot_general x4, matrix products, dot_tn(): lax.dot_general(a, b, (((0,), (0,)), ((), ())), preferred_element_type=F32)  19.7 us
    pallas_call x2, Pallas kernels, feed_in(): pl.pallas_call(functools.partial(feed_in_kernel, half), grid=(2 * half,),...  16.3 us
  transfers between devices with their start and end apart: 47, of which 23 were waited for; matrix products, arithmetic and copies ran while one was open for 16% of the time, Pallas kernels for 22%

profile of v1, /device:TPU:0, one launch (start us, length us, event | category | flops | bytes accessed | tf_op | source)
XLA Modules:
  0.0 465.4 jit_solution(14045177408575540040)
XLA Ops:
  11.2 3.0 collective-permute-start.1
  17.9 2.4 collective-permute-done.2
  22.1 2.6 collective-permute-start.4
  38.6 12.0 %all-gather.4.cloned.1.call-done = bf16[2,1152,640]{2,1,0:T(8,128)(2,1)} async-done(((bf16[2,144,640]{2,1,0:T(8,128)(2,1)}), bf16[2,1152,640]{2,1,0:T(8,128)(2,1)}) %all-gather.4.cloned.1.call-update) | async-done | bytes 2949136 | tf_op jit(solution)/shard_map/all_gather | solution.py:708
  53.5 9.2 %collective-permute-done.10.cot0 = bf16[512,1152]{1,0:T(8,128)(2,1)} collective-permute-done((bf16[512,1152]{1,0:T(8,128)(2,1)}, bf16[512,1152]{1,0:T(8,128)(2,1)}, u32[]{:S(2)}, u32[]{:S(2)}) %collective-permute-start.10) | collective-permute-done | bytes 1179680 | tf_op jit(solution)/shard_map/ppermute | solution.py:644
  63.0 2.4 constant_dynamic-update-slice_fusion.1
  71.9 12.4 %collective-permute-done.8.w_ref.refs_5_.refs_6_ = bf16[1152,640]{1,0:T(8,128)(2,1)S(1)} collective-permute-done((bf16[1152,640]{1,0:T(8,128)(2,1)S(1)}, bf16[1152,640]{1,0:T(8,128)(2,1)S(1)}, u32[]{:S(2)}, u32[]{:S(2)}) %collective-permute-start.8) | collective-permute-done | bytes 1474592 | tf_op jit(solution)/shard_map/ppermute | solution.py:644
  86.6 5.7 %attend.4 = (bf16[1024,512]{1,0:T(8,128)(2,1)}, bf16[1024,256]{1,0:T(8,128)(2,1)}, f32[1024,2]{1,0:T(8,128)}) custom-call(bf16[1024,1152]{1,0:T(8,128)(2,1)} %pad_maximum_fusion.rows_ref, bf16[1152,640]{1,0:T(8,128)(2,1)S(1)} %dynamic-slice_bitcast_fusion.w_ref.refs_3_.refs_4_, f32[1,512]{1,0:T(1,128)S(1)} %get-tuple-element.205.scale_ref, ...), custom_call_target="tpu_custom_call" | custom-call | flops 1778384896 | bytes 5013504 | tf_op jit(solution)/shard_map/attend/pallas_call | solution.py:161
  92.2 5.7 %attend.5 = (bf16[1024,512]{1,0:T(8,128)(2,1)}, bf16[1024,256]{1,0:T(8,128)(2,1)}, f32[1024,2]{1,0:T(8,128)}) custom-call(bf16[1024,1152]{1,0:T(8,128)(2,1)} %pad_maximum_fusion.rows_ref, bf16[1152,640]{1,0:T(8,128)(2,1)S(1)} %collective-permute-done.8.w_ref.refs_5_.refs_6_, f32[1,512]{1,0:T(1,128)S(1)} %get-tuple-element.205.scale_ref, ...), custom_call_target="tpu_custom_call" | custom-call | flops 1778384896 | bytes 5013504 | tf_op jit(solution)/shard_map/attend/pallas_call | solution.py:161
  98.0 6.2 %attend.6 = (bf16[1024,512]{1,0:T(8,128)(2,1)}, bf16[1024,256]{1,0:T(8,128)(2,1)}, f32[1024,2]{1,0:T(8,128)}) custom-call(bf16[1024,1152]{1,0:T(8,128)(2,1)} %pad_maximum_fusion.rows_ref, bf16[1152,640]{1,0:T(8,128)(2,1)} %collective-permute-done.13.w_ref.refs_7_.refs_8_.refs_6_, f32[1,512]{1,0:T(1,128)S(1)} %get-tuple-element.205.scale_ref, ...), custom_call_target="tpu_custom_call" | custom-call | flops 1778384896 | bytes 5013504 | tf_op jit(solution)/shard_map/attend/pallas_call | solution.py:161
  104.7 11.1 %attend.7 = (bf16[1024,512]{1,0:T(8,128)(2,1)}, bf16[1024,256]{1,0:T(8,128)(2,1)}, f32[1024,2]{1,0:T(8,128)}, bf16[512,1152]{1,0:T(8,128)(2,1)S(1)}, bf16[512,1152]{1,0:T(8,128)(2,1)}) custom-call(bf16[1024,1152]{1,0:T(8,128)(2,1)} %pad_maximum_fusion.rows_ref, bf16[1152,640]{1,0:T(8,128)(2,1)} %collective-permute-done.12.w_ref.refs_7_, ...), custom_call_target="tpu_custom_call" | custom-call | flops 1778384896 | bytes 5013504 | tf_op jit(solution)/shard_map/attend/pallas_call | solution.py:161
  116.8 5.5 %collective-permute-start.14 = (bf16[512,1152]{1,0:T(8,128)(2,1)}, bf16[512,1152]{1,0:T(8,128)(2,1)S(1)}, u32[]{:S(2)}, u32[]{:S(2)}) collective-permute-start(bf16[512,1152]{1,0:T(8,128)(2,1)} %get-tuple-element.95), channel_id=1, source_target_pairs={{0,4},{1,5},{2,6},{3,7},{4,0},{5,1},{6,2},{7,3},{8,12},{9,13},{10,... | collective-permute-start | bytes 3538952 | tf_op jit(solution)/shard_map/ppermute | solution.py:644
  125.5 2.2 collective-permute-start.16
  127.8 2.2 fusion.39
  134.3 8.8 %feed_in.2 = (bf16[1024,1152]{1,0:T(8,128)(2,1)S(1)}, bf16[1024,1152]{1,0:T(8,128)(2,1)S(1)}, bf16[1024,1152]{1,0:T(8,128)(2,1)S(1)}) custom-call(s32[1]{0:T(128)} %bitcast.21.core_ref, bf16[512,1152]{1,0:T(8,128)(2,1)S(1)} %add_convert_fusion.3.rows0, bf16[512,1152]{1,0:T(8,128)(2,1)} %collective-permute-done.15.rows1, ...), custom_call_target="tpu_custom_call" | custom-call | flops 2717908992 | bytes 12091392 | tf_op jit(solution)/shard_map/feed_in/pallas_call | solution.py:432
  143.1 5.7 %fusion.48 = f32[1152,1152]{1,0:T(8,128)} fusion(bf16[1024,1152]{1,0:T(8,128)(2,1)S(1)} %copy-done.32, bf16[1024,1152]{1,0:T(8,128)(2,1)S(1)} %get-tuple-element.100.act_ref), kind=kOutput, calls=%fused_computation.121 | convolution fusion | flops 2717908992 | bytes 10027008 | tf_op jit(solution)/shard_map/dot_general | solution.py:48
  148.8 12.0 %collective-permute-done.17.rows0 = bf16[512,1152]{1,0:T(8,128)(2,1)S(1)} collective-permute-done((bf16[512,1152]{1,0:T(8,128)(2,1)S(1)}, bf16[512,1152]{1,0:T(8,128)(2,1)S(1)}, u32[]{:S(2)}, u32[]{:S(2)}) %collective-permute-start.17) | collective-permute-done | bytes 1179680 | tf_op jit(solution)/shard_map/ppermute | solution.py:644
  160.8 12.4 %collective-permute-start.18 = (bf16[512,1152]{1,0:T(8,128)(2,1)S(1)}, bf16[512,1152]{1,0:T(8,128)(2,1)S(1)}, u32[]{:S(2)}, u32[]{:S(2)}) collective-permute-start(bf16[512,1152]{1,0:T(8,128)(2,1)S(1)} %collective-permute-done.17.rows0), channel_id=1, source_target_pairs={{0,4},{1,5},{2,6},{3,7},{4,0},{5,1},{6,2},{7,3},{8,12},{9,13},{10,... | collective-permute-start | bytes 3538952 | tf_op jit(solution)/shard_map/ppermute | solution.py:644
  173.2 2.5 collective-permute-done.18.rows1
  175.7 7.5 %feed_in.3 = (bf16[1024,1152]{1,0:T(8,128)(2,1)S(1)}, bf16[1024,1152]{1,0:T(8,128)(2,1)S(1)}, bf16[1024,1152]{1,0:T(8,128)(2,1)S(1)}) custom-call(s32[1]{0:T(128)} %bitcast.21.core_ref, bf16[512,1152]{1,0:T(8,128)(2,1)S(1)} %collective-permute-done.17.rows0, bf16[512,1152]{1,0:T(8,128)(2,1)S(1)} %collective-permute-done.18.rows1, ...), custom_call_target="tpu_custom_call" | custom-call | flops 2717908992 | bytes 12091392 | tf_op jit(solution)/shard_map/feed_in/pallas_call | solution.py:432
  184.7 16.1 %feed_out.2 = (bf16[1024,1152]{1,0:T(8,128)(2,1)S(1)}, bf16[512,1152]{1,0:T(8,128)(2,1)S(1)}, bf16[512,1152]{1,0:T(8,128)(2,1)S(1)}, bf16[512,1152]{1,0:T(8,128)...) custom-call(s32[1]{0:T(128)} %bitcast.21.core_ref, bf16[512,1152]{1,0:T(8,128)(2,1)} %collective-permute-done.10.cot0, ...), custom_call_target="tpu_custom_call" | custom-call | flops 8153726976 | bytes 19464192 | tf_op jit(solution)/shard_map/feed_out/pallas_call | solution.py:510
  200.8 3.7 collective-permute-start.20
  204.6 5.8 %convolution_add_fusion.1 = bf16[1152,1152]{1,0:T(8,128)(2,1)S(1)} fusion(f32[1152,1152]{1,0:T(8,128)} %fusion.48, bf16[1024,1152]{1,0:T(8,128)(2,1)S(1)} %copy-done.34, bf16[1024,1152]{1,0:T(8,128)(2,1)S(1)} %get-tuple-element.110.act_ref), kind=kOutput, calls=%fused_computation.1 | convolution fusion | flops 2720563200 | bytes 12681216 | tf_op jit(solution)/shard_map/dot_general | solution.py:48
  213.1 15.5 %feed_out.3 = (bf16[1024,1152]{1,0:T(8,128)(2,1)S(1)}, bf16[512,1152]{1,0:T(8,128)(2,1)S(1)}, bf16[512,1152]{1,0:T(8,128)(2,1)S(1)}, bf16[512,1152]{1,0:T(8,128)...) custom-call(s32[1]{0:T(128)} %bitcast.21.core_ref, bf16[512,1152]{1,0:T(8,128)(2,1)} %refs_4_.1, ...), custom_call_target="tpu_custom_call" | custom-call | flops 8153726976 | bytes 19464192 | tf_op jit(solution)/shard_map/feed_out/pallas_call | solution.py:510
  234.1 3.3 fusion.49
  237.4 5.0 %fusion = bf16[1152,1152]{1,0:T(8,128)(2,1)} fusion(f32[1152,1152]{1,0:T(8,128)S(1)} %fusion.49, bf16[1024,1152]{1,0:T(8,128)(2,1)S(1)} %get-tuple-element.121, bf16[1024,1152]{1,0:T(8,128)(2,1)S(1)} %get-tuple-element.122), kind=kOutput, calls=%fused_computation.2 | convolution fusion | flops 2720563200 | bytes 12681216 | tf_op jit(solution)/shard_map/dot_general | solution.py:48
  246.3 14.3 %collective-permute-done.25.refs_2_ = bf16[512,1152]{1,0:T(8,128)(2,1)S(1)} collective-permute-done((bf16[512,1152]{1,0:T(8,128)(2,1)}, bf16[512,1152]{1,0:T(8,128)(2,1)S(1)}, u32[]{:S(2)}, u32[]{:S(2)}) %collective-permute-start.25) | collective-permute-done | bytes 1179680 | tf_op jit(solution)/shard_map/ppermute | solution.py:644
  261.9 4.2 norm_back.1
  268.3 20.1 %collective-permute-start.27 = (bf16[512,1152]{1,0:T(8,128)(2,1)S(1)}, bf16[512,1152]{1,0:T(8,128)(2,1)S(1)}, u32[]{:S(2)}, u32[]{:S(2)}) collective-permute-start(bf16[512,1152]{1,0:T(8,128)(2,1)S(1)} %get-tuple-element.128.own_ref), channel_id=1, source_target_pairs={{0,4},{1,5},{2,6},{3,7},{4,0},{5,1},{6,2},{7,3},{8,12},{9,13},{10,... | collective-permute-start | bytes 3538952 | tf_op jit(solution)/shard_map/ppermute | solution.py:644
  288.4 2.5 collective-permute-done.27.other_hbm
  292.0 10.3 %attend_back.4 = (bf16[1024,512]{1,0:T(8,128)(2,1)}, bf16[1152,640]{1,0:T(8,128)(2,1)S(1)}, f32[2,256]{1,0:T(2,128)S(1)}) custom-call(bf16[512,1152]{1,0:T(8,128)(2,1)S(1)} %get-tuple-element.128.own_ref, bf16[512,1152]{1,0:T(8,128)(2,1)} %copy-done.52, bf16[1024,1152]{1,0:T(8,128)(2,1)} %pad_maximum_fusion.rows_ref, ...), custom_call_target="tpu_custom_call" | custom-call | flops 2785017856 | bytes 9732096 | tf_op jit(solution)/shard_map/attend_back/pallas_call | solution.py:279
  303.4 10.4 %attend_back.5 = (bf16[1024,512]{1,0:T(8,128)(2,1)}, bf16[1152,640]{1,0:T(8,128)(2,1)S(1)}, f32[2,256]{1,0:T(2,128)S(1)}) custom-call(bf16[512,1152]{1,0:T(8,128)(2,1)S(1)} %get-tuple-element.128.own_ref, bf16[512,1152]{1,0:T(8,128)(2,1)} %copy-done.52, bf16[1024,1152]{1,0:T(8,128)(2,1)} %pad_maximum_fusion.rows_ref, ...), custom_call_target="tpu_custom_call" | custom-call | flops 2785017856 | bytes 9732096 | tf_op jit(solution)/shard_map/attend_back/pallas_call | solution.py:279
  319.2 17.5 %collective-permute-done.29.refs_0_ = bf16[1152,640]{1,0:T(8,128)(2,1)S(1)} collective-permute-done((bf16[1152,640]{1,0:T(8,128)(2,1)}, bf16[1152,640]{1,0:T(8,128)(2,1)S(1)}, u32[]{:S(2)}, u32[]{:S(2)}) %collective-permute-start.29) | collective-permute-done | bytes 1474592 | tf_op jit(solution)/shard_map/ppermute | solution.py:644
  340.6 10.4 %attend_back.6 = (bf16[1024,512]{1,0:T(8,128)(2,1)}, bf16[1152,640]{1,0:T(8,128)(2,1)}, f32[2,256]{1,0:T(2,128)S(1)}) custom-call(bf16[512,1152]{1,0:T(8,128)(2,1)S(1)} %copy-done.25, bf16[512,1152]{1,0:T(8,128)(2,1)} %copy-done.52, bf16[1024,1152]{1,0:T(8,128)(2,1)} %pad_maximum_fusion.rows_ref, bf16[1152,640]{1,0:T(8,128)(2,1)S(1)} %copy-done.4, ...), custom_call_target="tpu_custom_call" | custom-call | flops 2785017856 | bytes 9732096 | tf_op jit(solution)/shard_map/attend_back/pallas_call | solution.py:279
  357.7 9.9 %attend_back.7 = (bf16[1024,512]{1,0:T(8,128)(2,1)}, bf16[1152,640]{1,0:T(8,128)(2,1)S(1)}, f32[2,256]{1,0:T(2,128)S(1)}) custom-call(bf16[512,1152]{1,0:T(8,128)(2,1)S(1)} %copy-done.26, bf16[512,1152]{1,0:T(8,128)(2,1)} %copy-done.52, bf16[1024,1152]{1,0:T(8,128)(2,1)} %pad_maximum_fusion.rows_ref, bf16[1152,640]{1,0:T(8,128)(2,1)S(1)} %copy-done.1, ...), custom_call_target="tpu_custom_call" | custom-call | flops 2785017856 | bytes 9732096 | tf_op jit(solution)/shard_map/attend_back/pallas_call | solution.py:279
  367.6 15.9 %collective-permute-done.31 = bf16[1152,640]{1,0:T(8,128)(2,1)} collective-permute-done((bf16[1152,640]{1,0:T(8,128)(2,1)}, bf16[1152,640]{1,0:T(8,128)(2,1)}, u32[]{:S(2)}, u32[]{:S(2)}) %collective-permute-start.31) | collective-permute-done | bytes 1474592 | tf_op jit(solution)/shard_map/ppermute | solution.py:644
  383.4 2.9 add_convert_fusion
  389.0 10.0 %sum_nt.1 = (bf16[512,1152]{1,0:T(8,128)(2,1)S(1)}, bf16[512,1152]{1,0:T(8,128)(2,1)}) custom-call(bf16[1024,512]{1,0:T(8,128)(2,1)} %get-tuple-element.149.refs_0_, bf16[1024,512]{1,0:T(8,128)(2,1)} %get-tuple-element.150.refs_1_, bf16[1024,512]{1,0:T(8,128)(2,1)} %get-tuple-element.151.refs_2_, bf16[1024,512]{1,0:T(8,128)(2,1)} %get-tuple-element.152.refs_3_, ...), custom_call_target="tpu_custom_call" | custom-call | flops 4831838208 | bytes 11272192 | tf_op jit(solution)/shard_map/sum_nt/pallas_call | solution.py:342
  399.1 3.4 convert_add_fusion.2
  402.6 3.3 add_add_fusion
  406.0 3.6 fusion.13
  413.9 1.9 collective-permute-start.35
  417.2 4.1 fusion.12
  421.3 3.2 collective-permute-done.34
  424.7 3.2 collective-permute-start.37
  429.3 8.6 %collective-permute-done.36 = f32[5,8,1152]{2,1,0:T(8,128)S(1)} collective-permute-done((f32[5,8,1152]{2,1,0:T(8,128)S(1)}, f32[5,8,1152]{2,1,0:T(8,128)S(1)}, u32[]{:S(2)}, u32[]{:S(2)}) %collective-permute-start.36) | collective-permute-done | bytes 184352 | tf_op jit(solution)/shard_map/ppermute | solution.py:644
  437.8 8.8 %collective-permute-done.37 = f32[5,8,1152]{2,1,0:T(8,128)S(1)} collective-permute-done((f32[5,8,1152]{2,1,0:T(8,128)S(1)}, f32[5,8,1152]{2,1,0:T(8,128)S(1)}, u32[]{:S(2)}, u32[]{:S(2)}) %collective-permute-start.37) | collective-permute-done | bytes 184352 | tf_op jit(solution)/shard_map/ppermute | solution.py:644
  446.7 1.9 slice_convert_fusion
  (289 shorter events, 98.7 us)
Async XLA Ops:
  7.2 43.3 %all-gather.4.cloned.1.call-start = ((), (), s32[]{:S(2)}) async-start(), calls=%async_computation.3 | async-start | bytes 3317760 | tf_op jit(solution)/shard_map/all_gather | solution.py:708
  10.8 114.7 %all-gather.6.cloned.1.call-start = ((), (), s32[]{:S(2)}) async-start(), calls=%async_computation.4 | async-start | bytes 2985984 | tf_op jit(solution)/shard_map/all_gather | solution.py:762
  11.2 6.2 %collective-permute-start.1 = (f32[1868]{0:T(1024)S(1)}, f32[1868]{0:T(1024)S(1)}, u32[]{:S(2)}, u32[]{:S(2)}) collective-permute-start(f32[1868]{0:T(1024)S(1)} %concatenate.39), channel_id=1, source_target_pairs={{0,2},{1,3},{2,0},{3,1},{4,6},{5,7},{6,4},{7,5},{8,10},{9,11},{10,... | collective-permute-start | bytes 22424 | tf_op jit(solution)/shard_map/ppermute | solution.py:644
  14.2 3.7 collective-permute-start
  15.7 4.5 collective-permute-start.2
  16.6 115.1 %all-gather.8.cloned.1.call-start = ((), (), s32[]{:S(2)}) async-start(), calls=%async_computation.5 | async-start | bytes 2985984 | tf_op jit(solution)/shard_map/all_gather | solution.py:762
  20.5 5.6 %collective-permute-start.3 = (f32[4,216]{1,0:T(4,128)S(1)}, f32[4,216]{1,0:T(4,128)S(1)}, u32[]{:S(2)}, u32[]{:S(2)}) collective-permute-start(f32[4,216]{1,0:T(4,128)S(1)} %pad_maximum_fusion.8), channel_id=1, source_target_pairs={{0,8},{1,9},{2,10},{3,11},{4,12},{5,13},{6,14},{7,15},{8,16},{9,17... | collective-permute-start | bytes 10376 | tf_op jit(solution)/shard_map/ppermute | solution.py:644
  22.1 4.9 %collective-permute-start.4 = (f32[4,216]{1,0:T(4,128)S(1)}, f32[4,216]{1,0:T(4,128)S(1)}, u32[]{:S(2)}, u32[]{:S(2)}) collective-permute-start(f32[4,216]{1,0:T(4,128)S(1)} %pad_maximum_fusion.8), channel_id=1, source_target_pairs={{0,16},{1,17},{2,18},{3,19},{4,20},{5,21},{6,22},{7,23},{8,24},{9,... | collective-permute-start | bytes 10376 | tf_op jit(solution)/shard_map/ppermute | solution.py:644
  24.7 3.8 collective-permute-start.5
  28.5 1.2 collective-permute-start.6
  33.9 3.0 collective-permute-start.7
  34.1 28.5 %collective-permute-start.10 = (bf16[512,1152]{1,0:T(8,128)(2,1)}, bf16[512,1152]{1,0:T(8,128)(2,1)}, u32[]{:S(2)}, u32[]{:S(2)}) collective-permute-start(bf16[512,1152]{1,0:T(8,128)(2,1)} %refs_4_.1), channel_id=1, source_target_pairs={{0,1},{1,0},{2,3},{3,2},{4,5},{5,4},{6,7},{7,6},{8,9},{9,8},{10,11... | collective-permute-start | bytes 3538952 | tf_op jit(solution)/shard_map/ppermute | solution.py:644
  35.2 32.2 %collective-permute-start.9 = (bf16[512,1152]{1,0:T(8,128)(2,1)}, bf16[512,1152]{1,0:T(8,128)(2,1)}, u32[]{:S(2)}, u32[]{:S(2)}) collective-permute-start(bf16[512,1152]{1,0:T(8,128)(2,1)} %refs_4_.1), channel_id=1, source_target_pairs={{0,4},{1,5},{2,6},{3,7},{4,0},{5,1},{6,2},{7,3},{8,12},{9,13},{10,... | collective-permute-start | bytes 3538952 | tf_op jit(solution)/shard_map/ppermute | solution.py:644
  52.0 52.6 %copy-start = (bf16[1152,640]{1,0:T(8,128)(2,1)}, bf16[1152,640]{1,0:T(8,128)(2,1)S(1)}, u32[]{:S(2)}) copy-start(bf16[1152,640]{1,0:T(8,128)(2,1)S(1)} %dynamic-slice_bitcast_fusion.w_ref.refs_3_.refs_4_) | copy-start | bytes 4423684
  52.0 32.2 %collective-permute-start.8 = (bf16[1152,640]{1,0:T(8,128)(2,1)S(1)}, bf16[1152,640]{1,0:T(8,128)(2,1)S(1)}, u32[]{:S(2)}, u32[]{:S(2)}) collective-permute-start(bf16[1152,640]{1,0:T(8,128)(2,1)S(1)} %dynamic-slice_bitcast_fusion.w_ref.refs_3_.refs_4_), channel_id=1, source_target_pairs={{0,1},{1,0},{2,3},{3,2},{4,6},{5,7},{6,4},{7,5},{8,9},{9,8},{10,11... | collective-permute-start | bytes 4423688 | tf_op jit(solution)/shard_map/ppermute | solution.py:644
  62.7 7.7 %collective-permute-start.11 = (bf16[512,1152]{1,0:T(8,128)(2,1)}, bf16[512,1152]{1,0:T(8,128)(2,1)}, u32[]{:S(2)}, u32[]{:S(2)}) collective-permute-start(bf16[512,1152]{1,0:T(8,128)(2,1)} %collective-permute-done.10.cot0), channel_id=1, source_target_pairs={{0,4},{1,5},{2,6},{3,7},{4,0},{5,1},{6,2},{7,3},{8,12},{9,13},{10,... | collective-permute-start | bytes 3538952 | tf_op jit(solution)/shard_map/ppermute | solution.py:644
  69.3 28.6 %collective-permute-start.13 = (bf16[1152,640]{1,0:T(8,128)(2,1)S(1)}, bf16[1152,640]{1,0:T(8,128)(2,1)}, u32[]{:S(2)}, u32[]{:S(2)}) collective-permute-start(bf16[1152,640]{1,0:T(8,128)(2,1)S(1)} %dynamic-slice_bitcast_fusion.w_ref.refs_3_.refs_4_), channel_id=1, source_target_pairs={{0,2},{1,3},{2,0},{3,1},{4,5},{5,4},{6,7},{7,6},{8,10},{9,11},{10,... | collective-permute-start | bytes 4423688 | tf_op jit(solution)/shard_map/ppermute | solution.py:644
  84.3 20.4 %collective-permute-start.12 = (bf16[1152,640]{1,0:T(8,128)(2,1)S(1)}, bf16[1152,640]{1,0:T(8,128)(2,1)}, u32[]{:S(2)}, u32[]{:S(2)}) collective-permute-start(bf16[1152,640]{1,0:T(8,128)(2,1)S(1)} %collective-permute-done.8.w_ref.refs_5_.refs_6_), channel_id=1, source_target_pairs={{0,2},{1,3},{2,0},{3,1},{4,5},{5,4},{6,7},{7,6},{8,10},{9,11},{10,... | collective-permute-start | bytes 4423688 | tf_op jit(solution)/shard_map/ppermute | solution.py:644
  86.2 319.7 %reduce-scatter.6.cloned.1.call-start = ((), (), s32[]{:S(2)}) async-start(), calls=%async_computation.7 | async-start | bytes 2985984 | tf_op jit(solution)/shard_map/reduce_scatter | solution.py:825
  116.8 11.0 %collective-permute-start.14 = (bf16[512,1152]{1,0:T(8,128)(2,1)}, bf16[512,1152]{1,0:T(8,128)(2,1)S(1)}, u32[]{:S(2)}, u32[]{:S(2)}) collective-permute-start(bf16[512,1152]{1,0:T(8,128)(2,1)} %get-tuple-element.95), channel_id=1, source_target_pairs={{0,4},{1,5},{2,6},{3,7},{4,0},{5,1},{6,2},{7,3},{8,12},{9,13},{10,... | collective-permute-start | bytes 3538952 | tf_op jit(solution)/shard_map/ppermute | solution.py:644
  125.5 8.8 %collective-permute-start.16 = (bf16[1152,1152]{1,0:T(8,128)(2,1)}, bf16[1152,1152]{1,0:T(8,128)(2,1)}, u32[]{:S(2)}, u32[]{:S(2)}) collective-permute-start(bf16[1152,1152]{1,0:T(8,128)(2,1)} %all-gather.6.cloned.1.call-done.w1_own), channel_id=1, source_target_pairs={{4,6},{5,7},{6,4},{7,5},{12,14},{13,15},{14,12},{15,13},{20,22},{2... | collective-permute-start | bytes 7962632 | tf_op jit(solution)/shard_map/ppermute | solution.py:665
  131.2 3.1 collective-permute-start.15
  131.7 51.5 %collective-permute-start.19 = (bf16[1152,1152]{1,0:T(8,128)(2,1)}, bf16[1152,1152]{1,0:T(8,128)(2,1)S(1)}, u32[]{:S(2)}, u32[]{:S(2)}) collective-permute-start(bf16[1152,1152]{1,0:T(8,128)(2,1)} %all-gather.8.cloned.1.call-done.w2_own), channel_id=1, source_target_pairs={{4,6},{5,7},{6,4},{7,5},{12,14},{13,15},{14,12},{15,13},{20,22},{2... | collective-permute-start | bytes 7962632 | tf_op jit(solution)/shard_map/ppermute | solution.py:665
  132.8 28.0 %collective-permute-start.17 = (bf16[512,1152]{1,0:T(8,128)(2,1)S(1)}, bf16[512,1152]{1,0:T(8,128)(2,1)S(1)}, u32[]{:S(2)}, u32[]{:S(2)}) collective-permute-start(bf16[512,1152]{1,0:T(8,128)(2,1)S(1)} %add_convert_fusion.3.rows0), channel_id=1, source_target_pairs={{0,1},{1,0},{2,3},{3,2},{4,5},{5,4},{6,7},{7,6},{8,9},{9,8},{10,11... | collective-permute-start | bytes 3538952 | tf_op jit(solution)/shard_map/ppermute | solution.py:644
  160.8 14.9 %collective-permute-start.18 = (bf16[512,1152]{1,0:T(8,128)(2,1)S(1)}, bf16[512,1152]{1,0:T(8,128)(2,1)S(1)}, u32[]{:S(2)}, u32[]{:S(2)}) collective-permute-start(bf16[512,1152]{1,0:T(8,128)(2,1)S(1)} %collective-permute-done.17.rows0), channel_id=1, source_target_pairs={{0,4},{1,5},{2,6},{3,7},{4,0},{5,1},{6,2},{7,3},{8,12},{9,13},{10,... | collective-permute-start | bytes 3538952 | tf_op jit(solution)/shard_map/ppermute | solution.py:644
  200.8 9.6 %collective-permute-start.20 = (bf16[512,1152]{1,0:T(8,128)(2,1)S(1)}, bf16[512,1152]{1,0:T(8,128)(2,1)S(1)}, u32[]{:S(2)}, u32[]{:S(2)}) collective-permute-start(bf16[512,1152]{1,0:T(8,128)(2,1)S(1)} %get-tuple-element.108), channel_id=1, source_target_pairs={{0,4},{1,5},{2,6},{3,7},{4,0},{5,1},{6,2},{7,3},{8,12},{9,13},{10,... | collective-permute-start | bytes 3538952 | tf_op jit(solution)/shard_map/ppermute | solution.py:644
  204.5 7.2 %collective-permute-start.21 = (bf16[512,1152]{1,0:T(8,128)(2,1)S(1)}, bf16[512,1152]{1,0:T(8,128)(2,1)S(1)}, u32[]{:S(2)}, u32[]{:S(2)}) collective-permute-start(bf16[512,1152]{1,0:T(8,128)(2,1)S(1)} %get-tuple-element.114), channel_id=1, source_target_pairs={{0,4},{1,5},{2,6},{3,7},{4,0},{5,1},{6,2},{7,3},{8,12},{9,13},{10,... | collective-permute-start | bytes 3538952 | tf_op jit(solution)/shard_map/ppermute | solution.py:644
  230.1 2.9 collective-permute-start.24
  230.6 11.8 %collective-permute-start.26 = (bf16[1152,1152]{1,0:T(8,128)(2,1)S(1)}, bf16[1152,1152]{1,0:T(8,128)(2,1)S(1)}, u32[]{:S(2)}, u32[]{:S(2)}) collective-permute-start(bf16[1152,1152]{1,0:T(8,128)(2,1)S(1)} %convolution_add_fusion.1), channel_id=1, source_target_pairs={{4,6},{5,7},{6,4},{7,5},{12,14},{13,15},{14,12},{15,13},{20,22},{2... | collective-permute-start | bytes 7962632 | tf_op jit(solution)/shard_map/ppermute | solution.py:665
  244.1 202.6 %reduce-scatter.4.cloned.1.call-start = ((), (), s32[]{:S(2)}) async-start(), calls=%async_computation.6 | async-start | bytes 2985984 | tf_op jit(solution)/shard_map/reduce_scatter | solution.py:825
  244.2 16.5 %collective-permute-start.25 = (bf16[512,1152]{1,0:T(8,128)(2,1)}, bf16[512,1152]{1,0:T(8,128)(2,1)S(1)}, u32[]{:S(2)}, u32[]{:S(2)}) collective-permute-start(bf16[512,1152]{1,0:T(8,128)(2,1)} %add_convert_fusion.2), channel_id=1, source_target_pairs={{0,1},{1,0},{2,3},{3,2},{4,5},{5,4},{6,7},{7,6},{8,9},{9,8},{10,11... | collective-permute-start | bytes 3538952 | tf_op jit(solution)/shard_map/ppermute | solution.py:644
  245.3 68.6 %collective-permute-start.28 = (bf16[1152,1152]{1,0:T(8,128)(2,1)}, bf16[1152,1152]{1,0:T(8,128)(2,1)S(1)}, u32[]{:S(2)}, u32[]{:S(2)}) collective-permute-start(bf16[1152,1152]{1,0:T(8,128)(2,1)} %fusion), channel_id=1, source_target_pairs={{4,6},{5,7},{6,4},{7,5},{12,14},{13,15},{14,12},{15,13},{20,22},{2... | collective-permute-start | bytes 7962632 | tf_op jit(solution)/shard_map/ppermute | solution.py:665
  268.3 22.7 %collective-permute-start.27 = (bf16[512,1152]{1,0:T(8,128)(2,1)S(1)}, bf16[512,1152]{1,0:T(8,128)(2,1)S(1)}, u32[]{:S(2)}, u32[]{:S(2)}) collective-permute-start(bf16[512,1152]{1,0:T(8,128)(2,1)S(1)} %get-tuple-element.128.own_ref), channel_id=1, source_target_pairs={{0,4},{1,5},{2,6},{3,7},{4,0},{5,1},{6,2},{7,3},{8,12},{9,13},{10,... | collective-permute-start | bytes 3538952 | tf_op jit(solution)/shard_map/ppermute | solution.py:644
  316.8 135.2 %reduce-scatter.8.cloned.1.call-start = ((), (), s32[]{:S(2)}) async-start(), calls=%async_computation.8 | async-start | bytes 1843200 | tf_op jit(solution)/shard_map/reduce_scatter | solution.py:865
  317.1 19.6 %collective-permute-start.29 = (bf16[1152,640]{1,0:T(8,128)(2,1)}, bf16[1152,640]{1,0:T(8,128)(2,1)S(1)}, u32[]{:S(2)}, u32[]{:S(2)}) collective-permute-start(bf16[1152,640]{1,0:T(8,128)(2,1)} %copy-done.22), channel_id=1, source_target_pairs={{0,2},{1,3},{2,0},{3,1},{4,5},{5,4},{6,7},{7,6},{8,10},{9,11},{10,... | collective-permute-start | bytes 4423688 | tf_op jit(solution)/shard_map/ppermute | solution.py:644
  318.4 36.6 %collective-permute-start.30 = (bf16[1152,640]{1,0:T(8,128)(2,1)}, bf16[1152,640]{1,0:T(8,128)(2,1)}, u32[]{:S(2)}, u32[]{:S(2)}) collective-permute-start(bf16[1152,640]{1,0:T(8,128)(2,1)} %copy-done.21), channel_id=1, source_target_pairs={{0,2},{1,3},{2,0},{3,1},{4,5},{5,4},{6,7},{7,6},{8,10},{9,11},{10,... | collective-permute-start | bytes 4423688 | tf_op jit(solution)/shard_map/ppermute | solution.py:644
  351.1 32.4 %collective-permute-start.31 = (bf16[1152,640]{1,0:T(8,128)(2,1)}, bf16[1152,640]{1,0:T(8,128)(2,1)}, u32[]{:S(2)}, u32[]{:S(2)}) collective-permute-start(bf16[1152,640]{1,0:T(8,128)(2,1)} %get-tuple-element.143), channel_id=1, source_target_pairs={{0,1},{1,0},{2,3},{3,2},{4,6},{5,7},{6,4},{7,5},{8,9},{9,8},{10,11... | collective-permute-start | bytes 4423688 | tf_op jit(solution)/shard_map/ppermute | solution.py:644
  353.7 45.4 %collective-permute-start.23 = (bf16[512,1152]{1,0:T(8,128)(2,1)}, bf16[512,1152]{1,0:T(8,128)(2,1)}, u32[]{:S(2)}, u32[]{:S(2)}) collective-permute-start(bf16[512,1152]{1,0:T(8,128)(2,1)} %add_convert_fusion.1), channel_id=1, source_target_pairs={{0,1},{1,0},{2,3},{3,2},{4,5},{5,4},{6,7},{7,6},{8,9},{9,8},{10,11... | collective-permute-start | bytes 3538952 | tf_op jit(solution)/shard_map/ppermute | solution.py:644
  354.4 44.7 %collective-permute-start.22 = (bf16[512,1152]{1,0:T(8,128)(2,1)}, bf16[512,1152]{1,0:T(8,128)(2,1)}, u32[]{:S(2)}, u32[]{:S(2)}) collective-permute-start(bf16[512,1152]{1,0:T(8,128)(2,1)} %copy-done.23), channel_id=1, source_target_pairs={{0,4},{1,5},{2,6},{3,7},{4,0},{5,1},{6,2},{7,3},{8,12},{9,13},{10,... | collective-permute-start | bytes 3538952 | tf_op jit(solution)/shard_map/ppermute | solution.py:644
  399.0 6.9 %collective-permute-start.32 = (bf16[512,1152]{1,0:T(8,128)(2,1)}, bf16[512,1152]{1,0:T(8,128)(2,1)}, u32[]{:S(2)}, u32[]{:S(2)}) collective-permute-start(bf16[512,1152]{1,0:T(8,128)(2,1)} %get-tuple-element.154), channel_id=1, source_target_pairs={{0,4},{1,5},{2,6},{3,7},{4,0},{5,1},{6,2},{7,3},{8,12},{9,13},{10,... | collective-permute-start | bytes 3538952 | tf_op jit(solution)/shard_map/ppermute | solution.py:644
  412.3 8.9 %collective-permute-start.33 = (f32[5,8,1152]{2,1,0:T(8,128)}, f32[5,8,1152]{2,1,0:T(8,128)S(1)}, u32[]{:S(2)}, u32[]{:S(2)}) collective-permute-start(f32[5,8,1152]{2,1,0:T(8,128)} %pack_small.1), channel_id=1, source_target_pairs={{0,1},{1,0},{2,3},{3,2},{4,5},{5,4},{6,7},{7,6},{8,9},{9,8},{10,11... | collective-permute-start | bytes 552968 | tf_op jit(solution)/shard_map/ppermute | solution.py:644
  413.5 10.9 %collective-permute-start.34 = (f32[5,8,1152]{2,1,0:T(8,128)}, f32[5,8,1152]{2,1,0:T(8,128)S(1)}, u32[]{:S(2)}, u32[]{:S(2)}) collective-permute-start(f32[5,8,1152]{2,1,0:T(8,128)} %pack_small.1), channel_id=1, source_target_pairs={{0,2},{1,3},{2,0},{3,1},{4,6},{5,7},{6,4},{7,5},{8,10},{9,11},{10,... | collective-permute-start | bytes 552968 | tf_op jit(solution)/shard_map/ppermute | solution.py:644
  413.9 10.5 %collective-permute-start.35 = (f32[5,8,1152]{2,1,0:T(8,128)}, f32[5,8,1152]{2,1,0:T(8,128)S(1)}, u32[]{:S(2)}, u32[]{:S(2)}) collective-permute-start(f32[5,8,1152]{2,1,0:T(8,128)} %pack_small.1), channel_id=1, source_target_pairs={{0,3},{1,2},{2,1},{3,0},{4,7},{5,6},{6,5},{7,4},{8,11},{9,10},{10,... | collective-permute-start | bytes 552968 | tf_op jit(solution)/shard_map/ppermute | solution.py:644
  424.5 13.3 %collective-permute-start.36 = (f32[5,8,1152]{2,1,0:T(8,128)S(1)}, f32[5,8,1152]{2,1,0:T(8,128)S(1)}, u32[]{:S(2)}, u32[]{:S(2)}) collective-permute-start(f32[5,8,1152]{2,1,0:T(8,128)S(1)} %add_add_fusion.2), channel_id=1, source_target_pairs={{0,8},{1,9},{2,10},{3,11},{4,12},{5,13},{6,14},{7,15},{8,16},{9,17... | collective-permute-start | bytes 552968 | tf_op jit(solution)/shard_map/ppermute | solution.py:644
  424.7 21.9 %collective-permute-start.37 = (f32[5,8,1152]{2,1,0:T(8,128)S(1)}, f32[5,8,1152]{2,1,0:T(8,128)S(1)}, u32[]{:S(2)}, u32[]{:S(2)}) collective-permute-start(f32[5,8,1152]{2,1,0:T(8,128)S(1)} %add_add_fusion.2), channel_id=1, source_target_pairs={{0,16},{1,17},{2,18},{3,19},{4,20},{5,21},{6,22},{7,23},{8,24},{9,... | collective-permute-start | bytes 552968 | tf_op jit(solution)/shard_map/ppermute | solution.py:644
  427.8 18.8 %collective-permute-start.38 = (f32[5,8,1152]{2,1,0:T(8,128)S(1)}, f32[5,8,1152]{2,1,0:T(8,128)S(1)}, u32[]{:S(2)}, u32[]{:S(2)}) collective-permute-start(f32[5,8,1152]{2,1,0:T(8,128)S(1)} %add_add_fusion.2), channel_id=1, source_target_pairs={{0,24},{1,25},{2,26},{3,27},{4,28},{5,29},{6,30},{7,31},{8,0},{9,1... | collective-permute-start | bytes 552968 | tf_op jit(solution)/shard_map/ppermute | solution.py:644
  448.6 1.4 collective-permute-start.39
  453.1 1.5 collective-permute-start.40
  (53 other events, 389.6 us)
Sparse Core Ops, SparseCore 0:
  11.0 39.4 all-gather.3
  52.1 32.7 all-gather.5
  86.6 33.0 all-gather.7
  244.3 57.7 reduce-scatter.5
  316.9 37.2 reduce-scatter.3
  402.7 39.6 reduce-scatter.7

commit v2 on v1

--- a/solution.py
+++ b/solution.py
@@ -58,6 +58,10 @@
 
 def far(x):
     return pltpu.with_memory_space_constraint(x, pltpu.HBM)
+
+
+def near(x):
+    return pltpu.with_memory_space_constraint(x, pltpu.VMEM)
 
 
 def padded(size):
@@ -114,8 +118,12 @@
         rows = slice(m * SEQ, (m + 1) * SEQ)
         group = slice(m * heads, (m + 1) * heads)
         mixed_ref[rows, :] = place(mixed[group], cols.shift, cols.window)
-        for h, (top, total) in enumerate(zip(tops[group], sums[group])):
-            lse_ref[rows, h : h + 1] = top + jnp.log(total)
+        lse = [top + jnp.log(total) for top, total in zip(tops[group], sums[group])]
+        lane = lax.broadcasted_iota(jnp.int32, (1, LANES), 1)
+        wide = jnp.broadcast_to(lse[0], (SEQ, LANES))
+        for h in range(1, heads):
+            wide = jnp.where(lane == h, lse[h], wide)
+        lse_ref[rows, :] = wide
     if len(outs) == 3:
         return
     mine_ref, other_ref = outs[3:]
@@ -148,12 +156,12 @@
     out_specs = [
         pl.BlockSpec((tile, cols.three), turn),
         pl.BlockSpec((tile, cols.window), turn),
-        pl.BlockSpec((tile, cols.heads), turn),
+        pl.BlockSpec((tile, LANES), turn),
     ]
     out_shape = [
         pltpu.HBM((total, cols.three), BF16),
         pltpu.HBM((total, cols.window), BF16),
-        pltpu.HBM((total, cols.heads), F32),
+        pltpu.HBM((total, LANES), F32),
     ]
     if last:
         out_specs += [pl.BlockSpec((tile, width), whole)] * 2
@@ -286,7 +294,7 @@
             pl.BlockSpec(weight.shape, whole),
             pl.BlockSpec((tile, cols.three), step),
             pl.BlockSpec((tile, cols.window), step),
-            pl.BlockSpec((tile, cols.heads), step),
+            pl.BlockSpec((tile, LANES), step),
         ]
         + [anywhere] * len(extra),
         out_specs=[
@@ -313,41 +321,46 @@
             transcendentals=total * SEQ * cols.heads,
         ),
         name="attend_back",
-    )(own, far(other), far(rows), weight, far(qkv), far(mixed), far(lse), *map(far, extra))
+    )(far(own), far(other), far(rows), far(weight), far(qkv), far(mixed), far(lse), *extra)
 
 
 def sum_nt_kernel(count, inner, *refs):
     lefts, rights = refs[:count], refs[count : 2 * count]
-    mine_ref, other_ref = refs[2 * count :]
+    before, (mine_ref, other_ref) = refs[2 * count : -2], refs[-2:]
     total = dot_nt(lefts[0][...], rights[0][:, :inner])
     for left, right in zip(lefts[1:], rights[1:]):
         total += dot_nt(left[...], right[:, :inner])
-    value = total.astype(BF16)
     half = pl.num_programs(0) // 2
 
+    def store(target, source):
+        value = total + source[0][...].astype(F32) if source else total
+        target[...] = value.astype(BF16)
+
     @pl.when(pl.program_id(0) < half)
     def _():
-        other_ref[...] = value
+        store(other_ref, before[1:])
 
     @pl.when(pl.program_id(0) >= half)
     def _():
-        mine_ref[...] = value
-
-
-def sum_nt(lefts, rights, tile=SEQ):
+        store(mine_ref, before[:1])
+
+
+def sum_nt(lefts, rights, before=(), tile=SEQ):
     count = len(lefts)
     total, inner = lefts[0].shape
     width = rights[0].shape[0]
     half = total // 2 // tile
+    rows_specs = [
+        pl.BlockSpec((tile, width), lambda i: (jnp.maximum(i - half, 0), 0)),
+        pl.BlockSpec((tile, width), lambda i: (jnp.minimum(i, half - 1), 0)),
+    ]
     return pl.pallas_call(
         functools.partial(sum_nt_kernel, count, inner),
         grid=(2 * half,),
         in_specs=[pl.BlockSpec((tile, inner), lambda i: (lax.rem(i + half, 2 * half), 0))] * count
-        + [pl.BlockSpec(right.shape, lambda i: (0, 0), pipeline_mode=pl.Buffered(1)) for right in rights],
-        out_specs=[
-            pl.BlockSpec((tile, width), lambda i: (jnp.maximum(i - half, 0), 0)),
-            pl.BlockSpec((tile, width), lambda i: (jnp.minimum(i, half - 1), 0)),
-        ],
+        + [pl.BlockSpec(r.shape, lambda i: (0, 0), pipeline_mode=pl.Buffered(1)) for r in rights]
+        + rows_specs[: len(before)],
+        out_specs=rows_specs,
         out_shape=[
             jax.ShapeDtypeStruct((total // 2, width), BF16),
             pltpu.HBM((total // 2, width), BF16),
@@ -359,7 +372,7 @@
             transcendentals=0,
         ),
         name="sum_nt",
-    )(*map(far, lefts), *rights)
+    )(*map(far, lefts), *map(far, rights), *before)
 
 
 def spread_kernel(count, in_ref, *out_refs):
@@ -402,15 +415,8 @@
         fetch(got)
 
 
-def feed_in_kernel(
-    half, core_ref, rows0, rows1, w1_own, w1_got, bias_ref, rows_ref, act_ref, slope_ref, w1, sems
-):
+def feed_in_kernel(half, rows0, rows1, w1, bias_ref, rows_ref, act_ref, slope_ref):
     step = pl.program_id(0)
-
-    @pl.when(step == 0)
-    def _():
-        fetch_weights(core_ref, [w1_own], [w1_got], [w1], sems)
-
     rows = jnp.where(step < half, rows0[...], rows1[...])
     rows_ref[...] = rows
     pre = dot_nn(rows, w1[...]) + bias_ref[...]
@@ -423,22 +429,20 @@
     slope_ref[...] = slope.astype(BF16)
 
 
-def feed_in(core, rows, weights, bias, tile=SEQ):
+def feed_in(rows, weight, bias, tile=SEQ):
     count, width = rows[0].shape
-    ff = weights[0].shape[1]
+    ff = weight.shape[1]
     half = count // tile
     step = lambda i: (i, 0)
-    anywhere = pl.BlockSpec(memory_space=pl.ANY)
+    whole = lambda i: (0, 0)
     return pl.pallas_call(
         functools.partial(feed_in_kernel, half),
         grid=(2 * half,),
         in_specs=[
-            pl.BlockSpec(memory_space=pltpu.SMEM),
             pl.BlockSpec((tile, width), lambda i: (jnp.minimum(i, half - 1), 0)),
             pl.BlockSpec((tile, width), lambda i: (jnp.maximum(i - half, 0), 0)),
-            anywhere,
-            anywhere,
-            pl.BlockSpec((1, ff), lambda i: (0, 0)),
+            pl.BlockSpec((width, ff), whole, pipeline_mode=pl.Buffered(1)),
+            pl.BlockSpec((1, ff), whole),
         ],
         out_specs=[
             pl.BlockSpec((tile, width), step),
@@ -450,7 +454,6 @@
             jax.ShapeDtypeStruct((2 * count, ff), BF16),
             jax.ShapeDtypeStruct((2 * count, ff), BF16),
         ],
-        scratch_shapes=[pltpu.VMEM((width, ff), BF16), pltpu.SemaphoreType.DMA((1,))],
         compiler_params=pltpu.CompilerParams(vmem_limit_bytes=FEED_VMEM),
         cost_estimate=pl.CostEstimate(
             flops=4 * count * width * ff,
@@ -458,18 +461,18 @@
             transcendentals=2 * count * ff,
         ),
         name="feed_in",
-    )(core, *rows, *[far(w) for w in weights], bias)
+    )(*rows, near(weight), bias)
 
 
 def feed_out_kernel(
-    half, core_ref, cot0, cot1, act_ref, slope_ref, w1_own, w1_got, w2_own, w2_got,
-    gpre_ref, out0, out1, grad0, grad1, sums_ref, w1, w2, sems,
+    half, core_ref, cot0, cot1, act_ref, slope_ref, w1, w2_own, w2_got,
+    gpre_ref, out0, out1, grad0, grad1, sums_ref, w2, sems,
 ):
     step = pl.program_id(0)
 
     @pl.when(step == 0)
     def _():
-        fetch_weights(core_ref, [w1_own, w2_own], [w1_got, w2_got], [w1, w2], sems)
+        fetch_weights(core_ref, [w2_own], [w2_got], [w2], sems)
 
     first = step < half
     cot = jnp.where(first, cot0[...], cot1[...])
@@ -517,7 +520,8 @@
             pl.BlockSpec((tile, ff), step),
             pl.BlockSpec((tile, ff), step),
         ]
-        + [anywhere] * 4,
+        + [pl.BlockSpec((width, ff), lambda i: (0, 0), pipeline_mode=pl.Buffered(1))]
+        + [anywhere] * 2,
         out_specs=[
             pl.BlockSpec((tile, ff), step),
             pl.BlockSpec((tile, width), low),
@@ -527,13 +531,9 @@
             pl.BlockSpec((1, ff), lambda i: (0, 0)),
         ],
         out_shape=[jax.ShapeDtypeStruct((2 * count, ff), BF16)]
-        + [jax.ShapeDtypeStruct((count, width), BF16)] * 4
+        + [pltpu.HBM((count, width), BF16)] * 4
         + [jax.ShapeDtypeStruct((1, ff), F32)],
-        scratch_shapes=[
-            pltpu.VMEM((width, ff), BF16),
-            pltpu.VMEM((width, ff), BF16),
-            pltpu.SemaphoreType.DMA((2,)),
-        ],
+        scratch_shapes=[pltpu.VMEM((width, ff), BF16), pltpu.SemaphoreType.DMA((1,))],
         compiler_params=pltpu.CompilerParams(vmem_limit_bytes=FEED_OUT_VMEM),
         cost_estimate=pl.CostEstimate(
             flops=12 * count * width * ff,
@@ -541,23 +541,24 @@
             transcendentals=0,
         ),
         name="feed_out",
-    )(core, *cots, act, slope, *[far(w) for w in weights])
+    )(core, *cots, act, slope, near(weights[0]), far(weights[1]), weights[2])
 
 
 def norm_back_kernel(count, *refs):
     grads, (rows_ref, cot_ref, gain_ref) = refs[:count], refs[count : count + 3]
-    out_ref, rounded_ref, sums_ref = refs[count + 3 :]
+    out_ref, *rounded_ref, sums_ref = refs[count + 3 :]
     grad = grads[0][...].astype(F32)
     for other in grads[1:]:
         grad += other[...].astype(F32)
-    rows = rows_ref[...]
+    rows = rows_ref[...].astype(F32)
     center = rows - jnp.mean(rows, axis=-1, keepdims=True)
     spread = lax.rsqrt(jnp.mean(center * center, axis=-1, keepdims=True) + EPS)
     normed = center * spread
     cot = cot_ref[...].astype(F32)
     out = cot + norm_back(grad, normed, spread, gain_ref[...])
     out_ref[...] = out
-    rounded_ref[...] = out.astype(BF16)
+    for ref in rounded_ref:
+        ref[...] = out.astype(BF16)
 
     @pl.when(pl.program_id(0) == 0)
     def _():
@@ -567,17 +568,18 @@
         sums_ref[i : i + 1, :] += jnp.sum(value, axis=0, keepdims=True)
 
 
-def norm_back_rows(grads, rows, cot, gain, tile=128):
+def norm_back_rows(grads, rows, cot, gain, rounded, tile=128):
     count, width = rows.shape
     step = pl.BlockSpec((tile, width), lambda i: (i, 0))
+    extra = [pltpu.HBM((count, width), BF16)] if rounded else []
     return pl.pallas_call(
         functools.partial(norm_back_kernel, len(grads)),
         grid=(count // tile,),
         in_specs=[step] * (len(grads) + 2) + [pl.BlockSpec((1, width), lambda i: (0, 0))],
-        out_specs=[step, step, pl.BlockSpec((8, width), lambda i: (0, 0))],
+        out_specs=[step] * (1 + len(extra)) + [pl.BlockSpec((8, width), lambda i: (0, 0))],
         out_shape=[
-            jax.ShapeDtypeStruct((count, width), F32),
-            jax.ShapeDtypeStruct((count, width), BF16),
+            pltpu.HBM((count, width), F32),
+            *extra,
             jax.ShapeDtypeStruct((8, width), F32),
         ],
         compiler_params=pltpu.CompilerParams(vmem_limit_bytes=16 << 20),
@@ -587,41 +589,74 @@
             transcendentals=count,
         ),
         name="norm_back",
-    )(*grads, rows, cot, gain)
-
-
-def pack_kernel(where_ref, gain_ref, shift_ref, second_ref, *refs):
+    )(*map(far, grads), far(rows), far(cot), gain)
+
+
+def norm_kernel(count, *refs):
+    parts, (shift_ref, gain_ref, bias_ref) = refs[:count], refs[count : count + 3]
+    rows_ref, out_ref = refs[count + 3 :]
+    rows = parts[0][...].astype(F32) + shift_ref[...]
+    for part in parts[1:]:
+        rows += part[...].astype(F32)
+    rows_ref[...] = rows
+    out_ref[...] = norm_rows(rows, gain_ref[...], bias_ref[...])[0].astype(BF16)
+
+
+def norm_sum(parts, shift, gain, bias, tile=128):
+    count, width = parts[0].shape
+    step = pl.BlockSpec((tile, width), lambda i: (i, 0))
+    row = pl.BlockSpec((1, width), lambda i: (0, 0))
+    return pl.pallas_call(
+        functools.partial(norm_kernel, len(parts)),
+        grid=(count // tile,),
+        in_specs=[step] * len(parts) + [row] * 3,
+        out_specs=[step, step],
+        out_shape=[pltpu.HBM((count, width), F32), jax.ShapeDtypeStruct((count, width), BF16)],
+        compiler_params=pltpu.CompilerParams(vmem_limit_bytes=16 << 20),
+        cost_estimate=pl.CostEstimate(
+            flops=12 * count * width,
+            bytes_accessed=count * width * (2 * len(parts) + 6),
+            transcendentals=count,
+        ),
+        name="norm_sum",
+    )(*parts, shift, gain, bias)
+
+
+def pack_kernel(where_ref, first_ref, second_ref, *refs):
     units, bias_ref, out_ref = refs[:-2], refs[-2], refs[-1]
     out_ref[...] = jnp.zeros_like(out_ref)
-    width = gain_ref.shape[1]
-    out_ref[0, 0:1, :width] = gain_ref[...]
-    out_ref[0, 2:3, :width] = shift_ref[...]
-    for spot, row in ((1, 0), (3, 2), (4, 1), (5, 3)):
-        out_ref[0, spot : spot + 1, :width] = second_ref[row : row + 1, :]
+    width = first_ref.shape[1]
+    for spot, ref, row in (
+        (0, first_ref, 0), (1, second_ref, 0), (2, first_ref, 1),
+        (3, second_ref, 2), (4, second_ref, 1), (5, second_ref, 3),
+    ):
+        out_ref[spot : spot + 1, :width] = ref[row : row + 1, :]
     core = where_ref[0]
     for n, unit in enumerate(units):
-        hp = unit.shape[1]
-        spot = 1 + where_ref[2 + n]
+        lanes = unit.shape[1]
+        spot = 7 + 2 * where_ref[2 + n]
+        sums = jnp.concatenate([unit[0:1, :], unit[1:2, :]], axis=1)
 
         @pl.when(core == 0)
         def _():
-            out_ref[spot, 1:3, :hp] = unit[...]
+            out_ref[pl.ds(spot, 1), : 2 * lanes] = sums
 
         @pl.when(core != 0)
         def _():
-            out_ref[spot, 3:5, :hp] = unit[...]
-
-    out_ref[1 + where_ref[1], 0:1, : bias_ref.shape[1]] = bias_ref[...]
+            out_ref[pl.ds(spot, 1), 2 * lanes : 4 * lanes] = sums
+
+    out_ref[pl.ds(6 + 2 * where_ref[1], 1), : bias_ref.shape[1]] = bias_ref[...]
 
 
 def pack_small(where, vectors, units, bias, spots):
-    lanes = max(x.shape[1] for x in [*vectors, *units, bias])
+    lanes = max(x.shape[1] for x in [*vectors, bias])
+    rows = -(-(6 + 2 * spots) // 8) * 8
     return pl.pallas_call(
         pack_kernel,
         in_specs=[pl.BlockSpec(memory_space=pltpu.SMEM)]
         + [pl.BlockSpec(memory_space=pltpu.VMEM)] * (len(vectors) + len(units) + 1),
         out_specs=pl.BlockSpec(memory_space=pltpu.VMEM),
-        out_shape=jax.ShapeDtypeStruct((1 + spots, 8, lanes), F32),
+        out_shape=jax.ShapeDtypeStruct((rows, lanes), F32),
         name="pack_small",
     )(where, *vectors, *units, bias)
 
@@ -744,14 +779,14 @@
         ff_bias = jnp.pad(ff_bias, (0, wide - ff)).reshape(1, wide)
 
         inputs_f = tokens.astype(F32)
-        first_f, normed_one, spread_one = norm_rows(inputs_f, gain_rows[0], shifts[0])
-        first = first_f.astype(BF16)
+        first = norm_rows(inputs_f, gain_rows[0], shifts[0])[0].astype(BF16)
         first_chip = jnp.concatenate([first, swap_core(first)], axis=0)
 
         cots = [(g, swap_core(g)) for g in [cotangent, *cot_far]]
-        cot_rows = [jnp.concatenate(pair, axis=0) for pair in cots]
         early = (first_chip, unit_bias, ff_bias)
         attn_w = [lax.dynamic_index_in_dim(tie(gathered, *early), c, 0, keepdims=False)]
+        saved = [attend(cols, first_chip, attn_w[0], scale, unit_bias[0])]
+        cot_rows = [jnp.concatenate([tie(g, saved[0][1]), o], axis=0) for g, o in cots]
         for i in range(bits):
             sent = list(attn_w)
             if i:
@@ -765,8 +800,7 @@
 
         fc1_own, fc2_own = gather_ff(w_fc1), gather_ff(tie(w_fc2.T, *vecs))
 
-        saved = []
-        for p in range(nt):
+        for p in range(1, nt):
             before = None
             if p == nt - 1:
                 before = ([s[1] for s in saved], attn_w[:p])
@@ -774,20 +808,19 @@
         attn_mine, attn_other = saved[-1][3:]
         fc1_got = swap_top(tie(fc1_own, attn_w[nt - 1], attn_w[nt - 2]))
         fc2_got = swap_top(fc2_own)
-        attention = attn_mine.astype(F32) + swap_core(attn_other).astype(F32)
-        hidden_one = inputs_f + attention + shifts[1]
-        second_f = norm_rows(hidden_one, gain_rows[1], shifts[2])[0]
+        hidden_one, second = norm_sum(
+            [tokens, attn_mine, swap_core(attn_other)], shifts[1], gain_rows[1], shifts[2]
+        )
 
         core = c.astype(jnp.int32).reshape(1)
-        second = second_f.astype(BF16)
         second_far = [swap_tensor(second, i) for i in others]
-        fc1_pair, fc2_pair = (fc1_own, fc1_got), (fc2_own, fc2_got)
+        fc1 = by_core(fc1_own, fc1_got)
         ins = [None] * low
-        ins[0] = feed_in(core, (second, swap_core(second)), fc1_pair, ff_bias)
+        ins[0] = feed_in((second, swap_core(second)), fc1, ff_bias)
         grad_fc2_t = dot_tn(cot_rows[0], ins[0][1])
         for i, rows_far in zip(others, second_far):
             rows_far = tie(rows_far, grad_fc2_t)
-            ins[i] = feed_in(core, (rows_far, swap_core(rows_far)), fc1_pair, ff_bias)
+            ins[i] = feed_in((rows_far, swap_core(rows_far)), fc1, ff_bias)
 
         outs, grad_sums, pres, grad_fc1_bias = [None] * low, [None] * low, [None] * low, 0
         after = []
@@ -796,7 +829,7 @@
             if i == 0 or i == low - 1:
                 slope = tie(slope, *after)
             pres[i], out0, out1, grad0, grad1, sums = feed_out(
-                core, cots[i], act, slope, fc1_pair + fc2_pair
+                core, cots[i], act, slope, (fc1, fc2_own, fc2_got)
             )
             grad_fc1_bias = grad_fc1_bias + sums
             got = swap_core(grad1)
@@ -837,7 +870,7 @@
             mlp_out = mlp_out + swap_tensor(outs[i], i).astype(F32)
 
         grad_hidden, hidden_in, second_sums = norm_back_rows(
-            grad_second, hidden_one, cotangent, gain_rows[1]
+            grad_second, hidden_one, cotangent, gain_rows[1], True
         )
         hidden_pair = (hidden_in, swap_core(hidden_in))
         back, after = {}, None
@@ -853,6 +886,12 @@
             value = back[p][1]
             grad_w[p] = value
             after = [value]
+            if p == 1:
+                parts = [q for q in range(nt) if q > 1]
+                first_part = sum_nt(
+                    [tie(back[q][0], value) for q in parts], [attn_w[q] for q in parts]
+                )
+                after = [value, first_part[0]]
             if p == nt - 2:
                 grad_fc1 = by_core(grad_fc1, tie(got_fc1, value))
                 grad_fc1_own = scatter_ff(grad_fc1)
@@ -862,6 +901,9 @@
             i = p.bit_length() - 1
             got_w[p] = (p - (1 << i), stage(value, i))
         grad_w = [(grad_w[0].astype(F32) + got_w[1][1].astype(F32)).astype(BF16)]
+        first_mine, first_other = sum_nt(
+            [tie(back[q][0], grad_w[0]) for q in (1, 0)], attn_w[1::-1], first_part
+        )
         own_half = lax.psum_scatter(
             grad_w[0],
             "dp",
@@ -869,7 +911,7 @@
             axis_index_groups=[list(range(0, ndp, 2)), list(range(1, ndp, 2))],
             tiled=True,
         )
-        own_half = own_half.reshape(2, part, packed)
+        own_half = tie(own_half, grad_fc1_own, grad_fc2_own).reshape(2, part, packed)
         kept = by_core(own_half[0], own_half[1]).astype(F32)
         got = swap_core(by_core(own_half[1], own_half[0])).astype(F32)
         halves = [by_core(kept, got), by_core(got, kept)]
@@ -881,21 +923,16 @@
         )
         grad_out_own = jnp.concatenate([g[:, 3 * hh : 4 * hh] for g in halves], axis=1).T
 
-        projs = [back[p][0] for p in range(nt)]
-        projs[0] = tie(projs[0], grad_w[0])
-        first_mine, first_other = sum_nt(projs, attn_w)
-        grad_first = first_mine.astype(F32) + swap_core(first_other).astype(F32)
-        gain_one = jnp.sum(grad_first * normed_one, axis=0, keepdims=True)
-        shift_one = jnp.sum(grad_first, axis=0, keepdims=True)
-        grad_tokens = grad_hidden + norm_back(grad_first, normed_one, spread_one, gain_rows[0])
-
+        grad_tokens, first_sums = norm_back_rows(
+            [first_mine, swap_core(first_other)], tokens, grad_hidden, gain_rows[0], False
+        )
         output = hidden_one + tie(mlp_out, grad_w[0]) + shifts[3]
 
         spots = [by_core(t ^ p, t ^ reverse_bits(p)) for p in range(nt)]
         where = jnp.stack([c, by_core(t, t ^ top)] + spots).astype(jnp.int32)
         total = pack_small(
             where,
-            [gain_one, shift_one, second_sums],
+            [first_sums, second_sums],
             [back[p][2] for p in range(nt)],
             grad_fc1_bias,
             nt,
@@ -903,15 +940,15 @@
         total = functools.reduce(jnp.add, [swap_tensor(total, i) for i in range(1, nt)], total)
         total = tie(total, grad_tokens)
         total = functools.reduce(jnp.add, [shift_z(total, k) for k in range(1, nz)], total)
-        total = tie(total, output, grad_fc1_own, grad_fc2_own)
+        total = tie(total, output, grad_fc1_own, grad_fc2_own, grad_qkv_own, grad_out_own)
         total = total + swap_core(total)
         own = lax.dynamic_slice_in_dim(
-            total[0, :vec_count, :width], (d * nt + t) * piece, piece, axis=1
-        )
-        mine = lax.dynamic_index_in_dim(total, 1 + t, 0, keepdims=False)
-        units = mine[1:5, : heads * LANES].reshape(2, 2, heads, LANES)[:, :, :, :HD]
+            total[:vec_count, :width], (d * nt + t) * piece, piece, axis=1
+        )
+        mine = lax.dynamic_slice_in_dim(total, 6 + 2 * t, 2, axis=0)
+        bias_total = mine[0, :ff]
+        units = mine[1, : 4 * heads * LANES].reshape(2, 2, heads, LANES)[:, :, :, :HD]
         head_total = units.transpose(1, 0, 2, 3).reshape(2, block)
-        bias_total = mine[0, :ff]
         return (
             output,
             grad_tokens,

time: 473 us -> 433 us (0.915)
  other arithmetic: 45 us -> 28.9 us
  starting transfers between devices: 77.6 us -> 61.5 us
  Pallas kernels: 135 us -> 150 us
  local copies, waits for them, and re-layouts: 40.6 us -> 29.8 us
  waiting for transfers between devices: 132 us -> 126 us
    ppermute x37, starting transfers between devices: 71.6 us -> 54.9 us  [send(): return lax.ppermute(value, AXES, perm(move))]
    unnamed x110 -> x84, local copies, waits for them, and re-layouts: 25.7 us -> 15.3 us
    all_gather x1, waiting for transfers between devices: 12 us -> 4.2 us  [body(): lax.all_gather(jnp.stack([half(0), half(1)]), 'dp', axis=1, tiled=True)]
    pallas_call x1 -> x2, Pallas kernels: 4.22 us -> 11.9 us  [norm_back_rows(): pl.pallas_call(functools.partial(norm_back_kernel, len(grads)), grid=(cou...]
    pallas_call x2, Pallas kernels: 16.3 us -> 11.4 us  [feed_in(): pl.pallas_call(functools.partial(feed_in_kernel, half), grid=(2 * half,),...]
    pallas_call x1 -> x2, Pallas kernels: 9.96 us -> 14.1 us  [sum_nt(): pl.pallas_call(functools.partial(sum_nt_kernel, count, inner), grid=(2 *...]
  transfers between devices with their start and end apart: 47 -> 47, of which waited for: 23 -> 23; matrix products, arithmetic and copies ran while one was open for 16% -> 11% of each run, Pallas kernels for 22% -> 27%
where the time goes in v2:
time: 433 us; the launch traced here: 427 us
  Pallas kernels  150 us (35%)
  waiting for transfers between devices  126 us (29%)
  starting transfers between devices  61.5 us (14%)
  local copies, waits for them, and re-layouts  29.8 us (7%)
  other arithmetic  28.9 us (7%)
  between operations  15.1 us (3%)
  matrix products  15 us (3%)
    ppermute x37, waiting for transfers between devices, send(): return lax.ppermute(value, AXES, perm(move))  122 us
    ppermute x37, starting transfers between devices, send(): return lax.ppermute(value, AXES, perm(move))  54.9 us
    pallas_call x4, Pallas kernels, attend_back(): pl.pallas_call(functools.partial(attend_back_kernel, cols, images, len(ex...  45 us
    pallas_call x2, Pallas kernels, feed_out(): pl.pallas_call(functools.partial(feed_out_kernel, half), grid=(2 * half,)...  32.7 us
    pallas_call x4, Pallas kernels, attend(): pl.pallas_call(functools.partial(attend_kernel, cols, images, len(mixeds)...  29.2 us
    unnamed x84, local copies, waits for them, and re-layouts  15.3 us
    dot_general x4, matrix products, dot_tn(): lax.dot_general(a, b, (((0,), (0,)), ((), ())), preferred_element_type=F32)  15 us
    pallas_call x2, Pallas kernels, sum_nt(): pl.pallas_call(functools.partial(sum_nt_kernel, count, inner), grid=(2 *...  14.1 us
  transfers between devices with their start and end apart: 47, of which 23 were waited for; matrix products, arithmetic and copies ran while one was open for 11% of the time, Pallas kernels for 27%

profile of v2, /device:TPU:0, one launch (start us, length us, event | category | flops | bytes accessed | tf_op | source)
XLA Modules:
  0.0 426.8 jit_solution(15518758711813937074)
XLA Ops:
  11.2 3.9 collective-permute-start.2
  15.8 1.9 collective-permute-start.10
  21.2 2.6 collective-permute-start.4
  25.8 2.3 collective-permute-done.5
  35.1 8.3 %collective-permute-done.10.cot0 = bf16[512,1152]{1,0:T(8,128)(2,1)} collective-permute-done((bf16[512,1152]{1,0:T(8,128)(2,1)}, bf16[512,1152]{1,0:T(8,128)(2,1)}, u32[]{:S(2)}, u32[]{:S(2)}) %collective-permute-start.10) | collective-permute-done | bytes 1179680 | tf_op jit(solution)/shard_map/ppermute | solution.py:679
  43.4 2.9 pad_maximum_fusion.rows_ref
  46.2 4.2 all-gather.4.cloned.1.call-done
  55.9 5.7 %attend.4 = (bf16[1024,512]{1,0:T(8,128)(2,1)}, bf16[1024,256]{1,0:T(8,128)(2,1)}, f32[1024,128]{1,0:T(8,128)}) custom-call(bf16[1024,1152]{1,0:T(8,128)(2,1)} %pad_maximum_fusion.rows_ref, bf16[1152,640]{1,0:T(8,128)(2,1)S(1)} %dynamic-slice_bitcast_fusion.w_ref.refs_3_.refs_4_, f32[1,512]{1,0:T(1,128)S(1)} %get-tuple-element.223.scale_ref, ...), custom_call_target="tpu_custom_call" | custom-call | flops 1778384896 | bytes 5013504 | tf_op jit(solution)/shard_map/attend/pallas_call | solution.py:169
  65.8 2.3 constant_dynamic-update-slice_fusion.2
  68.1 17.8 %collective-permute-done.8.w_ref.refs_5_.refs_6_.refs_2_ = bf16[1152,640]{1,0:T(8,128)(2,1)} collective-permute-done((bf16[1152,640]{1,0:T(8,128)(2,1)S(1)}, bf16[1152,640]{1,0:T(8,128)(2,1)}, u32[]{:S(2)}, u32[]{:S(2)}) %collective-permute-start.8) | collective-permute-done | bytes 1474592 | tf_op jit(solution)/shard_map/ppermute | solution.py:679
  85.9 2.3 collective-permute-start.12
  88.2 17.6 %collective-permute-done.12.w_ref.refs_3_ = bf16[1152,640]{1,0:T(8,128)(2,1)} collective-permute-done((bf16[1152,640]{1,0:T(8,128)(2,1)}, bf16[1152,640]{1,0:T(8,128)(2,1)}, u32[]{:S(2)}, u32[]{:S(2)}) %collective-permute-start.12) | collective-permute-done | bytes 1474592 | tf_op jit(solution)/shard_map/ppermute | solution.py:679
  105.8 2.8 collective-permute-start.16
  108.6 6.2 %attend.5 = (bf16[1024,512]{1,0:T(8,128)(2,1)}, bf16[1024,256]{1,0:T(8,128)(2,1)}, f32[1024,128]{1,0:T(8,128)}) custom-call(bf16[1024,1152]{1,0:T(8,128)(2,1)} %pad_maximum_fusion.rows_ref, bf16[1152,640]{1,0:T(8,128)(2,1)} %collective-permute-done.8.w_ref.refs_5_.refs_6_.refs_2_, f32[1,512]{1,0:T(1,128)S(1)} %get-tuple-element.223.scale_ref, ...), custom_call_target="tpu_custom_call" | custom-call | flops 1778384896 | bytes 5013504 | tf_op jit(solution)/shard_map/attend/pallas_call | solution.py:169
  114.8 6.1 %attend.6 = (bf16[1024,512]{1,0:T(8,128)(2,1)}, bf16[1024,256]{1,0:T(8,128)(2,1)}, f32[1024,128]{1,0:T(8,128)}) custom-call(bf16[1024,1152]{1,0:T(8,128)(2,1)} %pad_maximum_fusion.rows_ref, bf16[1152,640]{1,0:T(8,128)(2,1)} %collective-permute-done.13.w_ref.refs_7_.refs_8_.refs_2_, f32[1,512]{1,0:T(1,128)S(1)} %get-tuple-element.223.scale_ref, ...), custom_call_target="tpu_custom_call" | custom-call | flops 1778384896 | bytes 5013504 | tf_op jit(solution)/shard_map/attend/pallas_call | solution.py:169
  121.0 11.2 %attend.7 = (bf16[1024,512]{1,0:T(8,128)(2,1)}, bf16[1024,256]{1,0:T(8,128)(2,1)}, f32[1024,128]{1,0:T(8,128)}, bf16[512,1152]{1,0:T(8,128)(2,1)S(1)}, bf16[512,1152]{1,0:T(8,128)(2,1)}) custom-call(bf16[1024,1152]{1,0:T(8,128)(2,1)} %pad_maximum_fusion.rows_ref, bf16[1152,640]{1,0:T(8,128)(2,1)} %collective-permute-done.12.w_ref.refs_3_, ...), custom_call_target="tpu_custom_call" | custom-call | flops 1778384896 | bytes 5013504 | tf_op jit(solution)/shard_map/attend/pallas_call | solution.py:169
  134.2 2.1 collective-permute-done.14.refs_2_
  137.6 2.4 norm_sum.1
  142.9 2.0 collective-permute-done.15.rows1
  144.9 5.7 %feed_in.2 = (bf16[1024,1152]{1,0:T(8,128)(2,1)S(1)}, bf16[1024,1152]{1,0:T(8,128)(2,1)S(1)}, bf16[1024,1152]{1,0:T(8,128)(2,1)S(1)}) custom-call(bf16[512,1152]{1,0:T(8,128)(2,1)S(1)} %get-tuple-element.114.rows0, bf16[512,1152]{1,0:T(8,128)(2,1)S(1)} %collective-permute-done.15.rows1, bf16[1152,1152]{1,0:T(8,128)(2,1)S(1)} %broadcast_select_fusion.2.w1, ...), custom_call_target="tpu_custom_call" | custom-call | flops 2717908992 | bytes 12091392 | tf_op jit(solution)/shard_map/feed_in/pallas_call | solution.py:438
  150.6 3.3 fusion.34
  153.9 14.6 %collective-permute-done.17.rows0 = bf16[512,1152]{1,0:T(8,128)(2,1)S(1)} collective-permute-done((bf16[512,1152]{1,0:T(8,128)(2,1)S(1)}, bf16[512,1152]{1,0:T(8,128)(2,1)S(1)}, u32[]{:S(2)}, u32[]{:S(2)}) %collective-permute-start.17) | collective-permute-done | bytes 1179680 | tf_op jit(solution)/shard_map/ppermute | solution.py:679
  168.6 2.7 collective-permute-done.18.rows1
  171.3 5.7 %feed_in.3 = (bf16[1024,1152]{1,0:T(8,128)(2,1)S(1)}, bf16[1024,1152]{1,0:T(8,128)(2,1)S(1)}, bf16[1024,1152]{1,0:T(8,128)(2,1)S(1)}) custom-call(bf16[512,1152]{1,0:T(8,128)(2,1)S(1)} %collective-permute-done.17.rows0, bf16[512,1152]{1,0:T(8,128)(2,1)S(1)} %collective-permute-done.18.rows1, bf16[1152,1152]{1,0:T(8,128)(2,1)S(1)} %broadcast_select_fusion.2.w1, ...), custom_call_target="tpu_custom_call" | custom-call | flops 2717908992 | bytes 12091392 | tf_op jit(solution)/shard_map/feed_in/pallas_call | solution.py:438
  177.1 16.6 %feed_out.2 = (bf16[1024,1152]{1,0:T(8,128)(2,1)S(1)}, bf16[512,1152]{1,0:T(8,128)(2,1)}, bf16[512,1152]{1,0:T(8,128)(2,1)}, bf16[512,1152]{1,0:T(8,128)(2,1)}, ...) custom-call(s32[1]{0:T(128)} %bitcast.21.core_ref, bf16[512,1152]{1,0:T(8,128)(2,1)} %collective-permute-done.10.cot0, ...), custom_call_target="tpu_custom_call" | custom-call | flops 8153726976 | bytes 19464192 | tf_op jit(solution)/shard_map/feed_out/pallas_call | solution.py:513
  194.2 3.5 convolution_add_fusion.1
  200.4 16.1 %feed_out.3 = (bf16[1024,1152]{1,0:T(8,128)(2,1)S(1)}, bf16[512,1152]{1,0:T(8,128)(2,1)}, bf16[512,1152]{1,0:T(8,128)(2,1)}, bf16[512,1152]{1,0:T(8,128)(2,1)}, ...) custom-call(s32[1]{0:T(128)} %bitcast.21.core_ref, bf16[512,1152]{1,0:T(8,128)(2,1)} %refs_4_.1, ...), custom_call_target="tpu_custom_call" | custom-call | flops 8153726976 | bytes 19464192 | tf_op jit(solution)/shard_map/feed_out/pallas_call | solution.py:513
  217.7 2.0 collective-permute-done.24.refs_1_
  219.7 3.3 fusion.35
  223.0 5.0 %fusion = bf16[1152,1152]{1,0:T(8,128)(2,1)} fusion(f32[1152,1152]{1,0:T(8,128)S(1)} %fusion.35, bf16[1024,1152]{1,0:T(8,128)(2,1)S(1)} %get-tuple-element.137, bf16[1024,1152]{1,0:T(8,128)(2,1)S(1)} %get-tuple-element.138), kind=kOutput, calls=%fused_computation.2 | convolution fusion | flops 2720563200 | bytes 12681216 | tf_op jit(solution)/shard_map/dot_general | solution.py:48
  233.8 13.5 %collective-permute-done.25.refs_2_ = bf16[512,1152]{1,0:T(8,128)(2,1)S(1)} collective-permute-done((bf16[512,1152]{1,0:T(8,128)(2,1)S(1)}, bf16[512,1152]{1,0:T(8,128)(2,1)S(1)}, u32[]{:S(2)}, u32[]{:S(2)}) %collective-permute-start.25) | collective-permute-done | bytes 1179680 | tf_op jit(solution)/shard_map/ppermute | solution.py:679
  248.3 6.2 %norm_back.2 = (f32[512,1152]{1,0:T(8,128)}, bf16[512,1152]{1,0:T(8,128)(2,1)}, f32[8,1152]{1,0:T(8,128)S(1)}) custom-call(bf16[512,1152]{1,0:T(8,128)(2,1)} %get-tuple-element.135.refs_0_, bf16[512,1152]{1,0:T(8,128)(2,1)} %copy-done.22, bf16[512,1152]{1,0:T(8,128)(2,1)} %copy-done.25, f32[512,1152]{1,0:T(8,128)} %get-tuple-element.113.refs_3_, ...), custom_call_target="tpu_custom_call" | custom-call | flops 17694720 | bytes 10616832 | tf_op jit(solution)/shard_map/norm_back/pallas_call | solution.py:575
  255.2 21.2 %collective-permute-start.27 = (bf16[512,1152]{1,0:T(8,128)(2,1)}, bf16[512,1152]{1,0:T(8,128)(2,1)S(1)}, u32[]{:S(2)}, u32[]{:S(2)}) collective-permute-start(bf16[512,1152]{1,0:T(8,128)(2,1)} %get-tuple-element.144.own_ref), channel_id=1, source_target_pairs={{0,4},{1,5},{2,6},{3,7},{4,0},{5,1},{6,2},{7,3},{8,12},{9,13},{10,... | collective-permute-start | bytes 3538952 | tf_op jit(solution)/shard_map/ppermute | solution.py:679
  276.3 2.8 collective-permute-done.27.other_hbm
  280.2 11.2 %attend_back.4 = (bf16[1024,512]{1,0:T(8,128)(2,1)}, bf16[1152,640]{1,0:T(8,128)(2,1)}, f32[2,256]{1,0:T(2,128)S(1)}) custom-call(bf16[512,1152]{1,0:T(8,128)(2,1)} %get-tuple-element.144.own_ref, bf16[512,1152]{1,0:T(8,128)(2,1)} %copy-done.39, bf16[1024,1152]{1,0:T(8,128)(2,1)} %pad_maximum_fusion.rows_ref, ...), custom_call_target="tpu_custom_call" | custom-call | flops 2785017856 | bytes 9732096 | tf_op jit(solution)/shard_map/attend_back/pallas_call | solution.py:287
  291.9 10.7 %attend_back.5 = (bf16[1024,512]{1,0:T(8,128)(2,1)}, bf16[1152,640]{1,0:T(8,128)(2,1)S(1)}, f32[2,256]{1,0:T(2,128)S(1)}) custom-call(bf16[512,1152]{1,0:T(8,128)(2,1)} %get-tuple-element.144.own_ref, bf16[512,1152]{1,0:T(8,128)(2,1)} %copy-done.39, bf16[1024,1152]{1,0:T(8,128)(2,1)} %pad_maximum_fusion.rows_ref, ...), custom_call_target="tpu_custom_call" | custom-call | flops 2785017856 | bytes 9732096 | tf_op jit(solution)/shard_map/attend_back/pallas_call | solution.py:287
  307.4 17.5 %collective-permute-done.29.refs_0_ = bf16[1152,640]{1,0:T(8,128)(2,1)S(1)} collective-permute-done((bf16[1152,640]{1,0:T(8,128)(2,1)}, bf16[1152,640]{1,0:T(8,128)(2,1)S(1)}, u32[]{:S(2)}, u32[]{:S(2)}) %collective-permute-start.29) | collective-permute-done | bytes 1474592 | tf_op jit(solution)/shard_map/ppermute | solution.py:679
  325.0 11.8 %attend_back.6 = (bf16[1024,512]{1,0:T(8,128)(2,1)}, bf16[1152,640]{1,0:T(8,128)(2,1)}, f32[2,256]{1,0:T(2,128)S(1)}) custom-call(bf16[512,1152]{1,0:T(8,128)(2,1)} %get-tuple-element.144.own_ref, bf16[512,1152]{1,0:T(8,128)(2,1)} %copy-done.39, bf16[1024,1152]{1,0:T(8,128)(2,1)} %pad_maximum_fusion.rows_ref, ...), custom_call_target="tpu_custom_call" | custom-call | flops 2785017856 | bytes 9732096 | tf_op jit(solution)/shard_map/attend_back/pallas_call | solution.py:287
  340.7 7.0 %sum_nt.2 = (bf16[512,1152]{1,0:T(8,128)(2,1)S(1)}, bf16[512,1152]{1,0:T(8,128)(2,1)}) custom-call(bf16[1024,512]{1,0:T(8,128)(2,1)} %get-tuple-element.161.refs_0_, bf16[1024,512]{1,0:T(8,128)(2,1)} %get-tuple-element.163.refs_1_, bf16[1152,640]{1,0:T(8,128)(2,1)} %collective-permute-done.13.w_ref.refs_7_.refs_8_.refs_2_, ...), custom_call_target="tpu_custom_call" | custom-call | flops 2415919104 | bytes 6815744 | tf_op jit(solution)/shard_map/sum_nt/pallas_call | solution.py:357
  348.8 11.3 %attend_back.7 = (bf16[1024,512]{1,0:T(8,128)(2,1)}, bf16[1152,640]{1,0:T(8,128)(2,1)S(1)}, f32[2,256]{1,0:T(2,128)S(1)}) custom-call(bf16[512,1152]{1,0:T(8,128)(2,1)} %get-tuple-element.144.own_ref, bf16[512,1152]{1,0:T(8,128)(2,1)} %copy-done.39, bf16[1024,1152]{1,0:T(8,128)(2,1)} %pad_maximum_fusion.rows_ref, bf16[1152,640]{1,0:T(8,128)(2,1)} %copy-done.1, ...), custom_call_target="tpu_custom_call" | custom-call | flops 2785017856 | bytes 9732096 | tf_op jit(solution)/shard_map/attend_back/pallas_call | solution.py:287
  360.6 9.1 %collective-permute-done.31 = bf16[1152,640]{1,0:T(8,128)(2,1)} collective-permute-done((bf16[1152,640]{1,0:T(8,128)(2,1)}, bf16[1152,640]{1,0:T(8,128)(2,1)}, u32[]{:S(2)}, u32[]{:S(2)}) %collective-permute-start.31) | collective-permute-done | bytes 1474592 | tf_op jit(solution)/shard_map/ppermute | solution.py:679
  369.7 3.0 add_convert_fusion
  372.8 7.1 %sum_nt.3 = (bf16[512,1152]{1,0:T(8,128)(2,1)S(1)}, bf16[512,1152]{1,0:T(8,128)(2,1)}) custom-call(bf16[1024,512]{1,0:T(8,128)(2,1)} %get-tuple-element.169.refs_0_, bf16[1024,512]{1,0:T(8,128)(2,1)} %get-tuple-element.171.refs_1_, bf16[1152,640]{1,0:T(8,128)(2,1)} %collective-permute-done.8.w_ref.refs_5_.refs_6_.refs_2_, bf16[1152,640]{1,0:T(8,128)(2,1)} %copy-done.1, ...), custom_call_target="tpu_custom_call" | custom-call | flops 2415919104 | bytes 6815744 | tf_op jit(solution)/shard_map/sum_nt/pallas_call | solution.py:357
  382.4 2.2 convert_add_fusion
  387.5 5.7 %norm_back.3 = (f32[512,1152]{1,0:T(8,128)}, f32[8,1152]{1,0:T(8,128)S(1)}) custom-call(bf16[512,1152]{1,0:T(8,128)(2,1)} %copy-done.4, bf16[512,1152]{1,0:T(8,128)(2,1)} %copy-done.27, bf16[512,1152]{1,0:T(8,128)(2,1)} %refs_2_.1, f32[512,1152]{1,0:T(8,128)} %get-tuple-element.175.refs_3_, f32[1,1152]{1,0:T(1,128)S(1)} %copy-done.8), custom_call_target="tpu_custom_call" | custom-call | flops 17694720 | bytes 9437184 | tf_op jit(solution)/shard_map/norm_back/pallas_call | solution.py:575
  395.3 1.9 collective-permute-start.35
  407.1 1.9 slice_convert_fusion
  410.1 2.3 collective-permute-done.37
  (251 shorter events, 82.3 us)
Async XLA Ops:
  7.2 43.2 %all-gather.4.cloned.1.call-start = ((), (), s32[]{:S(2)}) async-start(), calls=%async_computation.3 | async-start | bytes 3317760 | tf_op jit(solution)/shard_map/all_gather | solution.py:743
  10.9 77.3 %all-gather.6.cloned.1.call-start = ((), (), s32[]{:S(2)}) async-start(), calls=%async_computation.4 | async-start | bytes 2985984 | tf_op jit(solution)/shard_map/all_gather | solution.py:797
  11.2 8.1 %collective-permute-start.2 = (f32[1868]{0:T(1024)S(1)}, f32[1868]{0:T(1024)S(1)}, u32[]{:S(2)}, u32[]{:S(2)}) collective-permute-start(f32[1868]{0:T(1024)S(1)} %concatenate.39), channel_id=1, source_target_pairs={{0,3},{1,2},{2,1},{3,0},{4,7},{5,6},{6,5},{7,4},{8,11},{9,10},{10,... | collective-permute-start | bytes 22424 | tf_op jit(solution)/shard_map/ppermute | solution.py:679
  15.2 4.2 collective-permute-start.1
  15.7 3.7 collective-permute-start
  15.8 27.6 %collective-permute-start.10 = (bf16[512,1152]{1,0:T(8,128)(2,1)}, bf16[512,1152]{1,0:T(8,128)(2,1)}, u32[]{:S(2)}, u32[]{:S(2)}) collective-permute-start(bf16[512,1152]{1,0:T(8,128)(2,1)} %refs_4_.1), channel_id=1, source_target_pairs={{0,1},{1,0},{2,3},{3,2},{4,5},{5,4},{6,7},{7,6},{8,9},{9,8},{10,11... | collective-permute-start | bytes 3538952 | tf_op jit(solution)/shard_map/ppermute | solution.py:679
  18.5 114.7 %all-gather.8.cloned.1.call-start = ((), (), s32[]{:S(2)}) async-start(), calls=%async_computation.5 | async-start | bytes 2985984 | tf_op jit(solution)/shard_map/all_gather | solution.py:797
  19.6 5.6 %collective-permute-start.3 = (f32[4,216]{1,0:T(4,128)S(1)}, f32[4,216]{1,0:T(4,128)S(1)}, u32[]{:S(2)}, u32[]{:S(2)}) collective-permute-start(f32[4,216]{1,0:T(4,128)S(1)} %pad_maximum_fusion.8), channel_id=1, source_target_pairs={{0,8},{1,9},{2,10},{3,11},{4,12},{5,13},{6,14},{7,15},{8,16},{9,17... | collective-permute-start | bytes 10376 | tf_op jit(solution)/shard_map/ppermute | solution.py:679
  21.2 4.5 %collective-permute-start.4 = (f32[4,216]{1,0:T(4,128)S(1)}, f32[4,216]{1,0:T(4,128)S(1)}, u32[]{:S(2)}, u32[]{:S(2)}) collective-permute-start(f32[4,216]{1,0:T(4,128)S(1)} %pad_maximum_fusion.8), channel_id=1, source_target_pairs={{0,16},{1,17},{2,18},{3,19},{4,20},{5,21},{6,22},{7,23},{8,24},{9,... | collective-permute-start | bytes 10376 | tf_op jit(solution)/shard_map/ppermute | solution.py:679
  23.8 4.3 %collective-permute-start.5 = (f32[4,216]{1,0:T(4,128)S(1)}, f32[4,216]{1,0:T(4,128)S(1)}, u32[]{:S(2)}, u32[]{:S(2)}) collective-permute-start(f32[4,216]{1,0:T(4,128)S(1)} %pad_maximum_fusion.8), channel_id=1, source_target_pairs={{0,24},{1,25},{2,26},{3,27},{4,28},{5,29},{6,30},{7,31},{8,0},{9,1... | collective-permute-start | bytes 10376 | tf_op jit(solution)/shard_map/ppermute | solution.py:679
  28.1 1.2 collective-permute-start.6
  33.5 9.9 %collective-permute-start.7 = (bf16[512,1152]{1,0:T(8,128)(2,1)S(1)}, bf16[512,1152]{1,0:T(8,128)(2,1)}, u32[]{:S(2)}, u32[]{:S(2)}) collective-permute-start(bf16[512,1152]{1,0:T(8,128)(2,1)S(1)} %fusion.6), channel_id=1, source_target_pairs={{0,4},{1,5},{2,6},{3,7},{4,0},{5,1},{6,2},{7,3},{8,12},{9,13},{10,... | collective-permute-start | bytes 3538952 | tf_op jit(solution)/shard_map/ppermute | solution.py:679
  33.7 30.5 %collective-permute-start.9 = (bf16[512,1152]{1,0:T(8,128)(2,1)}, bf16[512,1152]{1,0:T(8,128)(2,1)}, u32[]{:S(2)}, u32[]{:S(2)}) collective-permute-start(bf16[512,1152]{1,0:T(8,128)(2,1)} %refs_4_.1), channel_id=1, source_target_pairs={{0,4},{1,5},{2,6},{3,7},{4,0},{5,1},{6,2},{7,3},{8,12},{9,13},{10,... | collective-permute-start | bytes 3538952 | tf_op jit(solution)/shard_map/ppermute | solution.py:679
  43.4 22.4 %collective-permute-start.11 = (bf16[512,1152]{1,0:T(8,128)(2,1)}, bf16[512,1152]{1,0:T(8,128)(2,1)}, u32[]{:S(2)}, u32[]{:S(2)}) collective-permute-start(bf16[512,1152]{1,0:T(8,128)(2,1)} %collective-permute-done.10.cot0), channel_id=1, source_target_pairs={{0,4},{1,5},{2,6},{3,7},{4,0},{5,1},{6,2},{7,3},{8,12},{9,13},{10,... | collective-permute-start | bytes 3538952 | tf_op jit(solution)/shard_map/ppermute | solution.py:679
  51.9 69.0 %copy-start.1 = (bf16[1152,640]{1,0:T(8,128)(2,1)}, bf16[1152,640]{1,0:T(8,128)(2,1)S(1)}, u32[]{:S(2)}) copy-start(bf16[1152,640]{1,0:T(8,128)(2,1)S(1)} %dynamic-slice_bitcast_fusion.w_ref.refs_3_.refs_4_) | copy-start | bytes 4423684
  51.9 33.9 %collective-permute-start.8 = (bf16[1152,640]{1,0:T(8,128)(2,1)S(1)}, bf16[1152,640]{1,0:T(8,128)(2,1)}, u32[]{:S(2)}, u32[]{:S(2)}) collective-permute-start(bf16[1152,640]{1,0:T(8,128)(2,1)S(1)} %dynamic-slice_bitcast_fusion.w_ref.refs_3_.refs_4_), channel_id=1, source_target_pairs={{0,1},{1,0},{2,3},{3,2},{4,6},{5,7},{6,4},{7,5},{8,9},{9,8},{10,11... | collective-permute-start | bytes 4423688 | tf_op jit(solution)/shard_map/ppermute | solution.py:679
  54.3 332.1 %reduce-scatter.6.cloned.1.call-start = ((), (), s32[]{:S(2)}) async-start(), calls=%async_computation.7 | async-start | bytes 2985984 | tf_op jit(solution)/shard_map/reduce_scatter | solution.py:858
  54.3 33.8 %collective-permute-start.13 = (bf16[1152,640]{1,0:T(8,128)(2,1)S(1)}, bf16[1152,640]{1,0:T(8,128)(2,1)}, u32[]{:S(2)}, u32[]{:S(2)}) collective-permute-start(bf16[1152,640]{1,0:T(8,128)(2,1)S(1)} %dynamic-slice_bitcast_fusion.w_ref.refs_3_.refs_4_), channel_id=1, source_target_pairs={{0,2},{1,3},{2,0},{3,1},{4,5},{5,4},{6,7},{7,6},{8,10},{9,11},{10,... | collective-permute-start | bytes 4423688 | tf_op jit(solution)/shard_map/ppermute | solution.py:679
  85.9 19.9 %collective-permute-start.12 = (bf16[1152,640]{1,0:T(8,128)(2,1)}, bf16[1152,640]{1,0:T(8,128)(2,1)}, u32[]{:S(2)}, u32[]{:S(2)}) collective-permute-start(bf16[1152,640]{1,0:T(8,128)(2,1)} %collective-permute-done.8.w_ref.refs_5_.refs_6_.refs_2_), channel_id=1, source_target_pairs={{0,2},{1,3},{2,0},{3,1},{4,5},{5,4},{6,7},{7,6},{8,10},{9,11},{10,... | collective-permute-start | bytes 4423688 | tf_op jit(solution)/shard_map/ppermute | solution.py:679
  105.8 36.6 %collective-permute-start.16 = (bf16[1152,1152]{1,0:T(8,128)(2,1)}, bf16[1152,1152]{1,0:T(8,128)(2,1)}, u32[]{:S(2)}, u32[]{:S(2)}) collective-permute-start(bf16[1152,1152]{1,0:T(8,128)(2,1)} %all-gather.6.cloned.1.call-done), channel_id=1, source_target_pairs={{4,6},{5,7},{6,4},{7,5},{12,14},{13,15},{14,12},{15,13},{20,22},{2... | collective-permute-start | bytes 7962632 | tf_op jit(solution)/shard_map/ppermute | solution.py:700
  133.2 3.1 collective-permute-start.14
  133.2 43.8 %collective-permute-start.19 = (bf16[1152,1152]{1,0:T(8,128)(2,1)}, bf16[1152,1152]{1,0:T(8,128)(2,1)S(1)}, u32[]{:S(2)}, u32[]{:S(2)}) collective-permute-start(bf16[1152,1152]{1,0:T(8,128)(2,1)} %all-gather.8.cloned.1.call-done.w2_own), channel_id=1, source_target_pairs={{4,6},{5,7},{6,4},{7,5},{12,14},{13,15},{14,12},{15,13},{20,22},{2... | collective-permute-start | bytes 7962632 | tf_op jit(solution)/shard_map/ppermute | solution.py:700
  140.0 28.5 %collective-permute-start.17 = (bf16[512,1152]{1,0:T(8,128)(2,1)S(1)}, bf16[512,1152]{1,0:T(8,128)(2,1)S(1)}, u32[]{:S(2)}, u32[]{:S(2)}) collective-permute-start(bf16[512,1152]{1,0:T(8,128)(2,1)S(1)} %get-tuple-element.114.rows0), channel_id=1, source_target_pairs={{0,1},{1,0},{2,3},{3,2},{4,5},{5,4},{6,7},{7,6},{8,9},{9,8},{10,11... | collective-permute-start | bytes 3538952 | tf_op jit(solution)/shard_map/ppermute | solution.py:679
  141.4 3.5 collective-permute-start.15
  168.5 2.8 collective-permute-start.18
  193.7 4.1 collective-permute-start.20
  193.7 5.3 %collective-permute-start.21 = (bf16[512,1152]{1,0:T(8,128)(2,1)}, bf16[512,1152]{1,0:T(8,128)(2,1)S(1)}, u32[]{:S(2)}, u32[]{:S(2)}) collective-permute-start(bf16[512,1152]{1,0:T(8,128)(2,1)} %get-tuple-element.130), channel_id=1, source_target_pairs={{0,4},{1,5},{2,6},{3,7},{4,0},{5,1},{6,2},{7,3},{8,12},{9,13},{10,... | collective-permute-start | bytes 3538952 | tf_op jit(solution)/shard_map/ppermute | solution.py:679
  216.6 3.1 collective-permute-start.24
  216.7 11.4 %collective-permute-start.26 = (bf16[1152,1152]{1,0:T(8,128)(2,1)S(1)}, bf16[1152,1152]{1,0:T(8,128)(2,1)S(1)}, u32[]{:S(2)}, u32[]{:S(2)}) collective-permute-start(bf16[1152,1152]{1,0:T(8,128)(2,1)S(1)} %convolution_add_fusion.1), channel_id=1, source_target_pairs={{4,6},{5,7},{6,4},{7,5},{12,14},{13,15},{14,12},{15,13},{20,22},{2... | collective-permute-start | bytes 7962632 | tf_op jit(solution)/shard_map/ppermute | solution.py:700
  229.8 177.3 %reduce-scatter.4.cloned.1.call-start = ((), (), s32[]{:S(2)}) async-start(), calls=%async_computation.6 | async-start | bytes 2985984 | tf_op jit(solution)/shard_map/reduce_scatter | solution.py:858
  231.1 16.2 %collective-permute-start.25 = (bf16[512,1152]{1,0:T(8,128)(2,1)S(1)}, bf16[512,1152]{1,0:T(8,128)(2,1)S(1)}, u32[]{:S(2)}, u32[]{:S(2)}) collective-permute-start(bf16[512,1152]{1,0:T(8,128)(2,1)S(1)} %copy-done.21), channel_id=1, source_target_pairs={{0,1},{1,0},{2,3},{3,2},{4,5},{5,4},{6,7},{7,6},{8,9},{9,8},{10,11... | collective-permute-start | bytes 3538952 | tf_op jit(solution)/shard_map/ppermute | solution.py:679
  232.5 70.7 %collective-permute-start.28 = (bf16[1152,1152]{1,0:T(8,128)(2,1)}, bf16[1152,1152]{1,0:T(8,128)(2,1)S(1)}, u32[]{:S(2)}, u32[]{:S(2)}) collective-permute-start(bf16[1152,1152]{1,0:T(8,128)(2,1)} %fusion), channel_id=1, source_target_pairs={{4,6},{5,7},{6,4},{7,5},{12,14},{13,15},{14,12},{15,13},{20,22},{2... | collective-permute-start | bytes 7962632 | tf_op jit(solution)/shard_map/ppermute | solution.py:700
  255.2 24.0 %collective-permute-start.27 = (bf16[512,1152]{1,0:T(8,128)(2,1)}, bf16[512,1152]{1,0:T(8,128)(2,1)S(1)}, u32[]{:S(2)}, u32[]{:S(2)}) collective-permute-start(bf16[512,1152]{1,0:T(8,128)(2,1)} %get-tuple-element.144.own_ref), channel_id=1, source_target_pairs={{0,4},{1,5},{2,6},{3,7},{4,0},{5,1},{6,2},{7,3},{8,12},{9,13},{10,... | collective-permute-start | bytes 3538952 | tf_op jit(solution)/shard_map/ppermute | solution.py:679
  305.1 103.9 %reduce-scatter.8.cloned.1.call-start = ((), (), s32[]{:S(2)}) async-start(), calls=%async_computation.8 | async-start | bytes 1843200 | tf_op jit(solution)/shard_map/reduce_scatter | solution.py:907
  305.3 19.6 %collective-permute-start.29 = (bf16[1152,640]{1,0:T(8,128)(2,1)}, bf16[1152,640]{1,0:T(8,128)(2,1)S(1)}, u32[]{:S(2)}, u32[]{:S(2)}) collective-permute-start(bf16[1152,640]{1,0:T(8,128)(2,1)} %get-tuple-element.154), channel_id=1, source_target_pairs={{0,2},{1,3},{2,0},{3,1},{4,5},{5,4},{6,7},{7,6},{8,10},{9,11},{10,... | collective-permute-start | bytes 4423688 | tf_op jit(solution)/shard_map/ppermute | solution.py:679
  306.9 41.9 %collective-permute-start.30 = (bf16[1152,640]{1,0:T(8,128)(2,1)S(1)}, bf16[1152,640]{1,0:T(8,128)(2,1)S(1)}, u32[]{:S(2)}, u32[]{:S(2)}) collective-permute-start(bf16[1152,640]{1,0:T(8,128)(2,1)S(1)} %get-tuple-element.156), channel_id=1, source_target_pairs={{0,2},{1,3},{2,0},{3,1},{4,5},{5,4},{6,7},{7,6},{8,10},{9,11},{10,... | collective-permute-start | bytes 4423688 | tf_op jit(solution)/shard_map/ppermute | solution.py:679
  337.4 32.3 %collective-permute-start.31 = (bf16[1152,640]{1,0:T(8,128)(2,1)}, bf16[1152,640]{1,0:T(8,128)(2,1)}, u32[]{:S(2)}, u32[]{:S(2)}) collective-permute-start(bf16[1152,640]{1,0:T(8,128)(2,1)} %get-tuple-element.159), channel_id=1, source_target_pairs={{0,1},{1,0},{2,3},{3,2},{4,6},{5,7},{6,4},{7,5},{8,9},{9,8},{10,11... | collective-permute-start | bytes 4423688 | tf_op jit(solution)/shard_map/ppermute | solution.py:679
  339.5 42.9 %collective-permute-start.23 = (bf16[512,1152]{1,0:T(8,128)(2,1)}, bf16[512,1152]{1,0:T(8,128)(2,1)}, u32[]{:S(2)}, u32[]{:S(2)}) collective-permute-start(bf16[512,1152]{1,0:T(8,128)(2,1)} %add_convert_fusion.1), channel_id=1, source_target_pairs={{0,1},{1,0},{2,3},{3,2},{4,5},{5,4},{6,7},{7,6},{8,9},{9,8},{10,11... | collective-permute-start | bytes 3538952 | tf_op jit(solution)/shard_map/ppermute | solution.py:679
  340.1 42.2 %collective-permute-start.22 = (bf16[512,1152]{1,0:T(8,128)(2,1)}, bf16[512,1152]{1,0:T(8,128)(2,1)}, u32[]{:S(2)}, u32[]{:S(2)}) collective-permute-start(bf16[512,1152]{1,0:T(8,128)(2,1)} %get-tuple-element.134), channel_id=1, source_target_pairs={{0,4},{1,5},{2,6},{3,7},{4,0},{5,1},{6,2},{7,3},{8,12},{9,13},{10,... | collective-permute-start | bytes 3538952 | tf_op jit(solution)/shard_map/ppermute | solution.py:679
  381.0 5.5 %collective-permute-start.32 = (bf16[512,1152]{1,0:T(8,128)(2,1)}, bf16[512,1152]{1,0:T(8,128)(2,1)S(1)}, u32[]{:S(2)}, u32[]{:S(2)}) collective-permute-start(bf16[512,1152]{1,0:T(8,128)(2,1)} %get-tuple-element.174), channel_id=1, source_target_pairs={{0,4},{1,5},{2,6},{3,7},{4,0},{5,1},{6,2},{7,3},{8,12},{9,13},{10,... | collective-permute-start | bytes 3538952 | tf_op jit(solution)/shard_map/ppermute | solution.py:679
  395.3 6.2 %collective-permute-start.35 = (f32[16,1152]{1,0:T(8,128)}, f32[16,1152]{1,0:T(8,128)S(1)}, u32[]{:S(2)}, u32[]{:S(2)}) collective-permute-start(f32[16,1152]{1,0:T(8,128)} %pack_small.1), channel_id=1, source_target_pairs={{0,3},{1,2},{2,1},{3,0},{4,7},{5,6},{6,5},{7,4},{8,11},{9,10},{10,... | collective-permute-start | bytes 221192 | tf_op jit(solution)/shard_map/ppermute | solution.py:679
  397.2 4.8 %collective-permute-start.34 = (f32[16,1152]{1,0:T(8,128)}, f32[16,1152]{1,0:T(8,128)S(1)}, u32[]{:S(2)}, u32[]{:S(2)}) collective-permute-start(f32[16,1152]{1,0:T(8,128)} %pack_small.1), channel_id=1, source_target_pairs={{0,2},{1,3},{2,0},{3,1},{4,6},{5,7},{6,4},{7,5},{8,10},{9,11},{10,... | collective-permute-start | bytes 221192 | tf_op jit(solution)/shard_map/ppermute | solution.py:679
  398.2 4.6 %collective-permute-start.33 = (f32[16,1152]{1,0:T(8,128)}, f32[16,1152]{1,0:T(8,128)S(1)}, u32[]{:S(2)}, u32[]{:S(2)}) collective-permute-start(f32[16,1152]{1,0:T(8,128)} %pack_small.1), channel_id=1, source_target_pairs={{0,1},{1,0},{2,3},{3,2},{4,5},{5,4},{6,7},{7,6},{8,9},{9,8},{10,11... | collective-permute-start | bytes 221192 | tf_op jit(solution)/shard_map/ppermute | solution.py:679
  403.7 6.4 %collective-permute-start.38 = (f32[16,1152]{1,0:T(8,128)S(1)}, f32[16,1152]{1,0:T(8,128)S(1)}, u32[]{:S(2)}, u32[]{:S(2)}) collective-permute-start(f32[16,1152]{1,0:T(8,128)S(1)} %add_add_fusion.2), channel_id=1, source_target_pairs={{0,24},{1,25},{2,26},{3,27},{4,28},{5,29},{6,30},{7,31},{8,0},{9,1... | collective-permute-start | bytes 221192 | tf_op jit(solution)/shard_map/ppermute | solution.py:679
  405.2 7.2 %collective-permute-start.37 = (f32[16,1152]{1,0:T(8,128)S(1)}, f32[16,1152]{1,0:T(8,128)S(1)}, u32[]{:S(2)}, u32[]{:S(2)}) collective-permute-start(f32[16,1152]{1,0:T(8,128)S(1)} %add_add_fusion.2), channel_id=1, source_target_pairs={{0,16},{1,17},{2,18},{3,19},{4,20},{5,21},{6,22},{7,23},{8,24},{9,... | collective-permute-start | bytes 221192 | tf_op jit(solution)/shard_map/ppermute | solution.py:679
  405.9 6.5 %collective-permute-start.36 = (f32[16,1152]{1,0:T(8,128)S(1)}, f32[16,1152]{1,0:T(8,128)S(1)}, u32[]{:S(2)}, u32[]{:S(2)}) collective-permute-start(f32[16,1152]{1,0:T(8,128)S(1)} %add_add_fusion.2), channel_id=1, source_target_pairs={{0,8},{1,9},{2,10},{3,11},{4,12},{5,13},{6,14},{7,15},{8,16},{9,17... | collective-permute-start | bytes 221192 | tf_op jit(solution)/shard_map/ppermute | solution.py:679
  410.0 2.4 collective-permute-start.39
  415.9 1.3 collective-permute-start.40
  (40 other events, 235.4 us)
Sparse Core Ops, SparseCore 0:
  11.0 39.4 all-gather.3
  52.6 32.8 all-gather.5
  87.2 33.0 all-gather.7
  230.0 58.6 reduce-scatter.5
  305.2 36.9 reduce-scatter.3
  372.9 32.4 reduce-scatter.7

commit v3 on v2

--- a/solution.py
+++ b/solution.py
@@ -97,10 +97,11 @@
 
 
 def attend_kernel(cols, images, before, rows_ref, w_ref, scale_ref, bias_ref, *refs):
-    lefts, rights, outs = refs[:before], refs[before : 3 * before], refs[3 * before :]
+    lefts, rights = refs[:before], refs[before : 3 * before + 2]
+    outs = refs[3 * before + 2 :] if before else refs
     qkv_ref, mixed_ref, lse_ref = outs[:3]
     heads, hh = cols.heads, cols.hh
-    proj = dot_nn(rows_ref[...], w_ref[...])[:, : cols.three]
+    proj = dot_nn(rows_ref[...], w_ref[...])
     qkv = ((proj + bias_ref[...]) * scale_ref[...]).astype(BF16)
     qkv_ref[...] = qkv
     units = [(m, h) for m in range(images) for h in range(heads)]
@@ -127,8 +128,8 @@
     if len(outs) == 3:
         return
     mine_ref, other_ref = outs[3:]
-    total = dot_nt(mixed_ref[...], w_ref[:, cols.low :])
-    for n, left in enumerate(lefts):
+    total = 0.0
+    for n, left in enumerate([*lefts, mixed_ref]):
         right = jnp.concatenate([rights[2 * n][...], rights[2 * n + 1][...]], axis=1)
         total += dot_nt(left[...], right)
     value = total.astype(BF16)
@@ -152,7 +153,7 @@
     whole = lambda i: (0, 0)
     block = cols.low // LANES
     assert not last or cols.window == 2 * LANES
-    rights = [w for weight in weights for w in (weight, weight)]
+    rights = [w for w in [*weights, weight] for _ in range(2)] if last else []
     out_specs = [
         pl.BlockSpec((tile, cols.three), turn),
         pl.BlockSpec((tile, cols.window), turn),
@@ -171,15 +172,14 @@
         grid=(2,),
         in_specs=[
             pl.BlockSpec((tile, width), turn),
-            pl.BlockSpec(weight.shape, whole),
+            pl.BlockSpec((width, cols.three), whole),
             pl.BlockSpec(scale.shape, whole),
             pl.BlockSpec(bias.shape, whole),
         ]
         + [pl.BlockSpec((tile, cols.window), turn)] * len(mixeds)
         + [
-            pl.BlockSpec((width, LANES), lambda i, j=j: (0, block + j))
-            for _ in weights
-            for j in range(2)
+            pl.BlockSpec((width, LANES), lambda i, j=n % 2: (0, block + j))
+            for n in range(len(rights))
         ],
         out_specs=out_specs,
         out_shape=out_shape,
@@ -194,7 +194,8 @@
 
 
 def attend_back_kernel(
-    cols, images, extras, own_ref, other_hbm, rows_ref, w_ref, qkv_ref, mixed_ref, lse_ref, *refs
+    cols, images, extras, own_ref, other_hbm, rows_ref, w0_ref, w1_ref, qkv_ref, mixed_ref,
+    lse_ref, *refs
 ):
     extra_hbm = refs[:extras]
     proj_ref, gw_ref, sums_ref, acc, grad, other, sems = refs[extras : extras + 7]
@@ -218,7 +219,7 @@
         grad[...] = other[...]
 
     gh = grad[...]
-    gmix = dot_nn(gh, w_ref[:, cols.low :]).astype(BF16)
+    gmix = dot_nn(gh, jnp.concatenate([w0_ref[...], w1_ref[...]], axis=1)).astype(BF16)
     units = [(m, h) for m in range(images) for h in range(heads)]
 
     def unit(kind, m, h):
@@ -282,6 +283,8 @@
     step = lambda i: (i, 0)
     whole = lambda i: (0, 0)
     lanes = cols.heads * LANES
+    block = cols.low // LANES
+    assert cols.window == 2 * LANES
     anywhere = pl.BlockSpec(memory_space=pl.ANY)
     own, other = grad_rows
     return pl.pallas_call(
@@ -291,7 +294,8 @@
             pl.BlockSpec((tile, width), whole),
             anywhere,
             pl.BlockSpec((tile, width), step),
-            pl.BlockSpec(weight.shape, whole),
+            pl.BlockSpec((width, LANES), lambda i: (0, block)),
+            pl.BlockSpec((width, LANES), lambda i: (0, block + 1)),
             pl.BlockSpec((tile, cols.three), step),
             pl.BlockSpec((tile, cols.window), step),
             pl.BlockSpec((tile, LANES), step),
@@ -304,7 +308,7 @@
         ],
         out_shape=[
             pltpu.HBM((total, cols.three), BF16),
-            jax.ShapeDtypeStruct(weight.shape, BF16),
+            pltpu.HBM(weight.shape, BF16),
             jax.ShapeDtypeStruct((2, lanes), F32),
         ],
         scratch_shapes=[
@@ -321,15 +325,18 @@
             transcendentals=total * SEQ * cols.heads,
         ),
         name="attend_back",
-    )(far(own), far(other), far(rows), far(weight), far(qkv), far(mixed), far(lse), *extra)
-
-
-def sum_nt_kernel(count, inner, *refs):
+    )(
+        far(own), far(other), far(rows), far(weight), far(weight), far(qkv), far(mixed), far(lse),
+        *map(far, extra),
+    )
+
+
+def sum_nt_kernel(count, *refs):
     lefts, rights = refs[:count], refs[count : 2 * count]
     before, (mine_ref, other_ref) = refs[2 * count : -2], refs[-2:]
-    total = dot_nt(lefts[0][...], rights[0][:, :inner])
+    total = dot_nt(lefts[0][...], rights[0][...])
     for left, right in zip(lefts[1:], rights[1:]):
-        total += dot_nt(left[...], right[:, :inner])
+        total += dot_nt(left[...], right[...])
     half = pl.num_programs(0) // 2
 
     def store(target, source):
@@ -355,10 +362,13 @@
         pl.BlockSpec((tile, width), lambda i: (jnp.minimum(i, half - 1), 0)),
     ]
     return pl.pallas_call(
-        functools.partial(sum_nt_kernel, count, inner),
+        functools.partial(sum_nt_kernel, count),
         grid=(2 * half,),
         in_specs=[pl.BlockSpec((tile, inner), lambda i: (lax.rem(i + half, 2 * half), 0))] * count
-        + [pl.BlockSpec(r.shape, lambda i: (0, 0), pipeline_mode=pl.Buffered(1)) for r in rights]
+        + [
+            pl.BlockSpec((width, inner), lambda i: (0, 0), pipeline_mode=pl.Buffered(1))
+        ]
+        * count
         + rows_specs[: len(before)],
         out_specs=rows_specs,
         out_shape=[
@@ -531,7 +541,7 @@
             pl.BlockSpec((1, ff), lambda i: (0, 0)),
         ],
         out_shape=[jax.ShapeDtypeStruct((2 * count, ff), BF16)]
-        + [pltpu.HBM((count, width), BF16)] * 4
+        + [jax.ShapeDtypeStruct((count, width), BF16)] * 4
         + [jax.ShapeDtypeStruct((1, ff), F32)],
         scratch_shapes=[pltpu.VMEM((width, ff), BF16), pltpu.SemaphoreType.DMA((1,))],
         compiler_params=pltpu.CompilerParams(vmem_limit_bytes=FEED_OUT_VMEM),
@@ -589,7 +599,7 @@
             transcendentals=count,
         ),
         name="norm_back",
-    )(*map(far, grads), far(rows), far(cot), gain)
+    )(*grads, far(rows), far(cot), gain)
 
 
 def norm_kernel(count, *refs):
@@ -874,6 +884,7 @@
         )
         hidden_pair = (hidden_in, swap_core(hidden_in))
         back, after = {}, None
+        no_sum = jnp.zeros(attn_w[0].shape, BF16)
         grad_w = [None] * nt
         got_w = {}
         for p in reversed(range(nt)):
@@ -881,7 +892,7 @@
             if after is not None:
                 lse = tie(lse, *after)
             come = sorted((q for q in got_w if got_w[q][0] == p and (p or q > 1)), reverse=True)
-            extra = [got_w[q][1] for q in come]
+            extra = [got_w[q][1] for q in come] or [no_sum]
             back[p] = attend_back(cols, hidden_pair, first_chip, attn_w[p], qkv, mix, lse, extra)
             value = back[p][1]
             grad_w[p] = value
@@ -926,7 +937,6 @@
         grad_tokens, first_sums = norm_back_rows(
             [first_mine, swap_core(first_other)], tokens, grad_hidden, gain_rows[0], False
         )
-        output = hidden_one + tie(mlp_out, grad_w[0]) + shifts[3]
 
         spots = [by_core(t ^ p, t ^ reverse_bits(p)) for p in range(nt)]
         where = jnp.stack([c, by_core(t, t ^ top)] + spots).astype(jnp.int32)
@@ -937,8 +947,9 @@
             grad_fc1_bias,
             nt,
         )
+        output = hidden_one + tie(mlp_out, total) + shifts[3]
         total = functools.reduce(jnp.add, [swap_tensor(total, i) for i in range(1, nt)], total)
-        total = tie(total, grad_tokens)
+        total = tie(total, grad_tokens, output)
         total = functools.reduce(jnp.add, [shift_z(total, k) for k in range(1, nz)], total)
         total = tie(total, output, grad_fc1_own, grad_fc2_own, grad_qkv_own, grad_out_own)
         total = total + swap_core(total)

time: 433 us -> 431 us (level)
  other arithmetic: 28.9 us -> 34.7 us
  Pallas kernels: 150 us -> 145 us
  matrix products: 15 us -> 19.9 us
    ppermute x37, waiting for transfers between devices: 122 us -> 117 us  [send(): return lax.ppermute(value, AXES, perm(move))]
    dot_general x4, matrix products: 15 us -> 19.9 us  [dot_tn(): lax.dot_general(a, b, (((0,), (0,)), ((), ())), preferred_element_type=F32)]
    unnamed x84 -> x80, local copies, waits for them, and re-layouts: 15.3 us -> 11.5 us
  transfers between devices with their start and end apart: 47 -> 47, of which waited for: 23 -> 20; matrix products, arithmetic and copies ran while one was open for 11% -> 14% of each run, Pallas kernels for 27% -> 27%
where the time goes in v3:
time: 431 us; the launch traced here: 425 us
  Pallas kernels  145 us (34%)
  waiting for transfers between devices  122 us (28%)
  starting transfers between devices  60.8 us (14%)
  other arithmetic  34.7 us (8%)
  local copies, waits for them, and re-layouts  27.4 us (6%)
  matrix products  19.9 us (5%)
  between operations  15.2 us (4%)
    ppermute x37, waiting for transfers between devices, send(): return lax.ppermute(value, AXES, perm(move))  117 us
    ppermute x37, starting transfers between devices, send(): return lax.ppermute(value, AXES, perm(move))  54.9 us
    pallas_call x4, Pallas kernels, attend_back(): pl.pallas_call(functools.partial(attend_back_kernel, cols, images, len(ex...  45.1 us
    pallas_call x2, Pallas kernels, feed_out(): pl.pallas_call(functools.partial(feed_out_kernel, half), grid=(2 * half,)...  30.4 us
    pallas_call x4, Pallas kernels, attend(): pl.pallas_call(functools.partial(attend_kernel, cols, images, len(mixeds)...  28.5 us
    dot_general x4, matrix products, dot_tn(): lax.dot_general(a, b, (((0,), (0,)), ((), ())), preferred_element_type=F32)  19.9 us
    pallas_call x2, Pallas kernels, sum_nt(): pl.pallas_call(functools.partial(sum_nt_kernel, count), grid=(2 * half,),...  13.6 us
    unnamed x80, local copies, waits for them, and re-layouts  11.5 us
  transfers between devices with their start and end apart: 47, of which 20 were waited for; matrix products, arithmetic and copies ran while one was open for 14% of the time, Pallas kernels for 27%

profile of v3, /device:TPU:0, one launch (start us, length us, event | category | flops | bytes accessed | tf_op | source)
XLA Modules:
  0.0 424.7 jit_solution(6767508922243441526)
XLA Ops:
  11.3 3.9 collective-permute-start.2
  15.9 1.9 collective-permute-start.10
  21.3 2.6 collective-permute-start.4
  25.8 2.4 collective-permute-done.5
  36.1 7.1 %collective-permute-done.10.cot0 = bf16[512,1152]{1,0:T(8,128)(2,1)} collective-permute-done((bf16[512,1152]{1,0:T(8,128)(2,1)S(1)}, bf16[512,1152]{1,0:T(8,128)(2,1)}, u32[]{:S(2)}, u32[]{:S(2)}) %collective-permute-start.10) | collective-permute-done | bytes 1179680 | tf_op jit(solution)/shard_map/ppermute | solution.py:689
  43.2 2.9 pad_maximum_fusion.rows_ref
  46.1 4.4 %all-gather.4.cloned.1.call-done = bf16[2,1152,640]{2,1,0:T(8,128)(2,1)} async-done(((bf16[2,144,640]{2,1,0:T(8,128)(2,1)}), bf16[2,1152,640]{2,1,0:T(8,128)(2,1)}) %all-gather.4.cloned.1.call-update) | async-done | bytes 2949136 | tf_op jit(solution)/shard_map/all_gather | solution.py:753
  55.9 5.7 %attend.4 = (bf16[1024,512]{1,0:T(8,128)(2,1)}, bf16[1024,256]{1,0:T(8,128)(2,1)}, f32[1024,128]{1,0:T(8,128)}) custom-call(bf16[1024,1152]{1,0:T(8,128)(2,1)} %pad_maximum_fusion.rows_ref, bf16[1152,640]{1,0:T(8,128)(2,1)S(1)} %dynamic-slice_bitcast_fusion.w_ref.refs_3_.refs_4_.w0_ref.w1_ref, f32[1,512]{1,0:T(1,128)S(1)} %get-tuple-element.223.scale_ref, ...), custom_call_target="tpu_custom_call" | custom-call | flops 1778384896 | bytes 5013504 | tf_op jit(solution)/shard_map/attend/pallas_call | solution.py:170
  64.5 2.3 constant_dynamic-update-slice_fusion.2
  66.8 19.2 %collective-permute-done.8.w_ref.refs_5_.refs_6_.w0_ref.w1_ref.refs_2_ = bf16[1152,640]{1,0:T(8,128)(2,1)} collective-permute-done((bf16[1152,640]{1,0:T(8,128)(2,1)S(1)}, bf16[1152,640]{1,0:T(8,128)(2,1)}, u32[]{:S(2)}, u32[]{:S(2)}) %collective-permute-start.8) | collective-permute-done | bytes 1474592 | tf_op jit(solution)/shard_map/ppermute | solution.py:689
  86.0 2.3 collective-permute-start.12
  88.3 17.5 %collective-permute-done.12.w_ref.refs_9_.refs_10_.w0_ref.w1_ref.refs_3_ = bf16[1152,640]{1,0:T(8,128)(2,1)S(1)} collective-permute-done((bf16[1152,640]{1,0:T(8,128)(2,1)}, bf16[1152,640]{1,0:T(8,128)(2,1)S(1)}, u32[]{:S(2)}, u32[]{:S(2)}) %collective-permute-start.12) | collective-permute-done | bytes 1474592 | tf_op jit(solution)/shard_map/ppermute | solution.py:689
  105.8 2.4 collective-permute-start.16
  108.2 6.1 %attend.5 = (bf16[1024,512]{1,0:T(8,128)(2,1)}, bf16[1024,256]{1,0:T(8,128)(2,1)}, f32[1024,128]{1,0:T(8,128)}) custom-call(bf16[1024,1152]{1,0:T(8,128)(2,1)} %pad_maximum_fusion.rows_ref, bf16[1152,640]{1,0:T(8,128)(2,1)} %collective-permute-done.8.w_ref.refs_5_.refs_6_.w0_ref.w1_ref.refs_2_, f32[1,512]{1,0:T(1,128)S(1)} %get-tuple-element.223.scale_ref, ...), custom_call_target="tpu_custom_call" | custom-call | flops 1778384896 | bytes 5013504 | tf_op jit(solution)/shard_map/attend/pallas_call | solution.py:170
  114.2 6.1 %attend.6 = (bf16[1024,512]{1,0:T(8,128)(2,1)}, bf16[1024,256]{1,0:T(8,128)(2,1)}, f32[1024,128]{1,0:T(8,128)}) custom-call(bf16[1024,1152]{1,0:T(8,128)(2,1)} %pad_maximum_fusion.rows_ref, bf16[1152,640]{1,0:T(8,128)(2,1)} %collective-permute-done.13.w_ref.refs_7_.refs_8_.w0_ref.w1_ref.refs_2_, f32[1,512]{1,0:T(1,128)S(1)} %get-tuple-element.223.scale_ref, ...), custom_call_target="tpu_custom_call" | custom-call | flops 1778384896 | bytes 5013504 | tf_op jit(solution)/shard_map/attend/pallas_call | solution.py:170
  120.4 10.7 %attend.7 = (bf16[1024,512]{1,0:T(8,128)(2,1)}, bf16[1024,256]{1,0:T(8,128)(2,1)}, f32[1024,128]{1,0:T(8,128)}, bf16[512,1152]{1,0:T(8,128)(2,1)S(1)}, bf16[512,1152]{1,0:T(8,128)(2,1)}) custom-call(bf16[1024,1152]{1,0:T(8,128)(2,1)} %pad_maximum_fusion.rows_ref, bf16[1152,640]{1,0:T(8,128)(2,1)S(1)} %collective-permute-done.12.w_ref.refs_9_.refs_10_.w0_ref.w1_ref.refs_3_, ...), custom_call_target="tpu_custom_call" | custom-call | flops 1778384896 | bytes 5013504 | tf_op jit(solution)/shard_map/attend/pallas_call | solution.py:170
  133.1 2.0 collective-permute-done.14.refs_2_
  137.7 2.4 norm_sum.1
  143.1 2.0 collective-permute-done.15.rows1
  145.0 5.7 %feed_in.2 = (bf16[1024,1152]{1,0:T(8,128)(2,1)S(1)}, bf16[1024,1152]{1,0:T(8,128)(2,1)S(1)}, bf16[1024,1152]{1,0:T(8,128)(2,1)S(1)}) custom-call(bf16[512,1152]{1,0:T(8,128)(2,1)S(1)} %get-tuple-element.114.rows0, bf16[512,1152]{1,0:T(8,128)(2,1)S(1)} %collective-permute-done.15.rows1, bf16[1152,1152]{1,0:T(8,128)(2,1)S(1)} %broadcast_select_fusion.2.w1, ...), custom_call_target="tpu_custom_call" | custom-call | flops 2717908992 | bytes 12091392 | tf_op jit(solution)/shard_map/feed_in/pallas_call | solution.py:448
  150.8 5.7 %fusion.34 = f32[1152,1152]{1,0:T(8,128)} fusion(bf16[1024,1152]{1,0:T(8,128)(2,1)S(1)} %copy-done.28, bf16[1024,1152]{1,0:T(8,128)(2,1)S(1)} %get-tuple-element.116.act_ref), kind=kOutput, calls=%fused_computation.99 | convolution fusion | flops 2717908992 | bytes 10027008 | tf_op jit(solution)/shard_map/dot_general | solution.py:48
  156.5 12.0 %collective-permute-done.17.rows0 = bf16[512,1152]{1,0:T(8,128)(2,1)S(1)} collective-permute-done((bf16[512,1152]{1,0:T(8,128)(2,1)S(1)}, bf16[512,1152]{1,0:T(8,128)(2,1)S(1)}, u32[]{:S(2)}, u32[]{:S(2)}) %collective-permute-start.17) | collective-permute-done | bytes 1179680 | tf_op jit(solution)/shard_map/ppermute | solution.py:689
  168.7 2.6 collective-permute-done.18.rows1
  171.4 5.7 %feed_in.3 = (bf16[1024,1152]{1,0:T(8,128)(2,1)S(1)}, bf16[1024,1152]{1,0:T(8,128)(2,1)S(1)}, bf16[1024,1152]{1,0:T(8,128)(2,1)S(1)}) custom-call(bf16[512,1152]{1,0:T(8,128)(2,1)S(1)} %collective-permute-done.17.rows0, bf16[512,1152]{1,0:T(8,128)(2,1)S(1)} %collective-permute-done.18.rows1, bf16[1152,1152]{1,0:T(8,128)(2,1)S(1)} %broadcast_select_fusion.2.w1, ...), custom_call_target="tpu_custom_call" | custom-call | flops 2717908992 | bytes 12091392 | tf_op jit(solution)/shard_map/feed_in/pallas_call | solution.py:448
  177.1 15.1 %feed_out.2 = (bf16[1024,1152]{1,0:T(8,128)(2,1)S(1)}, bf16[512,1152]{1,0:T(8,128)(2,1)S(1)}, bf16[512,1152]{1,0:T(8,128)(2,1)S(1)}, bf16[512,1152]{1,0:T(8,128)...) custom-call(s32[1]{0:T(128)} %bitcast.21.core_ref, bf16[512,1152]{1,0:T(8,128)(2,1)} %collective-permute-done.10.cot0, ...), custom_call_target="tpu_custom_call" | custom-call | flops 8153726976 | bytes 19464192 | tf_op jit(solution)/shard_map/feed_out/pallas_call | solution.py:523
  192.8 5.8 %convolution_add_fusion.1 = bf16[1152,1152]{1,0:T(8,128)(2,1)S(1)} fusion(f32[1152,1152]{1,0:T(8,128)} %fusion.34, bf16[1024,1152]{1,0:T(8,128)(2,1)S(1)} %copy-done.26, bf16[1024,1152]{1,0:T(8,128)(2,1)S(1)} %get-tuple-element.126.act_ref), kind=kOutput, calls=%fused_computation.1 | convolution fusion | flops 2720563200 | bytes 12681216 | tf_op jit(solution)/shard_map/dot_general | solution.py:48
  201.3 15.3 %feed_out.3 = (bf16[1024,1152]{1,0:T(8,128)(2,1)S(1)}, bf16[512,1152]{1,0:T(8,128)(2,1)S(1)}, bf16[512,1152]{1,0:T(8,128)(2,1)}, bf16[512,1152]{1,0:T(8,128)(2,1...) custom-call(s32[1]{0:T(128)} %bitcast.21.core_ref, bf16[512,1152]{1,0:T(8,128)(2,1)S(1)} %copy-done.5, ...), custom_call_target="tpu_custom_call" | custom-call | flops 8153726976 | bytes 19464192 | tf_op jit(solution)/shard_map/feed_out/pallas_call | solution.py:523
  219.5 3.3 fusion.35
  222.9 5.1 %fusion = bf16[1152,1152]{1,0:T(8,128)(2,1)} fusion(f32[1152,1152]{1,0:T(8,128)S(1)} %fusion.35, bf16[1024,1152]{1,0:T(8,128)(2,1)S(1)} %get-tuple-element.137, bf16[1024,1152]{1,0:T(8,128)(2,1)S(1)} %get-tuple-element.138), kind=kOutput, calls=%fused_computation.2 | convolution fusion | flops 2720563200 | bytes 12681216 | tf_op jit(solution)/shard_map/dot_general | solution.py:48
  227.9 1.9 broadcast_select_fusion.1
  232.4 14.0 %collective-permute-done.25.refs_2_ = bf16[512,1152]{1,0:T(8,128)(2,1)S(1)} collective-permute-done((bf16[512,1152]{1,0:T(8,128)(2,1)}, bf16[512,1152]{1,0:T(8,128)(2,1)S(1)}, u32[]{:S(2)}, u32[]{:S(2)}) %collective-permute-start.25) | collective-permute-done | bytes 1179680 | tf_op jit(solution)/shard_map/ppermute | solution.py:689
  246.3 5.5 %norm_back.2 = (f32[512,1152]{1,0:T(8,128)}, bf16[512,1152]{1,0:T(8,128)(2,1)}, f32[8,1152]{1,0:T(8,128)S(1)}) custom-call(bf16[512,1152]{1,0:T(8,128)(2,1)S(1)} %get-tuple-element.135.refs_0_, bf16[512,1152]{1,0:T(8,128)(2,1)S(1)} %collective-permute-done.24.refs_1_, bf16[512,1152]{1,0:T(8,128)(2,1)S(1)} %collective-permute-done.25.refs_2_, ...), custom_call_target="tpu_custom_call" | custom-call | flops 17694720 | bytes 10616832 | tf_op jit(solution)/shard_map/norm_back/pallas_call | solution.py:585
  252.4 21.1 %collective-permute-start.27 = (bf16[512,1152]{1,0:T(8,128)(2,1)}, bf16[512,1152]{1,0:T(8,128)(2,1)S(1)}, u32[]{:S(2)}, u32[]{:S(2)}) collective-permute-start(bf16[512,1152]{1,0:T(8,128)(2,1)} %get-tuple-element.144.own_ref), channel_id=1, source_target_pairs={{0,4},{1,5},{2,6},{3,7},{4,0},{5,1},{6,2},{7,3},{8,12},{9,13},{10,... | collective-permute-start | bytes 3538952 | tf_op jit(solution)/shard_map/ppermute | solution.py:689
  273.5 2.8 collective-permute-done.27.other_hbm
  277.9 11.2 %attend_back.4 = (bf16[1024,512]{1,0:T(8,128)(2,1)}, bf16[1152,640]{1,0:T(8,128)(2,1)}, f32[2,256]{1,0:T(2,128)S(1)}) custom-call(bf16[512,1152]{1,0:T(8,128)(2,1)} %get-tuple-element.144.own_ref, bf16[512,1152]{1,0:T(8,128)(2,1)} %copy-done.21, bf16[1024,1152]{1,0:T(8,128)(2,1)} %pad_maximum_fusion.rows_ref, bf16[1152,640]{1,0:T(8,128)(2,1)} %copy-done.1, ...), custom_call_target="tpu_custom_call" | custom-call | flops 2785017856 | bytes 9732096 | tf_op jit(solution)/shard_map/attend_back/pallas_call | solution.py:290
  289.1 11.4 %attend_back.5 = (bf16[1024,512]{1,0:T(8,128)(2,1)}, bf16[1152,640]{1,0:T(8,128)(2,1)}, f32[2,256]{1,0:T(2,128)S(1)}) custom-call(bf16[512,1152]{1,0:T(8,128)(2,1)} %get-tuple-element.144.own_ref, bf16[512,1152]{1,0:T(8,128)(2,1)} %copy-done.21, bf16[1024,1152]{1,0:T(8,128)(2,1)} %pad_maximum_fusion.rows_ref, ...), custom_call_target="tpu_custom_call" | custom-call | flops 2785017856 | bytes 9732096 | tf_op jit(solution)/shard_map/attend_back/pallas_call | solution.py:290
  305.7 17.3 %collective-permute-done.29.refs_0_ = bf16[1152,640]{1,0:T(8,128)(2,1)S(1)} collective-permute-done((bf16[1152,640]{1,0:T(8,128)(2,1)S(1)}, bf16[1152,640]{1,0:T(8,128)(2,1)S(1)}, u32[]{:S(2)}, u32[]{:S(2)}) %collective-permute-start.29) | collective-permute-done | bytes 1474592 | tf_op jit(solution)/shard_map/ppermute | solution.py:689
  324.2 11.4 %attend_back.6 = (bf16[1024,512]{1,0:T(8,128)(2,1)}, bf16[1152,640]{1,0:T(8,128)(2,1)}, f32[2,256]{1,0:T(2,128)S(1)}) custom-call(bf16[512,1152]{1,0:T(8,128)(2,1)} %get-tuple-element.144.own_ref, bf16[512,1152]{1,0:T(8,128)(2,1)} %copy-done.21, bf16[1024,1152]{1,0:T(8,128)(2,1)} %pad_maximum_fusion.rows_ref, ...), custom_call_target="tpu_custom_call" | custom-call | flops 2785017856 | bytes 9732096 | tf_op jit(solution)/shard_map/attend_back/pallas_call | solution.py:290
  340.1 6.8 %sum_nt.2 = (bf16[512,1152]{1,0:T(8,128)(2,1)S(1)}, bf16[512,1152]{1,0:T(8,128)(2,1)}) custom-call(bf16[1024,512]{1,0:T(8,128)(2,1)} %get-tuple-element.162.refs_0_, bf16[1024,512]{1,0:T(8,128)(2,1)} %get-tuple-element.164.refs_1_, bf16[1152,640]{1,0:T(8,128)(2,1)} %collective-permute-done.13.w_ref.refs_7_.refs_8_.w0_ref.w1_ref.refs_2_, ...), custom_call_target="tpu_custom_call" | custom-call | flops 2415919104 | bytes 6815744 | tf_op jit(solution)/shard_map/sum_nt/pallas_call | solution.py:364
  346.8 11.1 %attend_back.7 = (bf16[1024,512]{1,0:T(8,128)(2,1)}, bf16[1152,640]{1,0:T(8,128)(2,1)}, f32[2,256]{1,0:T(2,128)S(1)}) custom-call(bf16[512,1152]{1,0:T(8,128)(2,1)} %get-tuple-element.144.own_ref, bf16[512,1152]{1,0:T(8,128)(2,1)} %copy-done.21, bf16[1024,1152]{1,0:T(8,128)(2,1)} %pad_maximum_fusion.rows_ref, bf16[1152,640]{1,0:T(8,128)(2,1)} %copy-done, ...), custom_call_target="tpu_custom_call" | custom-call | flops 2785017856 | bytes 9732096 | tf_op jit(solution)/shard_map/attend_back/pallas_call | solution.py:290
  358.6 9.9 %collective-permute-done.31 = bf16[1152,640]{1,0:T(8,128)(2,1)} collective-permute-done((bf16[1152,640]{1,0:T(8,128)(2,1)}, bf16[1152,640]{1,0:T(8,128)(2,1)}, u32[]{:S(2)}, u32[]{:S(2)}) %collective-permute-start.31) | collective-permute-done | bytes 1474592 | tf_op jit(solution)/shard_map/ppermute | solution.py:689
  368.5 3.4 add_convert_fusion
  373.1 6.9 %sum_nt.3 = (bf16[512,1152]{1,0:T(8,128)(2,1)S(1)}, bf16[512,1152]{1,0:T(8,128)(2,1)}) custom-call(bf16[1024,512]{1,0:T(8,128)(2,1)} %get-tuple-element.168.refs_0_, bf16[1024,512]{1,0:T(8,128)(2,1)} %get-tuple-element.170.refs_1_, bf16[1152,640]{1,0:T(8,128)(2,1)} %collective-permute-done.8.w_ref.refs_5_.refs_6_.w0_ref.w1_ref.refs_2_, ...), custom_call_target="tpu_custom_call" | custom-call | flops 2415919104 | bytes 6815744 | tf_op jit(solution)/shard_map/sum_nt/pallas_call | solution.py:364
  381.1 3.5 convert_add_fusion
  386.5 5.1 %norm_back.3 = (f32[512,1152]{1,0:T(8,128)}, f32[8,1152]{1,0:T(8,128)S(1)}) custom-call(bf16[512,1152]{1,0:T(8,128)(2,1)S(1)} %get-tuple-element.172.refs_0_, bf16[512,1152]{1,0:T(8,128)(2,1)S(1)} %collective-permute-done.32.refs_1_, bf16[512,1152]{1,0:T(8,128)(2,1)} %refs_2_.1, f32[512,1152]{1,0:T(8,128)} %get-tuple-element.174.refs_3_, ...), custom_call_target="tpu_custom_call" | custom-call | flops 17694720 | bytes 9437184 | tf_op jit(solution)/shard_map/norm_back/pallas_call | solution.py:585
  393.8 2.4 collective-permute-start.35
  397.3 4.0 add_add_fusion
  407.8 2.5 collective-permute-done.37
  (248 shorter events, 77.4 us)
Async XLA Ops:
  7.2 43.2 %all-gather.4.cloned.1.call-start = ((), (), s32[]{:S(2)}) async-start(), calls=%async_computation.3 | async-start | bytes 3317760 | tf_op jit(solution)/shard_map/all_gather | solution.py:753
  10.9 77.4 %all-gather.6.cloned.1.call-start = ((), (), s32[]{:S(2)}) async-start(), calls=%async_computation.4 | async-start | bytes 2985984 | tf_op jit(solution)/shard_map/all_gather | solution.py:807
  11.3 8.1 %collective-permute-start.2 = (f32[1868]{0:T(1024)S(1)}, f32[1868]{0:T(1024)S(1)}, u32[]{:S(2)}, u32[]{:S(2)}) collective-permute-start(f32[1868]{0:T(1024)S(1)} %concatenate.39), channel_id=1, source_target_pairs={{0,3},{1,2},{2,1},{3,0},{4,7},{5,6},{6,5},{7,4},{8,11},{9,10},{10,... | collective-permute-start | bytes 22424 | tf_op jit(solution)/shard_map/ppermute | solution.py:689
  15.2 4.2 collective-permute-start.1
  15.7 3.7 collective-permute-start
  15.9 27.3 %collective-permute-start.10 = (bf16[512,1152]{1,0:T(8,128)(2,1)S(1)}, bf16[512,1152]{1,0:T(8,128)(2,1)}, u32[]{:S(2)}, u32[]{:S(2)}) collective-permute-start(bf16[512,1152]{1,0:T(8,128)(2,1)S(1)} %copy-done.4), channel_id=1, source_target_pairs={{0,1},{1,0},{2,3},{3,2},{4,5},{5,4},{6,7},{7,6},{8,9},{9,8},{10,11... | collective-permute-start | bytes 3538952 | tf_op jit(solution)/shard_map/ppermute | solution.py:689
  18.6 113.5 %all-gather.8.cloned.1.call-start = ((), (), s32[]{:S(2)}) async-start(), calls=%async_computation.5 | async-start | bytes 2985984 | tf_op jit(solution)/shard_map/all_gather | solution.py:807
  19.7 5.6 %collective-permute-start.3 = (f32[4,216]{1,0:T(4,128)S(1)}, f32[4,216]{1,0:T(4,128)S(1)}, u32[]{:S(2)}, u32[]{:S(2)}) collective-permute-start(f32[4,216]{1,0:T(4,128)S(1)} %pad_maximum_fusion.8), channel_id=1, source_target_pairs={{0,8},{1,9},{2,10},{3,11},{4,12},{5,13},{6,14},{7,15},{8,16},{9,17... | collective-permute-start | bytes 10376 | tf_op jit(solution)/shard_map/ppermute | solution.py:689
  21.3 4.5 %collective-permute-start.4 = (f32[4,216]{1,0:T(4,128)S(1)}, f32[4,216]{1,0:T(4,128)S(1)}, u32[]{:S(2)}, u32[]{:S(2)}) collective-permute-start(f32[4,216]{1,0:T(4,128)S(1)} %pad_maximum_fusion.8), channel_id=1, source_target_pairs={{0,16},{1,17},{2,18},{3,19},{4,20},{5,21},{6,22},{7,23},{8,24},{9,... | collective-permute-start | bytes 10376 | tf_op jit(solution)/shard_map/ppermute | solution.py:689
  23.9 4.3 %collective-permute-start.5 = (f32[4,216]{1,0:T(4,128)S(1)}, f32[4,216]{1,0:T(4,128)S(1)}, u32[]{:S(2)}, u32[]{:S(2)}) collective-permute-start(f32[4,216]{1,0:T(4,128)S(1)} %pad_maximum_fusion.8), channel_id=1, source_target_pairs={{0,24},{1,25},{2,26},{3,27},{4,28},{5,29},{6,30},{7,31},{8,0},{9,1... | collective-permute-start | bytes 10376 | tf_op jit(solution)/shard_map/ppermute | solution.py:689
  28.2 1.2 collective-permute-start.6
  34.6 8.6 %collective-permute-start.7 = (bf16[512,1152]{1,0:T(8,128)(2,1)}, bf16[512,1152]{1,0:T(8,128)(2,1)S(1)}, u32[]{:S(2)}, u32[]{:S(2)}) collective-permute-start(bf16[512,1152]{1,0:T(8,128)(2,1)} %fusion.6), channel_id=1, source_target_pairs={{0,4},{1,5},{2,6},{3,7},{4,0},{5,1},{6,2},{7,3},{8,12},{9,13},{10,... | collective-permute-start | bytes 3538952 | tf_op jit(solution)/shard_map/ppermute | solution.py:689
  34.8 28.3 %collective-permute-start.9 = (bf16[512,1152]{1,0:T(8,128)(2,1)S(1)}, bf16[512,1152]{1,0:T(8,128)(2,1)}, u32[]{:S(2)}, u32[]{:S(2)}) collective-permute-start(bf16[512,1152]{1,0:T(8,128)(2,1)S(1)} %copy-done.4), channel_id=1, source_target_pairs={{0,4},{1,5},{2,6},{3,7},{4,0},{5,1},{6,2},{7,3},{8,12},{9,13},{10,... | collective-permute-start | bytes 3538952 | tf_op jit(solution)/shard_map/ppermute | solution.py:689
  43.2 21.3 %collective-permute-start.11 = (bf16[512,1152]{1,0:T(8,128)(2,1)}, bf16[512,1152]{1,0:T(8,128)(2,1)}, u32[]{:S(2)}, u32[]{:S(2)}) collective-permute-start(bf16[512,1152]{1,0:T(8,128)(2,1)} %collective-permute-done.10.cot0), channel_id=1, source_target_pairs={{0,4},{1,5},{2,6},{3,7},{4,0},{5,1},{6,2},{7,3},{8,12},{9,13},{10,... | collective-permute-start | bytes 3538952 | tf_op jit(solution)/shard_map/ppermute | solution.py:689
  52.0 68.3 %copy-start = (bf16[1152,640]{1,0:T(8,128)(2,1)}, bf16[1152,640]{1,0:T(8,128)(2,1)S(1)}, u32[]{:S(2)}) copy-start(bf16[1152,640]{1,0:T(8,128)(2,1)S(1)} %dynamic-slice_bitcast_fusion.w_ref.refs_3_.refs_4_.w0_ref.w1_ref) | copy-start | bytes 4423684
  52.0 34.0 %collective-permute-start.8 = (bf16[1152,640]{1,0:T(8,128)(2,1)S(1)}, bf16[1152,640]{1,0:T(8,128)(2,1)}, u32[]{:S(2)}, u32[]{:S(2)}) collective-permute-start(bf16[1152,640]{1,0:T(8,128)(2,1)S(1)} %dynamic-slice_bitcast_fusion.w_ref.refs_3_.refs_4_.w0_ref.w1_ref), channel_id=1, source_target_pairs={{0,1},{1,0},{2,3},{3,2},{4,6},{5,7},{6,4},{7,5},{8,9},{9,8},{10,11... | collective-permute-start | bytes 4423688 | tf_op jit(solution)/shard_map/ppermute | solution.py:689
  54.3 330.3 %reduce-scatter.6.cloned.1.call-start = ((), (), s32[]{:S(2)}) async-start(), calls=%async_computation.7 | async-start | bytes 2985984 | tf_op jit(solution)/shard_map/reduce_scatter | solution.py:868
  54.4 33.9 %collective-permute-start.13 = (bf16[1152,640]{1,0:T(8,128)(2,1)S(1)}, bf16[1152,640]{1,0:T(8,128)(2,1)}, u32[]{:S(2)}, u32[]{:S(2)}) collective-permute-start(bf16[1152,640]{1,0:T(8,128)(2,1)S(1)} %dynamic-slice_bitcast_fusion.w_ref.refs_3_.refs_4_.w0_ref.w1_ref), channel_id=1, source_target_pairs={{0,2},{1,3},{2,0},{3,1},{4,5},{5,4},{6,7},{7,6},{8,10},{9,11},{10,... | collective-permute-start | bytes 4423688 | tf_op jit(solution)/shard_map/ppermute | solution.py:689
  86.0 19.8 %collective-permute-start.12 = (bf16[1152,640]{1,0:T(8,128)(2,1)}, bf16[1152,640]{1,0:T(8,128)(2,1)S(1)}, u32[]{:S(2)}, u32[]{:S(2)}) collective-permute-start(bf16[1152,640]{1,0:T(8,128)(2,1)} %collective-permute-done.8.w_ref.refs_5_.refs_6_.w0_ref.w1_ref.refs_2_), channel_id=1, source_target_pairs={{0,2},{1,3},{2,0},{3,1},{4,5},{5,4},{6,7},{7,6},{8,10},{9,11},{10,... | collective-permute-start | bytes 4423688 | tf_op jit(solution)/shard_map/ppermute | solution.py:689
  105.8 36.7 %collective-permute-start.16 = (bf16[1152,1152]{1,0:T(8,128)(2,1)}, bf16[1152,1152]{1,0:T(8,128)(2,1)}, u32[]{:S(2)}, u32[]{:S(2)}) collective-permute-start(bf16[1152,1152]{1,0:T(8,128)(2,1)} %all-gather.6.cloned.1.call-done), channel_id=1, source_target_pairs={{4,6},{5,7},{6,4},{7,5},{12,14},{13,15},{14,12},{15,13},{20,22},{2... | collective-permute-start | bytes 7962632 | tf_op jit(solution)/shard_map/ppermute | solution.py:710
  132.1 3.1 collective-permute-start.14
  132.1 45.0 %collective-permute-start.19 = (bf16[1152,1152]{1,0:T(8,128)(2,1)}, bf16[1152,1152]{1,0:T(8,128)(2,1)S(1)}, u32[]{:S(2)}, u32[]{:S(2)}) collective-permute-start(bf16[1152,1152]{1,0:T(8,128)(2,1)} %all-gather.8.cloned.1.call-done.w2_own), channel_id=1, source_target_pairs={{4,6},{5,7},{6,4},{7,5},{12,14},{13,15},{14,12},{15,13},{20,22},{2... | collective-permute-start | bytes 7962632 | tf_op jit(solution)/shard_map/ppermute | solution.py:710
  140.1 28.5 %collective-permute-start.17 = (bf16[512,1152]{1,0:T(8,128)(2,1)S(1)}, bf16[512,1152]{1,0:T(8,128)(2,1)S(1)}, u32[]{:S(2)}, u32[]{:S(2)}) collective-permute-start(bf16[512,1152]{1,0:T(8,128)(2,1)S(1)} %get-tuple-element.114.rows0), channel_id=1, source_target_pairs={{0,1},{1,0},{2,3},{3,2},{4,5},{5,4},{6,7},{7,6},{8,9},{9,8},{10,11... | collective-permute-start | bytes 3538952 | tf_op jit(solution)/shard_map/ppermute | solution.py:689
  141.5 3.5 collective-permute-start.15
  168.5 2.8 collective-permute-start.18
  192.2 6.4 %collective-permute-start.20 = (bf16[512,1152]{1,0:T(8,128)(2,1)S(1)}, bf16[512,1152]{1,0:T(8,128)(2,1)S(1)}, u32[]{:S(2)}, u32[]{:S(2)}) collective-permute-start(bf16[512,1152]{1,0:T(8,128)(2,1)S(1)} %get-tuple-element.124), channel_id=1, source_target_pairs={{0,4},{1,5},{2,6},{3,7},{4,0},{5,1},{6,2},{7,3},{8,12},{9,13},{10,... | collective-permute-start | bytes 3538952 | tf_op jit(solution)/shard_map/ppermute | solution.py:689
  192.3 7.6 %collective-permute-start.21 = (bf16[512,1152]{1,0:T(8,128)(2,1)S(1)}, bf16[512,1152]{1,0:T(8,128)(2,1)S(1)}, u32[]{:S(2)}, u32[]{:S(2)}) collective-permute-start(bf16[512,1152]{1,0:T(8,128)(2,1)S(1)} %get-tuple-element.130), channel_id=1, source_target_pairs={{0,4},{1,5},{2,6},{3,7},{4,0},{5,1},{6,2},{7,3},{8,12},{9,13},{10,... | collective-permute-start | bytes 3538952 | tf_op jit(solution)/shard_map/ppermute | solution.py:689
  216.6 2.9 collective-permute-start.24
  216.7 11.2 %collective-permute-start.26 = (bf16[1152,1152]{1,0:T(8,128)(2,1)S(1)}, bf16[1152,1152]{1,0:T(8,128)(2,1)S(1)}, u32[]{:S(2)}, u32[]{:S(2)}) collective-permute-start(bf16[1152,1152]{1,0:T(8,128)(2,1)S(1)} %convolution_add_fusion.1), channel_id=1, source_target_pairs={{4,6},{5,7},{6,4},{7,5},{12,14},{13,15},{14,12},{15,13},{20,22},{2... | collective-permute-start | bytes 7962632 | tf_op jit(solution)/shard_map/ppermute | solution.py:710
  229.8 175.0 %reduce-scatter.4.cloned.1.call-start = ((), (), s32[]{:S(2)}) async-start(), calls=%async_computation.6 | async-start | bytes 2985984 | tf_op jit(solution)/shard_map/reduce_scatter | solution.py:868
  229.9 16.5 %collective-permute-start.25 = (bf16[512,1152]{1,0:T(8,128)(2,1)}, bf16[512,1152]{1,0:T(8,128)(2,1)S(1)}, u32[]{:S(2)}, u32[]{:S(2)}) collective-permute-start(bf16[512,1152]{1,0:T(8,128)(2,1)} %add_convert_fusion.2), channel_id=1, source_target_pairs={{0,1},{1,0},{2,3},{3,2},{4,5},{5,4},{6,7},{7,6},{8,9},{9,8},{10,11... | collective-permute-start | bytes 3538952 | tf_op jit(solution)/shard_map/ppermute | solution.py:689
  231.4 69.2 %collective-permute-start.28 = (bf16[1152,1152]{1,0:T(8,128)(2,1)}, bf16[1152,1152]{1,0:T(8,128)(2,1)S(1)}, u32[]{:S(2)}, u32[]{:S(2)}) collective-permute-start(bf16[1152,1152]{1,0:T(8,128)(2,1)} %fusion), channel_id=1, source_target_pairs={{4,6},{5,7},{6,4},{7,5},{12,14},{13,15},{14,12},{15,13},{20,22},{2... | collective-permute-start | bytes 7962632 | tf_op jit(solution)/shard_map/ppermute | solution.py:710
  252.4 23.9 %collective-permute-start.27 = (bf16[512,1152]{1,0:T(8,128)(2,1)}, bf16[512,1152]{1,0:T(8,128)(2,1)S(1)}, u32[]{:S(2)}, u32[]{:S(2)}) collective-permute-start(bf16[512,1152]{1,0:T(8,128)(2,1)} %get-tuple-element.144.own_ref), channel_id=1, source_target_pairs={{0,4},{1,5},{2,6},{3,7},{4,0},{5,1},{6,2},{7,3},{8,12},{9,13},{10,... | collective-permute-start | bytes 3538952 | tf_op jit(solution)/shard_map/ppermute | solution.py:689
  302.4 104.3 %reduce-scatter.8.cloned.1.call-start = ((), (), s32[]{:S(2)}) async-start(), calls=%async_computation.8 | async-start | bytes 1843200 | tf_op jit(solution)/shard_map/reduce_scatter | solution.py:918
  303.7 19.4 %collective-permute-start.29 = (bf16[1152,640]{1,0:T(8,128)(2,1)S(1)}, bf16[1152,640]{1,0:T(8,128)(2,1)S(1)}, u32[]{:S(2)}, u32[]{:S(2)}) collective-permute-start(bf16[1152,640]{1,0:T(8,128)(2,1)S(1)} %copy-done.37), channel_id=1, source_target_pairs={{0,2},{1,3},{2,0},{3,1},{4,5},{5,4},{6,7},{7,6},{8,10},{9,11},{10,... | collective-permute-start | bytes 4423688 | tf_op jit(solution)/shard_map/ppermute | solution.py:689
  305.2 41.7 %collective-permute-start.30 = (bf16[1152,640]{1,0:T(8,128)(2,1)}, bf16[1152,640]{1,0:T(8,128)(2,1)}, u32[]{:S(2)}, u32[]{:S(2)}) collective-permute-start(bf16[1152,640]{1,0:T(8,128)(2,1)} %get-tuple-element.154), channel_id=1, source_target_pairs={{0,2},{1,3},{2,0},{3,1},{4,5},{5,4},{6,7},{7,6},{8,10},{9,11},{10,... | collective-permute-start | bytes 4423688 | tf_op jit(solution)/shard_map/ppermute | solution.py:689
  336.2 32.3 %collective-permute-start.31 = (bf16[1152,640]{1,0:T(8,128)(2,1)}, bf16[1152,640]{1,0:T(8,128)(2,1)}, u32[]{:S(2)}, u32[]{:S(2)}) collective-permute-start(bf16[1152,640]{1,0:T(8,128)(2,1)} %get-tuple-element.160), channel_id=1, source_target_pairs={{0,1},{1,0},{2,3},{3,2},{4,6},{5,7},{6,4},{7,5},{8,9},{9,8},{10,11... | collective-permute-start | bytes 4423688 | tf_op jit(solution)/shard_map/ppermute | solution.py:689
  338.9 42.2 %collective-permute-start.23 = (bf16[512,1152]{1,0:T(8,128)(2,1)}, bf16[512,1152]{1,0:T(8,128)(2,1)}, u32[]{:S(2)}, u32[]{:S(2)}) collective-permute-start(bf16[512,1152]{1,0:T(8,128)(2,1)} %add_convert_fusion.1), channel_id=1, source_target_pairs={{0,1},{1,0},{2,3},{3,2},{4,5},{5,4},{6,7},{7,6},{8,9},{9,8},{10,11... | collective-permute-start | bytes 3538952 | tf_op jit(solution)/shard_map/ppermute | solution.py:689
  339.5 41.6 %collective-permute-start.22 = (bf16[512,1152]{1,0:T(8,128)(2,1)}, bf16[512,1152]{1,0:T(8,128)(2,1)}, u32[]{:S(2)}, u32[]{:S(2)}) collective-permute-start(bf16[512,1152]{1,0:T(8,128)(2,1)} %get-tuple-element.134), channel_id=1, source_target_pairs={{0,4},{1,5},{2,6},{3,7},{4,0},{5,1},{6,2},{7,3},{8,12},{9,13},{10,... | collective-permute-start | bytes 3538952 | tf_op jit(solution)/shard_map/ppermute | solution.py:689
  380.0 6.5 %collective-permute-start.32 = (bf16[512,1152]{1,0:T(8,128)(2,1)}, bf16[512,1152]{1,0:T(8,128)(2,1)S(1)}, u32[]{:S(2)}, u32[]{:S(2)}) collective-permute-start(bf16[512,1152]{1,0:T(8,128)(2,1)} %get-tuple-element.173), channel_id=1, source_target_pairs={{0,4},{1,5},{2,6},{3,7},{4,0},{5,1},{6,2},{7,3},{8,12},{9,13},{10,... | collective-permute-start | bytes 3538952 | tf_op jit(solution)/shard_map/ppermute | solution.py:689
  393.8 7.5 %collective-permute-start.35 = (f32[16,1152]{1,0:T(8,128)}, f32[16,1152]{1,0:T(8,128)S(1)}, u32[]{:S(2)}, u32[]{:S(2)}) collective-permute-start(f32[16,1152]{1,0:T(8,128)} %pack_small.1), channel_id=1, source_target_pairs={{0,3},{1,2},{2,1},{3,0},{4,7},{5,6},{6,5},{7,4},{8,11},{9,10},{10,... | collective-permute-start | bytes 221192 | tf_op jit(solution)/shard_map/ppermute | solution.py:689
  396.1 5.2 %collective-permute-start.34 = (f32[16,1152]{1,0:T(8,128)}, f32[16,1152]{1,0:T(8,128)S(1)}, u32[]{:S(2)}, u32[]{:S(2)}) collective-permute-start(f32[16,1152]{1,0:T(8,128)} %pack_small.1), channel_id=1, source_target_pairs={{0,2},{1,3},{2,0},{3,1},{4,6},{5,7},{6,4},{7,5},{8,10},{9,11},{10,... | collective-permute-start | bytes 221192 | tf_op jit(solution)/shard_map/ppermute | solution.py:689
  396.7 4.6 %collective-permute-start.33 = (f32[16,1152]{1,0:T(8,128)}, f32[16,1152]{1,0:T(8,128)S(1)}, u32[]{:S(2)}, u32[]{:S(2)}) collective-permute-start(f32[16,1152]{1,0:T(8,128)} %pack_small.1), channel_id=1, source_target_pairs={{0,1},{1,0},{2,3},{3,2},{4,5},{5,4},{6,7},{7,6},{8,9},{9,8},{10,11... | collective-permute-start | bytes 221192 | tf_op jit(solution)/shard_map/ppermute | solution.py:689
  401.4 6.4 %collective-permute-start.38 = (f32[16,1152]{1,0:T(8,128)S(1)}, f32[16,1152]{1,0:T(8,128)S(1)}, u32[]{:S(2)}, u32[]{:S(2)}) collective-permute-start(f32[16,1152]{1,0:T(8,128)S(1)} %add_add_fusion.2), channel_id=1, source_target_pairs={{0,24},{1,25},{2,26},{3,27},{4,28},{5,29},{6,30},{7,31},{8,0},{9,1... | collective-permute-start | bytes 221192 | tf_op jit(solution)/shard_map/ppermute | solution.py:689
  402.9 7.4 %collective-permute-start.37 = (f32[16,1152]{1,0:T(8,128)S(1)}, f32[16,1152]{1,0:T(8,128)S(1)}, u32[]{:S(2)}, u32[]{:S(2)}) collective-permute-start(f32[16,1152]{1,0:T(8,128)S(1)} %add_add_fusion.2), channel_id=1, source_target_pairs={{0,16},{1,17},{2,18},{3,19},{4,20},{5,21},{6,22},{7,23},{8,24},{9,... | collective-permute-start | bytes 221192 | tf_op jit(solution)/shard_map/ppermute | solution.py:689
  403.6 6.6 %collective-permute-start.36 = (f32[16,1152]{1,0:T(8,128)S(1)}, f32[16,1152]{1,0:T(8,128)S(1)}, u32[]{:S(2)}, u32[]{:S(2)}) collective-permute-start(f32[16,1152]{1,0:T(8,128)S(1)} %add_add_fusion.2), channel_id=1, source_target_pairs={{0,8},{1,9},{2,10},{3,11},{4,12},{5,13},{6,14},{7,15},{8,16},{9,17... | collective-permute-start | bytes 221192 | tf_op jit(solution)/shard_map/ppermute | solution.py:689
  407.7 2.6 collective-permute-start.39
  413.8 1.3 collective-permute-start.40
  (38 other events, 277.0 us)
Sparse Core Ops, SparseCore 0:
  11.0 39.4 all-gather.3
  52.7 32.8 all-gather.5
  87.3 33.0 all-gather.7
  229.9 58.6 reduce-scatter.5
  302.5 37.2 reduce-scatter.3
  372.0 33.2 reduce-scatter.7

commit v4 on v3

--- a/solution.py
+++ b/solution.py
@@ -371,10 +371,7 @@
         * count
         + rows_specs[: len(before)],
         out_specs=rows_specs,
-        out_shape=[
-            jax.ShapeDtypeStruct((total // 2, width), BF16),
-            pltpu.HBM((total // 2, width), BF16),
-        ],
+        out_shape=[pltpu.HBM((total // 2, width), BF16)] * 2,
         compiler_params=pltpu.CompilerParams(vmem_limit_bytes=SUM_VMEM),
         cost_estimate=pl.CostEstimate(
             flops=2 * total * inner * width * count,
@@ -382,7 +379,7 @@
             transcendentals=0,
         ),
         name="sum_nt",
-    )(*map(far, lefts), *map(far, rights), *before)
+    )(*map(far, lefts), *map(far, rights), *map(far, before))
 
 
 def spread_kernel(count, in_ref, *out_refs):
@@ -797,10 +794,11 @@
         attn_w = [lax.dynamic_index_in_dim(tie(gathered, *early), c, 0, keepdims=False)]
         saved = [attend(cols, first_chip, attn_w[0], scale, unit_bias[0])]
         cot_rows = [jnp.concatenate([tie(g, saved[0][1]), o], axis=0) for g, o in cots]
+        no_sum = lax.optimization_barrier(jnp.zeros(attn_w[0].shape, BF16))
         for i in range(bits):
             sent = list(attn_w)
             if i:
-                sent[-1] = tie(sent[-1], *cot_rows)
+                sent[-1] = tie(sent[-1], *cot_rows, no_sum)
             attn_w = attn_w + [stage(b, i) for b in sent]
 
         def gather_ff(own):
@@ -866,10 +864,10 @@
 
         def scatter_ff(partial):
             own = lax.psum_scatter(partial, "dp", scatter_dimension=0, tiled=True)
-            return lax.optimization_barrier(own)[:, :ff].astype(F32)
+            return lax.optimization_barrier(own)
 
         grad_fc2_t = by_core(grad_fc2_t, tie(got_fc2, grad_fc1))
-        grad_fc2_own = scatter_ff(grad_fc2_t).T
+        sum_fc2 = scatter_ff(grad_fc2_t)
 
         grad_second = [grad_near, grad_sums[0]]
         for i in others:
@@ -884,7 +882,6 @@
         )
         hidden_pair = (hidden_in, swap_core(hidden_in))
         back, after = {}, None
-        no_sum = jnp.zeros(attn_w[0].shape, BF16)
         grad_w = [None] * nt
         got_w = {}
         for p in reversed(range(nt)):
@@ -905,7 +902,7 @@
                 after = [value, first_part[0]]
             if p == nt - 2:
                 grad_fc1 = by_core(grad_fc1, tie(got_fc1, value))
-                grad_fc1_own = scatter_ff(grad_fc1)
+                sum_fc1 = scatter_ff(grad_fc1)
                 after = [value, grad_fc1]
             if p == 0:
                 break
@@ -922,9 +919,10 @@
             axis_index_groups=[list(range(0, ndp, 2)), list(range(1, ndp, 2))],
             tiled=True,
         )
-        own_half = tie(own_half, grad_fc1_own, grad_fc2_own).reshape(2, part, packed)
+        own_half = own_half.reshape(2, part, packed)
+        sent_half = by_core(own_half[1], own_half[0])
         kept = by_core(own_half[0], own_half[1]).astype(F32)
-        got = swap_core(by_core(own_half[1], own_half[0])).astype(F32)
+        got = swap_core(sent_half).astype(F32)
         halves = [by_core(kept, got), by_core(got, kept)]
         grad_qkv_own = jnp.stack(
             [
@@ -950,6 +948,8 @@
         output = hidden_one + tie(mlp_out, total) + shifts[3]
         total = functools.reduce(jnp.add, [swap_tensor(total, i) for i in range(1, nt)], total)
         total = tie(total, grad_tokens, output)
+        grad_fc2_own = sum_fc2[:, :ff].astype(F32).T
+        grad_fc1_own = sum_fc1[:, :ff].astype(F32)
         total = functools.reduce(jnp.add, [shift_z(total, k) for k in range(1, nz)], total)
         total = tie(total, output, grad_fc1_own, grad_fc2_own, grad_qkv_own, grad_out_own)
         total = total + swap_core(total)

time: 431 us -> 439 us (1.019)
  waiting for transfers between devices: 122 us -> 130 us
    ppermute x37, waiting for transfers between devices: 117 us -> 126 us  [send(): return lax.ppermute(value, AXES, perm(move))]
    unnamed x80 -> x86, local copies, waits for them, and re-layouts: 11.5 us -> 10.2 us
  transfers between devices with their start and end apart: 47 -> 47, of which waited for: 20 -> 20; matrix products, arithmetic and copies ran while one was open for 14% -> 13% of each run, Pallas kernels for 27% -> 27%
where the time goes in v4:
time: 439 us; the launch traced here: 432 us
  Pallas kernels  145 us (33%)
  waiting for transfers between devices  130 us (30%)
  starting transfers between devices  61.6 us (14%)
  other arithmetic  34.1 us (8%)
  local copies, waits for them, and re-layouts  26 us (6%)
  matrix products  19.8 us (5%)
  between operations  15.2 us (3%)
    ppermute x37, waiting for transfers between devices, send(): return lax.ppermute(value, AXES, perm(move))  126 us
    ppermute x37, starting transfers between devices, send(): return lax.ppermute(value, AXES, perm(move))  55.7 us
    pallas_call x4, Pallas kernels, attend_back(): pl.pallas_call(functools.partial(attend_back_kernel, cols, images, len(ex...  45.1 us
    pallas_call x2, Pallas kernels, feed_out(): pl.pallas_call(functools.partial(feed_out_kernel, half), grid=(2 * half,)...  29.5 us
    pallas_call x4, Pallas kernels, attend(): pl.pallas_call(functools.partial(attend_kernel, cols, images, len(mixeds)...  28.5 us
    dot_general x4, matrix products, dot_tn(): lax.dot_general(a, b, (((0,), (0,)), ((), ())), preferred_element_type=F32)  19.8 us
    pallas_call x2, Pallas kernels, sum_nt(): pl.pallas_call(functools.partial(sum_nt_kernel, count), grid=(2 * half,),...  14.6 us
    pallas_call x2, Pallas kernels, feed_in(): pl.pallas_call(functools.partial(feed_in_kernel, half), grid=(2 * half,),...  11.5 us
  transfers between devices with their start and end apart: 47, of which 20 were waited for; matrix products, arithmetic and copies ran while one was open for 13% of the time, Pallas kernels for 27%

profile of v4, /device:TPU:0, one launch (start us, length us, event | category | flops | bytes accessed | tf_op | source)
XLA Modules:
  0.0 432.5 jit_solution(16578386371626758545)
XLA Ops:
  11.3 3.9 collective-permute-start.2
  15.9 1.9 collective-permute-start.10
  21.3 2.6 collective-permute-start.4
  25.8 2.4 collective-permute-done.5
  36.1 7.1 %collective-permute-done.10.cot0 = bf16[512,1152]{1,0:T(8,128)(2,1)} collective-permute-done((bf16[512,1152]{1,0:T(8,128)(2,1)S(1)}, bf16[512,1152]{1,0:T(8,128)(2,1)}, u32[]{:S(2)}, u32[]{:S(2)}) %collective-permute-start.10) | collective-permute-done | bytes 1179680 | tf_op jit(solution)/shard_map/ppermute | solution.py:686
  43.2 2.9 pad_maximum_fusion.rows_ref
  46.1 4.4 %all-gather.4.cloned.1.call-done = bf16[2,1152,640]{2,1,0:T(8,128)(2,1)} async-done(((bf16[2,144,640]{2,1,0:T(8,128)(2,1)}), bf16[2,1152,640]{2,1,0:T(8,128)(2,1)}) %all-gather.4.cloned.1.call-update) | async-done | bytes 2949136 | tf_op jit(solution)/shard_map/all_gather | solution.py:750
  55.9 5.7 %attend.4 = (bf16[1024,512]{1,0:T(8,128)(2,1)}, bf16[1024,256]{1,0:T(8,128)(2,1)}, f32[1024,128]{1,0:T(8,128)}) custom-call(bf16[1024,1152]{1,0:T(8,128)(2,1)} %pad_maximum_fusion.rows_ref, bf16[1152,640]{1,0:T(8,128)(2,1)S(1)} %dynamic-slice_bitcast_fusion.w_ref.refs_3_.refs_4_.w0_ref.w1_ref, f32[1,512]{1,0:T(1,128)S(1)} %get-tuple-element.221.scale_ref, ...), custom_call_target="tpu_custom_call" | custom-call | flops 1778384896 | bytes 5013504 | tf_op jit(solution)/shard_map/attend/pallas_call | solution.py:170
  64.5 2.3 constant_dynamic-update-slice_fusion.2
  66.8 19.2 %collective-permute-done.8.w_ref.refs_5_.refs_6_.w0_ref.w1_ref.refs_2_ = bf16[1152,640]{1,0:T(8,128)(2,1)} collective-permute-done((bf16[1152,640]{1,0:T(8,128)(2,1)S(1)}, bf16[1152,640]{1,0:T(8,128)(2,1)}, u32[]{:S(2)}, u32[]{:S(2)}) %collective-permute-start.8) | collective-permute-done | bytes 1474592 | tf_op jit(solution)/shard_map/ppermute | solution.py:686
  86.0 2.3 collective-permute-start.12
  88.3 17.5 %collective-permute-done.12.w_ref.refs_9_.refs_10_.w0_ref.w1_ref.refs_3_ = bf16[1152,640]{1,0:T(8,128)(2,1)S(1)} collective-permute-done((bf16[1152,640]{1,0:T(8,128)(2,1)}, bf16[1152,640]{1,0:T(8,128)(2,1)S(1)}, u32[]{:S(2)}, u32[]{:S(2)}) %collective-permute-start.12) | collective-permute-done | bytes 1474592 | tf_op jit(solution)/shard_map/ppermute | solution.py:686
  105.8 2.3 collective-permute-start.16
  108.1 6.1 %attend.5 = (bf16[1024,512]{1,0:T(8,128)(2,1)}, bf16[1024,256]{1,0:T(8,128)(2,1)}, f32[1024,128]{1,0:T(8,128)}) custom-call(bf16[1024,1152]{1,0:T(8,128)(2,1)} %pad_maximum_fusion.rows_ref, bf16[1152,640]{1,0:T(8,128)(2,1)} %collective-permute-done.8.w_ref.refs_5_.refs_6_.w0_ref.w1_ref.refs_2_, f32[1,512]{1,0:T(1,128)S(1)} %get-tuple-element.221.scale_ref, ...), custom_call_target="tpu_custom_call" | custom-call | flops 1778384896 | bytes 5013504 | tf_op jit(solution)/shard_map/attend/pallas_call | solution.py:170
  114.2 6.1 %attend.6 = (bf16[1024,512]{1,0:T(8,128)(2,1)}, bf16[1024,256]{1,0:T(8,128)(2,1)}, f32[1024,128]{1,0:T(8,128)}) custom-call(bf16[1024,1152]{1,0:T(8,128)(2,1)} %pad_maximum_fusion.rows_ref, bf16[1152,640]{1,0:T(8,128)(2,1)} %collective-permute-done.13.w_ref.refs_7_.refs_8_.w0_ref.w1_ref.refs_2_, f32[1,512]{1,0:T(1,128)S(1)} %get-tuple-element.221.scale_ref, ...), custom_call_target="tpu_custom_call" | custom-call | flops 1778384896 | bytes 5013504 | tf_op jit(solution)/shard_map/attend/pallas_call | solution.py:170
  120.3 10.7 %attend.7 = (bf16[1024,512]{1,0:T(8,128)(2,1)}, bf16[1024,256]{1,0:T(8,128)(2,1)}, f32[1024,128]{1,0:T(8,128)}, bf16[512,1152]{1,0:T(8,128)(2,1)S(1)}, bf16[512,1152]{1,0:T(8,128)(2,1)}) custom-call(bf16[1024,1152]{1,0:T(8,128)(2,1)} %pad_maximum_fusion.rows_ref, bf16[1152,640]{1,0:T(8,128)(2,1)S(1)} %collective-permute-done.12.w_ref.refs_9_.refs_10_.w0_ref.w1_ref.refs_3_, ...), custom_call_target="tpu_custom_call" | custom-call | flops 1778384896 | bytes 5013504 | tf_op jit(solution)/shard_map/attend/pallas_call | solution.py:170
  133.1 2.0 collective-permute-done.14.refs_2_
  137.6 2.4 norm_sum.1
  143.0 2.0 collective-permute-done.15.rows1
  145.0 5.7 %feed_in.2 = (bf16[1024,1152]{1,0:T(8,128)(2,1)S(1)}, bf16[1024,1152]{1,0:T(8,128)(2,1)S(1)}, bf16[1024,1152]{1,0:T(8,128)(2,1)S(1)}) custom-call(bf16[512,1152]{1,0:T(8,128)(2,1)S(1)} %get-tuple-element.113.rows0, bf16[512,1152]{1,0:T(8,128)(2,1)S(1)} %collective-permute-done.15.rows1, bf16[1152,1152]{1,0:T(8,128)(2,1)S(1)} %broadcast_select_fusion.2.w1, ...), custom_call_target="tpu_custom_call" | custom-call | flops 2717908992 | bytes 12091392 | tf_op jit(solution)/shard_map/feed_in/pallas_call | solution.py:445
  150.7 5.7 %fusion.34 = f32[1152,1152]{1,0:T(8,128)} fusion(bf16[1024,1152]{1,0:T(8,128)(2,1)S(1)} %copy-done.31, bf16[1024,1152]{1,0:T(8,128)(2,1)S(1)} %get-tuple-element.115.act_ref), kind=kOutput, calls=%fused_computation.99 | convolution fusion | flops 2717908992 | bytes 10027008 | tf_op jit(solution)/shard_map/dot_general | solution.py:48
  156.4 12.0 %collective-permute-done.17.rows0 = bf16[512,1152]{1,0:T(8,128)(2,1)S(1)} collective-permute-done((bf16[512,1152]{1,0:T(8,128)(2,1)S(1)}, bf16[512,1152]{1,0:T(8,128)(2,1)S(1)}, u32[]{:S(2)}, u32[]{:S(2)}) %collective-permute-start.17) | collective-permute-done | bytes 1179680 | tf_op jit(solution)/shard_map/ppermute | solution.py:686
  168.7 2.6 collective-permute-done.18.rows1
  171.3 5.7 %feed_in.3 = (bf16[1024,1152]{1,0:T(8,128)(2,1)S(1)}, bf16[1024,1152]{1,0:T(8,128)(2,1)S(1)}, bf16[1024,1152]{1,0:T(8,128)(2,1)S(1)}) custom-call(bf16[512,1152]{1,0:T(8,128)(2,1)S(1)} %collective-permute-done.17.rows0, bf16[512,1152]{1,0:T(8,128)(2,1)S(1)} %collective-permute-done.18.rows1, bf16[1152,1152]{1,0:T(8,128)(2,1)S(1)} %broadcast_select_fusion.2.w1, ...), custom_call_target="tpu_custom_call" | custom-call | flops 2717908992 | bytes 12091392 | tf_op jit(solution)/shard_map/feed_in/pallas_call | solution.py:445
  177.1 15.1 %feed_out.2 = (bf16[1024,1152]{1,0:T(8,128)(2,1)S(1)}, bf16[512,1152]{1,0:T(8,128)(2,1)S(1)}, bf16[512,1152]{1,0:T(8,128)(2,1)S(1)}, bf16[512,1152]{1,0:T(8,128)...) custom-call(s32[1]{0:T(128)} %bitcast.21.core_ref, bf16[512,1152]{1,0:T(8,128)(2,1)} %collective-permute-done.10.cot0, ...), custom_call_target="tpu_custom_call" | custom-call | flops 8153726976 | bytes 19464192 | tf_op jit(solution)/shard_map/feed_out/pallas_call | solution.py:520
  192.7 5.8 %convolution_add_fusion.1 = bf16[1152,1152]{1,0:T(8,128)(2,1)S(1)} fusion(f32[1152,1152]{1,0:T(8,128)} %fusion.34, bf16[1024,1152]{1,0:T(8,128)(2,1)S(1)} %copy-done.29, bf16[1024,1152]{1,0:T(8,128)(2,1)S(1)} %get-tuple-element.125.act_ref), kind=kOutput, calls=%fused_computation.1 | convolution fusion | flops 2720563200 | bytes 12681216 | tf_op jit(solution)/shard_map/dot_general | solution.py:48
  201.3 14.4 %feed_out.3 = (bf16[1024,1152]{1,0:T(8,128)(2,1)S(1)}, bf16[512,1152]{1,0:T(8,128)(2,1)S(1)}, bf16[512,1152]{1,0:T(8,128)(2,1)S(1)}, bf16[512,1152]{1,0:T(8,128)...) custom-call(s32[1]{0:T(128)} %bitcast.21.core_ref, bf16[512,1152]{1,0:T(8,128)(2,1)S(1)} %copy-done.5, ...), custom_call_target="tpu_custom_call" | custom-call | flops 8153726976 | bytes 19464192 | tf_op jit(solution)/shard_map/feed_out/pallas_call | solution.py:520
  218.7 3.3 fusion.35
  222.0 5.0 %fusion = bf16[1152,1152]{1,0:T(8,128)(2,1)} fusion(f32[1152,1152]{1,0:T(8,128)S(1)} %fusion.35, bf16[1024,1152]{1,0:T(8,128)(2,1)S(1)} %get-tuple-element.136, bf16[1024,1152]{1,0:T(8,128)(2,1)S(1)} %get-tuple-element.137), kind=kOutput, calls=%fused_computation.2 | convolution fusion | flops 2720563200 | bytes 12681216 | tf_op jit(solution)/shard_map/dot_general | solution.py:48
  227.0 1.9 broadcast_select_fusion.1
  231.5 14.0 %collective-permute-done.25.refs_2_ = bf16[512,1152]{1,0:T(8,128)(2,1)S(1)} collective-permute-done((bf16[512,1152]{1,0:T(8,128)(2,1)}, bf16[512,1152]{1,0:T(8,128)(2,1)S(1)}, u32[]{:S(2)}, u32[]{:S(2)}) %collective-permute-start.25) | collective-permute-done | bytes 1179680 | tf_op jit(solution)/shard_map/ppermute | solution.py:686
  245.5 5.5 %norm_back.2 = (f32[512,1152]{1,0:T(8,128)}, bf16[512,1152]{1,0:T(8,128)(2,1)}, f32[8,1152]{1,0:T(8,128)S(1)}) custom-call(bf16[512,1152]{1,0:T(8,128)(2,1)S(1)} %get-tuple-element.134.refs_0_, bf16[512,1152]{1,0:T(8,128)(2,1)S(1)} %collective-permute-done.24.refs_1_, bf16[512,1152]{1,0:T(8,128)(2,1)S(1)} %collective-permute-done.25.refs_2_, ...), custom_call_target="tpu_custom_call" | custom-call | flops 17694720 | bytes 10616832 | tf_op jit(solution)/shard_map/norm_back/pallas_call | solution.py:582
  251.6 21.2 %collective-permute-start.27 = (bf16[512,1152]{1,0:T(8,128)(2,1)}, bf16[512,1152]{1,0:T(8,128)(2,1)S(1)}, u32[]{:S(2)}, u32[]{:S(2)}) collective-permute-start(bf16[512,1152]{1,0:T(8,128)(2,1)} %get-tuple-element.143.own_ref), channel_id=1, source_target_pairs={{0,4},{1,5},{2,6},{3,7},{4,0},{5,1},{6,2},{7,3},{8,12},{9,13},{10,... | collective-permute-start | bytes 3538952 | tf_op jit(solution)/shard_map/ppermute | solution.py:686
  272.7 2.8 collective-permute-done.27.other_hbm
  277.1 11.1 %attend_back.4 = (bf16[1024,512]{1,0:T(8,128)(2,1)}, bf16[1152,640]{1,0:T(8,128)(2,1)}, f32[2,256]{1,0:T(2,128)S(1)}) custom-call(bf16[512,1152]{1,0:T(8,128)(2,1)} %get-tuple-element.143.own_ref, bf16[512,1152]{1,0:T(8,128)(2,1)} %copy-done.23, bf16[1024,1152]{1,0:T(8,128)(2,1)} %pad_maximum_fusion.rows_ref, bf16[1152,640]{1,0:T(8,128)(2,1)} %copy-done.1, ...), custom_call_target="tpu_custom_call" | custom-call | flops 2785017856 | bytes 9732096 | tf_op jit(solution)/shard_map/attend_back/pallas_call | solution.py:290
  288.3 11.2 %attend_back.5 = (bf16[1024,512]{1,0:T(8,128)(2,1)}, bf16[1152,640]{1,0:T(8,128)(2,1)}, f32[2,256]{1,0:T(2,128)S(1)}) custom-call(bf16[512,1152]{1,0:T(8,128)(2,1)} %get-tuple-element.143.own_ref, bf16[512,1152]{1,0:T(8,128)(2,1)} %copy-done.23, bf16[1024,1152]{1,0:T(8,128)(2,1)} %pad_maximum_fusion.rows_ref, ...), custom_call_target="tpu_custom_call" | custom-call | flops 2785017856 | bytes 9732096 | tf_op jit(solution)/shard_map/attend_back/pallas_call | solution.py:290
  304.8 17.3 %collective-permute-done.29.refs_0_ = bf16[1152,640]{1,0:T(8,128)(2,1)S(1)} collective-permute-done((bf16[1152,640]{1,0:T(8,128)(2,1)S(1)}, bf16[1152,640]{1,0:T(8,128)(2,1)S(1)}, u32[]{:S(2)}, u32[]{:S(2)}) %collective-permute-start.29) | collective-permute-done | bytes 1474592 | tf_op jit(solution)/shard_map/ppermute | solution.py:686
  323.2 11.6 %attend_back.6 = (bf16[1024,512]{1,0:T(8,128)(2,1)}, bf16[1152,640]{1,0:T(8,128)(2,1)}, f32[2,256]{1,0:T(2,128)S(1)}) custom-call(bf16[512,1152]{1,0:T(8,128)(2,1)} %get-tuple-element.143.own_ref, bf16[512,1152]{1,0:T(8,128)(2,1)} %copy-done.23, bf16[1024,1152]{1,0:T(8,128)(2,1)} %pad_maximum_fusion.rows_ref, ...), custom_call_target="tpu_custom_call" | custom-call | flops 2785017856 | bytes 9732096 | tf_op jit(solution)/shard_map/attend_back/pallas_call | solution.py:290
  337.0 7.0 %sum_nt.2 = (bf16[512,1152]{1,0:T(8,128)(2,1)}, bf16[512,1152]{1,0:T(8,128)(2,1)}) custom-call(bf16[1024,512]{1,0:T(8,128)(2,1)} %get-tuple-element.161.refs_0_, bf16[1024,512]{1,0:T(8,128)(2,1)} %get-tuple-element.163.refs_1_, bf16[1152,640]{1,0:T(8,128)(2,1)} %collective-permute-done.13.w_ref.refs_7_.refs_8_.w0_ref.w1_ref.refs_2_, bf16[1152,640]{1,0:T(8,128)(2,1)} %copy-done.1), custom_call_target="tpu_custom_call" | custom-call | flops 2415919104 | bytes 6815744 | tf_op jit(solution)/shard_map/sum_nt/pallas_call | solution.py:364
  345.1 11.1 %attend_back.7 = (bf16[1024,512]{1,0:T(8,128)(2,1)}, bf16[1152,640]{1,0:T(8,128)(2,1)}, f32[2,256]{1,0:T(2,128)S(1)}) custom-call(bf16[512,1152]{1,0:T(8,128)(2,1)} %get-tuple-element.143.own_ref, bf16[512,1152]{1,0:T(8,128)(2,1)} %copy-done.23, bf16[1024,1152]{1,0:T(8,128)(2,1)} %pad_maximum_fusion.rows_ref, bf16[1152,640]{1,0:T(8,128)(2,1)} %copy-done, ...), custom_call_target="tpu_custom_call" | custom-call | flops 2785017856 | bytes 9732096 | tf_op jit(solution)/shard_map/attend_back/pallas_call | solution.py:290
  356.2 10.8 %collective-permute-done.31 = bf16[1152,640]{1,0:T(8,128)(2,1)S(1)} collective-permute-done((bf16[1152,640]{1,0:T(8,128)(2,1)}, bf16[1152,640]{1,0:T(8,128)(2,1)S(1)}, u32[]{:S(2)}, u32[]{:S(2)}) %collective-permute-start.31) | collective-permute-done | bytes 1474592 | tf_op jit(solution)/shard_map/ppermute | solution.py:686
  367.0 2.9 add_convert_fusion
  369.9 7.6 %sum_nt.3 = (bf16[512,1152]{1,0:T(8,128)(2,1)}, bf16[512,1152]{1,0:T(8,128)(2,1)}) custom-call(bf16[1024,512]{1,0:T(8,128)(2,1)} %get-tuple-element.167.refs_0_, bf16[1024,512]{1,0:T(8,128)(2,1)} %get-tuple-element.169.refs_1_, bf16[1152,640]{1,0:T(8,128)(2,1)} %collective-permute-done.8.w_ref.refs_5_.refs_6_.w0_ref.w1_ref.refs_2_, ...), custom_call_target="tpu_custom_call" | custom-call | flops 2415919104 | bytes 6815744 | tf_op jit(solution)/shard_map/sum_nt/pallas_call | solution.py:364
  380.1 3.5 convert_add_fusion
  383.6 5.1 %norm_back.3 = (f32[512,1152]{1,0:T(8,128)}, f32[8,1152]{1,0:T(8,128)S(1)}) custom-call(bf16[512,1152]{1,0:T(8,128)(2,1)S(1)} %copy-done.8, bf16[512,1152]{1,0:T(8,128)(2,1)S(1)} %collective-permute-done.32.refs_1_, bf16[512,1152]{1,0:T(8,128)(2,1)} %refs_2_.1, f32[512,1152]{1,0:T(8,128)} %get-tuple-element.173.refs_3_, f32[1,1152]{1,0:T(1,128)S(1)} %copy-done.12), custom_call_target="tpu_custom_call" | custom-call | flops 17694720 | bytes 9437184 | tf_op jit(solution)/shard_map/norm_back/pallas_call | solution.py:582
  394.4 4.0 add_add_fusion
  403.0 3.4 collective-permute-done.38
  406.4 8.5 %collective-permute-done.37 = f32[16,1152]{1,0:T(8,128)S(1)} collective-permute-done((f32[16,1152]{1,0:T(8,128)S(1)}, f32[16,1152]{1,0:T(8,128)S(1)}, u32[]{:S(2)}, u32[]{:S(2)}) %collective-permute-start.37) | collective-permute-done | bytes 73760 | tf_op jit(solution)/shard_map/ppermute | solution.py:686
  (254 shorter events, 77.7 us)
Async XLA Ops:
  7.2 43.2 %all-gather.4.cloned.1.call-start = ((), (), s32[]{:S(2)}) async-start(), calls=%async_computation.3 | async-start | bytes 3317760 | tf_op jit(solution)/shard_map/all_gather | solution.py:750
  10.9 77.3 %all-gather.6.cloned.1.call-start = ((), (), s32[]{:S(2)}) async-start(), calls=%async_computation.4 | async-start | bytes 2985984 | tf_op jit(solution)/shard_map/all_gather | solution.py:805
  11.3 8.1 %collective-permute-start.2 = (f32[1868]{0:T(1024)S(1)}, f32[1868]{0:T(1024)S(1)}, u32[]{:S(2)}, u32[]{:S(2)}) collective-permute-start(f32[1868]{0:T(1024)S(1)} %concatenate.39), channel_id=1, source_target_pairs={{0,3},{1,2},{2,1},{3,0},{4,7},{5,6},{6,5},{7,4},{8,11},{9,10},{10,... | collective-permute-start | bytes 22424 | tf_op jit(solution)/shard_map/ppermute | solution.py:686
  15.2 4.2 collective-permute-start.1
  15.7 3.7 collective-permute-start
  15.9 27.3 %collective-permute-start.10 = (bf16[512,1152]{1,0:T(8,128)(2,1)S(1)}, bf16[512,1152]{1,0:T(8,128)(2,1)}, u32[]{:S(2)}, u32[]{:S(2)}) collective-permute-start(bf16[512,1152]{1,0:T(8,128)(2,1)S(1)} %copy-done.4), channel_id=1, source_target_pairs={{0,1},{1,0},{2,3},{3,2},{4,5},{5,4},{6,7},{7,6},{8,9},{9,8},{10,11... | collective-permute-start | bytes 3538952 | tf_op jit(solution)/shard_map/ppermute | solution.py:686
  18.6 113.5 %all-gather.8.cloned.1.call-start = ((), (), s32[]{:S(2)}) async-start(), calls=%async_computation.5 | async-start | bytes 2985984 | tf_op jit(solution)/shard_map/all_gather | solution.py:805
  19.7 5.6 %collective-permute-start.3 = (f32[4,216]{1,0:T(4,128)S(1)}, f32[4,216]{1,0:T(4,128)S(1)}, u32[]{:S(2)}, u32[]{:S(2)}) collective-permute-start(f32[4,216]{1,0:T(4,128)S(1)} %pad_maximum_fusion.8), channel_id=1, source_target_pairs={{0,8},{1,9},{2,10},{3,11},{4,12},{5,13},{6,14},{7,15},{8,16},{9,17... | collective-permute-start | bytes 10376 | tf_op jit(solution)/shard_map/ppermute | solution.py:686
  21.3 4.5 %collective-permute-start.4 = (f32[4,216]{1,0:T(4,128)S(1)}, f32[4,216]{1,0:T(4,128)S(1)}, u32[]{:S(2)}, u32[]{:S(2)}) collective-permute-start(f32[4,216]{1,0:T(4,128)S(1)} %pad_maximum_fusion.8), channel_id=1, source_target_pairs={{0,16},{1,17},{2,18},{3,19},{4,20},{5,21},{6,22},{7,23},{8,24},{9,... | collective-permute-start | bytes 10376 | tf_op jit(solution)/shard_map/ppermute | solution.py:686
  23.9 4.3 collective-permute-start.5
  28.2 1.2 collective-permute-start.6
  34.6 8.6 %collective-permute-start.7 = (bf16[512,1152]{1,0:T(8,128)(2,1)}, bf16[512,1152]{1,0:T(8,128)(2,1)S(1)}, u32[]{:S(2)}, u32[]{:S(2)}) collective-permute-start(bf16[512,1152]{1,0:T(8,128)(2,1)} %fusion.6), channel_id=1, source_target_pairs={{0,4},{1,5},{2,6},{3,7},{4,0},{5,1},{6,2},{7,3},{8,12},{9,13},{10,... | collective-permute-start | bytes 3538952 | tf_op jit(solution)/shard_map/ppermute | solution.py:686
  34.8 28.3 %collective-permute-start.9 = (bf16[512,1152]{1,0:T(8,128)(2,1)S(1)}, bf16[512,1152]{1,0:T(8,128)(2,1)}, u32[]{:S(2)}, u32[]{:S(2)}) collective-permute-start(bf16[512,1152]{1,0:T(8,128)(2,1)S(1)} %copy-done.4), channel_id=1, source_target_pairs={{0,4},{1,5},{2,6},{3,7},{4,0},{5,1},{6,2},{7,3},{8,12},{9,13},{10,... | collective-permute-start | bytes 3538952 | tf_op jit(solution)/shard_map/ppermute | solution.py:686
  43.2 21.3 %collective-permute-start.11 = (bf16[512,1152]{1,0:T(8,128)(2,1)}, bf16[512,1152]{1,0:T(8,128)(2,1)}, u32[]{:S(2)}, u32[]{:S(2)}) collective-permute-start(bf16[512,1152]{1,0:T(8,128)(2,1)} %collective-permute-done.10.cot0), channel_id=1, source_target_pairs={{0,4},{1,5},{2,6},{3,7},{4,0},{5,1},{6,2},{7,3},{8,12},{9,13},{10,... | collective-permute-start | bytes 3538952 | tf_op jit(solution)/shard_map/ppermute | solution.py:686
  52.0 68.2 %copy-start = (bf16[1152,640]{1,0:T(8,128)(2,1)}, bf16[1152,640]{1,0:T(8,128)(2,1)S(1)}, u32[]{:S(2)}) copy-start(bf16[1152,640]{1,0:T(8,128)(2,1)S(1)} %dynamic-slice_bitcast_fusion.w_ref.refs_3_.refs_4_.w0_ref.w1_ref) | copy-start | bytes 4423684
  52.0 34.0 %collective-permute-start.8 = (bf16[1152,640]{1,0:T(8,128)(2,1)S(1)}, bf16[1152,640]{1,0:T(8,128)(2,1)}, u32[]{:S(2)}, u32[]{:S(2)}) collective-permute-start(bf16[1152,640]{1,0:T(8,128)(2,1)S(1)} %dynamic-slice_bitcast_fusion.w_ref.refs_3_.refs_4_.w0_ref.w1_ref), channel_id=1, source_target_pairs={{0,1},{1,0},{2,3},{3,2},{4,6},{5,7},{6,4},{7,5},{8,9},{9,8},{10,11... | collective-permute-start | bytes 4423688 | tf_op jit(solution)/shard_map/ppermute | solution.py:686
  54.3 329.3 %reduce-scatter.6.cloned.1.call-start = ((), (), s32[]{:S(2)}) async-start(), calls=%async_computation.7 | async-start | bytes 2985984 | tf_op jit(solution)/shard_map/reduce_scatter | solution.py:866
  54.4 33.9 %collective-permute-start.13 = (bf16[1152,640]{1,0:T(8,128)(2,1)S(1)}, bf16[1152,640]{1,0:T(8,128)(2,1)}, u32[]{:S(2)}, u32[]{:S(2)}) collective-permute-start(bf16[1152,640]{1,0:T(8,128)(2,1)S(1)} %dynamic-slice_bitcast_fusion.w_ref.refs_3_.refs_4_.w0_ref.w1_ref), channel_id=1, source_target_pairs={{0,2},{1,3},{2,0},{3,1},{4,5},{5,4},{6,7},{7,6},{8,10},{9,11},{10,... | collective-permute-start | bytes 4423688 | tf_op jit(solution)/shard_map/ppermute | solution.py:686
  86.0 19.8 %collective-permute-start.12 = (bf16[1152,640]{1,0:T(8,128)(2,1)}, bf16[1152,640]{1,0:T(8,128)(2,1)S(1)}, u32[]{:S(2)}, u32[]{:S(2)}) collective-permute-start(bf16[1152,640]{1,0:T(8,128)(2,1)} %collective-permute-done.8.w_ref.refs_5_.refs_6_.w0_ref.w1_ref.refs_2_), channel_id=1, source_target_pairs={{0,2},{1,3},{2,0},{3,1},{4,5},{5,4},{6,7},{7,6},{8,10},{9,11},{10,... | collective-permute-start | bytes 4423688 | tf_op jit(solution)/shard_map/ppermute | solution.py:686
  105.8 36.7 %collective-permute-start.16 = (bf16[1152,1152]{1,0:T(8,128)(2,1)}, bf16[1152,1152]{1,0:T(8,128)(2,1)}, u32[]{:S(2)}, u32[]{:S(2)}) collective-permute-start(bf16[1152,1152]{1,0:T(8,128)(2,1)} %all-gather.6.cloned.1.call-done), channel_id=1, source_target_pairs={{4,6},{5,7},{6,4},{7,5},{12,14},{13,15},{14,12},{15,13},{20,22},{2... | collective-permute-start | bytes 7962632 | tf_op jit(solution)/shard_map/ppermute | solution.py:707
  132.0 3.1 collective-permute-start.14
  132.0 45.0 %collective-permute-start.19 = (bf16[1152,1152]{1,0:T(8,128)(2,1)}, bf16[1152,1152]{1,0:T(8,128)(2,1)S(1)}, u32[]{:S(2)}, u32[]{:S(2)}) collective-permute-start(bf16[1152,1152]{1,0:T(8,128)(2,1)} %all-gather.8.cloned.1.call-done.w2_own), channel_id=1, source_target_pairs={{4,6},{5,7},{6,4},{7,5},{12,14},{13,15},{14,12},{15,13},{20,22},{2... | collective-permute-start | bytes 7962632 | tf_op jit(solution)/shard_map/ppermute | solution.py:707
  140.0 28.5 %collective-permute-start.17 = (bf16[512,1152]{1,0:T(8,128)(2,1)S(1)}, bf16[512,1152]{1,0:T(8,128)(2,1)S(1)}, u32[]{:S(2)}, u32[]{:S(2)}) collective-permute-start(bf16[512,1152]{1,0:T(8,128)(2,1)S(1)} %get-tuple-element.113.rows0), channel_id=1, source_target_pairs={{0,1},{1,0},{2,3},{3,2},{4,5},{5,4},{6,7},{7,6},{8,9},{9,8},{10,11... | collective-permute-start | bytes 3538952 | tf_op jit(solution)/shard_map/ppermute | solution.py:686
  141.4 3.5 collective-permute-start.15
  168.5 2.8 collective-permute-start.18
  192.2 6.4 %collective-permute-start.20 = (bf16[512,1152]{1,0:T(8,128)(2,1)S(1)}, bf16[512,1152]{1,0:T(8,128)(2,1)S(1)}, u32[]{:S(2)}, u32[]{:S(2)}) collective-permute-start(bf16[512,1152]{1,0:T(8,128)(2,1)S(1)} %get-tuple-element.123), channel_id=1, source_target_pairs={{0,4},{1,5},{2,6},{3,7},{4,0},{5,1},{6,2},{7,3},{8,12},{9,13},{10,... | collective-permute-start | bytes 3538952 | tf_op jit(solution)/shard_map/ppermute | solution.py:686
  192.2 7.7 %collective-permute-start.21 = (bf16[512,1152]{1,0:T(8,128)(2,1)S(1)}, bf16[512,1152]{1,0:T(8,128)(2,1)S(1)}, u32[]{:S(2)}, u32[]{:S(2)}) collective-permute-start(bf16[512,1152]{1,0:T(8,128)(2,1)S(1)} %get-tuple-element.129), channel_id=1, source_target_pairs={{0,4},{1,5},{2,6},{3,7},{4,0},{5,1},{6,2},{7,3},{8,12},{9,13},{10,... | collective-permute-start | bytes 3538952 | tf_op jit(solution)/shard_map/ppermute | solution.py:686
  215.8 2.9 collective-permute-start.24
  215.8 11.2 %collective-permute-start.26 = (bf16[1152,1152]{1,0:T(8,128)(2,1)S(1)}, bf16[1152,1152]{1,0:T(8,128)(2,1)S(1)}, u32[]{:S(2)}, u32[]{:S(2)}) collective-permute-start(bf16[1152,1152]{1,0:T(8,128)(2,1)S(1)} %convolution_add_fusion.1), channel_id=1, source_target_pairs={{4,6},{5,7},{6,4},{7,5},{12,14},{13,15},{14,12},{15,13},{20,22},{2... | collective-permute-start | bytes 7962632 | tf_op jit(solution)/shard_map/ppermute | solution.py:707
  228.9 186.0 %reduce-scatter.4.cloned.1.call-start = ((), (), s32[]{:S(2)}) async-start(), calls=%async_computation.6 | async-start | bytes 2985984 | tf_op jit(solution)/shard_map/reduce_scatter | solution.py:866
  229.0 16.5 %collective-permute-start.25 = (bf16[512,1152]{1,0:T(8,128)(2,1)}, bf16[512,1152]{1,0:T(8,128)(2,1)S(1)}, u32[]{:S(2)}, u32[]{:S(2)}) collective-permute-start(bf16[512,1152]{1,0:T(8,128)(2,1)} %add_convert_fusion.2), channel_id=1, source_target_pairs={{0,1},{1,0},{2,3},{3,2},{4,5},{5,4},{6,7},{7,6},{8,9},{9,8},{10,11... | collective-permute-start | bytes 3538952 | tf_op jit(solution)/shard_map/ppermute | solution.py:686
  230.5 69.1 %collective-permute-start.28 = (bf16[1152,1152]{1,0:T(8,128)(2,1)}, bf16[1152,1152]{1,0:T(8,128)(2,1)S(1)}, u32[]{:S(2)}, u32[]{:S(2)}) collective-permute-start(bf16[1152,1152]{1,0:T(8,128)(2,1)} %fusion), channel_id=1, source_target_pairs={{4,6},{5,7},{6,4},{7,5},{12,14},{13,15},{14,12},{15,13},{20,22},{2... | collective-permute-start | bytes 7962632 | tf_op jit(solution)/shard_map/ppermute | solution.py:707
  251.6 24.0 %collective-permute-start.27 = (bf16[512,1152]{1,0:T(8,128)(2,1)}, bf16[512,1152]{1,0:T(8,128)(2,1)S(1)}, u32[]{:S(2)}, u32[]{:S(2)}) collective-permute-start(bf16[512,1152]{1,0:T(8,128)(2,1)} %get-tuple-element.143.own_ref), channel_id=1, source_target_pairs={{0,4},{1,5},{2,6},{3,7},{4,0},{5,1},{6,2},{7,3},{8,12},{9,13},{10,... | collective-permute-start | bytes 3538952 | tf_op jit(solution)/shard_map/ppermute | solution.py:686
  301.4 113.6 %reduce-scatter.8.cloned.1.call-start = ((), (), s32[]{:S(2)}) async-start(), calls=%async_computation.8 | async-start | bytes 1843200 | tf_op jit(solution)/shard_map/reduce_scatter | solution.py:915
  302.8 19.4 %collective-permute-start.29 = (bf16[1152,640]{1,0:T(8,128)(2,1)S(1)}, bf16[1152,640]{1,0:T(8,128)(2,1)S(1)}, u32[]{:S(2)}, u32[]{:S(2)}) collective-permute-start(bf16[1152,640]{1,0:T(8,128)(2,1)S(1)} %copy-done.40), channel_id=1, source_target_pairs={{0,2},{1,3},{2,0},{3,1},{4,5},{5,4},{6,7},{7,6},{8,10},{9,11},{10,... | collective-permute-start | bytes 4423688 | tf_op jit(solution)/shard_map/ppermute | solution.py:686
  304.2 39.7 %collective-permute-start.30 = (bf16[1152,640]{1,0:T(8,128)(2,1)}, bf16[1152,640]{1,0:T(8,128)(2,1)S(1)}, u32[]{:S(2)}, u32[]{:S(2)}) collective-permute-start(bf16[1152,640]{1,0:T(8,128)(2,1)} %get-tuple-element.153), channel_id=1, source_target_pairs={{0,2},{1,3},{2,0},{3,1},{4,5},{5,4},{6,7},{7,6},{8,10},{9,11},{10,... | collective-permute-start | bytes 4423688 | tf_op jit(solution)/shard_map/ppermute | solution.py:686
  334.9 32.1 %collective-permute-start.31 = (bf16[1152,640]{1,0:T(8,128)(2,1)}, bf16[1152,640]{1,0:T(8,128)(2,1)S(1)}, u32[]{:S(2)}, u32[]{:S(2)}) collective-permute-start(bf16[1152,640]{1,0:T(8,128)(2,1)} %get-tuple-element.159), channel_id=1, source_target_pairs={{0,1},{1,0},{2,3},{3,2},{4,6},{5,7},{6,4},{7,5},{8,9},{9,8},{10,11... | collective-permute-start | bytes 4423688 | tf_op jit(solution)/shard_map/ppermute | solution.py:686
  336.4 43.6 %collective-permute-start.23 = (bf16[512,1152]{1,0:T(8,128)(2,1)}, bf16[512,1152]{1,0:T(8,128)(2,1)}, u32[]{:S(2)}, u32[]{:S(2)}) collective-permute-start(bf16[512,1152]{1,0:T(8,128)(2,1)} %add_convert_fusion.1), channel_id=1, source_target_pairs={{0,1},{1,0},{2,3},{3,2},{4,5},{5,4},{6,7},{7,6},{8,9},{9,8},{10,11... | collective-permute-start | bytes 3538952 | tf_op jit(solution)/shard_map/ppermute | solution.py:686
  337.0 43.1 %collective-permute-start.22 = (bf16[512,1152]{1,0:T(8,128)(2,1)S(1)}, bf16[512,1152]{1,0:T(8,128)(2,1)}, u32[]{:S(2)}, u32[]{:S(2)}) collective-permute-start(bf16[512,1152]{1,0:T(8,128)(2,1)S(1)} %copy-done.22), channel_id=1, source_target_pairs={{0,4},{1,5},{2,6},{3,7},{4,0},{5,1},{6,2},{7,3},{8,12},{9,13},{10,... | collective-permute-start | bytes 3538952 | tf_op jit(solution)/shard_map/ppermute | solution.py:686
  377.5 6.1 %collective-permute-start.32 = (bf16[512,1152]{1,0:T(8,128)(2,1)}, bf16[512,1152]{1,0:T(8,128)(2,1)S(1)}, u32[]{:S(2)}, u32[]{:S(2)}) collective-permute-start(bf16[512,1152]{1,0:T(8,128)(2,1)} %get-tuple-element.172), channel_id=1, source_target_pairs={{0,4},{1,5},{2,6},{3,7},{4,0},{5,1},{6,2},{7,3},{8,12},{9,13},{10,... | collective-permute-start | bytes 3538952 | tf_op jit(solution)/shard_map/ppermute | solution.py:686
  390.9 7.5 %collective-permute-start.35 = (f32[16,1152]{1,0:T(8,128)}, f32[16,1152]{1,0:T(8,128)S(1)}, u32[]{:S(2)}, u32[]{:S(2)}) collective-permute-start(f32[16,1152]{1,0:T(8,128)} %pack_small.1), channel_id=1, source_target_pairs={{0,3},{1,2},{2,1},{3,0},{4,7},{5,6},{6,5},{7,4},{8,11},{9,10},{10,... | collective-permute-start | bytes 221192 | tf_op jit(solution)/shard_map/ppermute | solution.py:686
  392.3 6.1 %collective-permute-start.34 = (f32[16,1152]{1,0:T(8,128)}, f32[16,1152]{1,0:T(8,128)S(1)}, u32[]{:S(2)}, u32[]{:S(2)}) collective-permute-start(f32[16,1152]{1,0:T(8,128)} %pack_small.1), channel_id=1, source_target_pairs={{0,2},{1,3},{2,0},{3,1},{4,6},{5,7},{6,4},{7,5},{8,10},{9,11},{10,... | collective-permute-start | bytes 221192 | tf_op jit(solution)/shard_map/ppermute | solution.py:686
  393.8 4.6 %collective-permute-start.33 = (f32[16,1152]{1,0:T(8,128)}, f32[16,1152]{1,0:T(8,128)S(1)}, u32[]{:S(2)}, u32[]{:S(2)}) collective-permute-start(f32[16,1152]{1,0:T(8,128)} %pack_small.1), channel_id=1, source_target_pairs={{0,1},{1,0},{2,3},{3,2},{4,5},{5,4},{6,7},{7,6},{8,9},{9,8},{10,11... | collective-permute-start | bytes 221192 | tf_op jit(solution)/shard_map/ppermute | solution.py:686
  398.5 7.9 %collective-permute-start.38 = (f32[16,1152]{1,0:T(8,128)S(1)}, f32[16,1152]{1,0:T(8,128)S(1)}, u32[]{:S(2)}, u32[]{:S(2)}) collective-permute-start(f32[16,1152]{1,0:T(8,128)S(1)} %add_add_fusion.2), channel_id=1, source_target_pairs={{0,24},{1,25},{2,26},{3,27},{4,28},{5,29},{6,30},{7,31},{8,0},{9,1... | collective-permute-start | bytes 221192 | tf_op jit(solution)/shard_map/ppermute | solution.py:686
  400.3 14.6 %collective-permute-start.37 = (f32[16,1152]{1,0:T(8,128)S(1)}, f32[16,1152]{1,0:T(8,128)S(1)}, u32[]{:S(2)}, u32[]{:S(2)}) collective-permute-start(f32[16,1152]{1,0:T(8,128)S(1)} %add_add_fusion.2), channel_id=1, source_target_pairs={{0,16},{1,17},{2,18},{3,19},{4,20},{5,21},{6,22},{7,23},{8,24},{9,... | collective-permute-start | bytes 221192 | tf_op jit(solution)/shard_map/ppermute | solution.py:686
  400.9 14.0 %collective-permute-start.36 = (f32[16,1152]{1,0:T(8,128)S(1)}, f32[16,1152]{1,0:T(8,128)S(1)}, u32[]{:S(2)}, u32[]{:S(2)}) collective-permute-start(f32[16,1152]{1,0:T(8,128)S(1)} %add_add_fusion.2), channel_id=1, source_target_pairs={{0,8},{1,9},{2,10},{3,11},{4,12},{5,13},{6,14},{7,15},{8,16},{9,17... | collective-permute-start | bytes 221192 | tf_op jit(solution)/shard_map/ppermute | solution.py:686
  416.0 1.9 collective-permute-start.39
  421.4 1.4 collective-permute-start.40
  (41 other events, 311.4 us)
Sparse Core Ops, SparseCore 0:
  11.0 39.4 all-gather.3
  52.7 32.8 all-gather.5
  87.3 33.0 all-gather.7
  229.0 58.7 reduce-scatter.5
  301.5 37.1 reduce-scatter.3
  377.6 37.0 reduce-scatter.7
